TPU v7x, 256 devices: a whole 4x4x8 slice. The times are simulated.
256 devices in a mesh: seq: 32 (over x, z), dp: 8 (over y, core).
Axes of the slice: x: 4, y: 4, z: 8, core: 2. Of those that a mesh axis runs over, the one named last changes fastest.
Arguments:
- signal: bfloat16 [8, 16384, 768], P('dp', 'seq'), may hold values from -6 to 6
- first_kernel: bfloat16 [3, 768, 768], replicated, may hold values from -0.125 to 0.125
- second_kernel: bfloat16 [3, 768, 768], replicated, may hold values from -0.125 to 0.125
- cotangent: bfloat16 [8, 16384, 768], P('dp', 'seq'), may hold values from -6 to 6
Outputs:
- output: bfloat16 [8, 16384, 768], P('dp', 'seq')
- grad_signal: bfloat16 [8, 16384, 768], P('dp', 'seq')
- first_kernel_gradient: float32 [3, 768, 768], P(None, 'seq')
- second_kernel_gradient: float32 [3, 768, 768], P(None, 'seq')
All inputs are finite; a program needn't handle non-finite values.
Results may differ from a plain program's by a relative error of at most 0.01.
Values may be sent and summed in bfloat16 or wider, within the bound.
No kernel may reach another device: no remote copies, remote signals or barrier semaphores. Data moves between devices by JAX's collectives and lax.ppermute only.
A program may use at most 128 MiB of HBM per device.

v0:
```python
import math

import jax
import jax.numpy as jnp
from jax import lax
from jax.sharding import PartitionSpec as P

FIRST_DILATION = 64
SECOND_DILATION = 128


def padded(block, sides, width):
    for axis, dim in sides:
        count = lax.axis_size(axis)
        forward = [(i, i + 1) for i in range(count - 1)]
        backward = [(target, source) for source, target in forward]
        low = lax.ppermute(
            lax.slice_in_dim(block, block.shape[dim] - width, None, axis=dim), axis, forward
        )
        high = lax.ppermute(lax.slice_in_dim(block, 0, width, axis=dim), axis, backward)
        block = jnp.concatenate([low, block, high], axis=dim)
    return block


def gelu_tanh(v):
    return jax.nn.gelu(v, approximate=True)


def convolve_forward(padded_input, kernel_weight, dilation_step, element_count):
    total_sum = jnp.einsum(
        "wlc,cd->wld",
        padded_input[:, 0:element_count],
        kernel_weight[0],
        preferred_element_type=jnp.float32,
    )
    for tap_index in range(1, 3):
        total_sum = total_sum + jnp.einsum(
            "wlc,cd->wld",
            padded_input[:, tap_index * dilation_step : tap_index * dilation_step + element_count],
            kernel_weight[tap_index],
            preferred_element_type=jnp.float32,
        )
    return total_sum


def convolve_backward(gradient_padded, kernel_weight, dilation_step, element_count):
    total_sum = jnp.einsum(
        "wld,cd->wlc",
        gradient_padded[:, 2 * dilation_step : 2 * dilation_step + element_count],
        kernel_weight[0],
        preferred_element_type=jnp.float32,
    )
    for tap_index in range(1, 3):
        total_sum = total_sum + jnp.einsum(
            "wld,cd->wlc",
            gradient_padded[
                :, (2 - tap_index) * dilation_step : (2 - tap_index) * dilation_step + element_count
            ],
            kernel_weight[tap_index],
            preferred_element_type=jnp.float32,
        )
    return total_sum


def kernel_pieces(activation_padded, gradient_value, dilation_step, element_count, scale_factor):
    return (
        jnp.stack(
            [
                jnp.einsum(
                    "wlc,wld->cd",
                    activation_padded[
                        :, tap_index * dilation_step : tap_index * dilation_step + element_count
                    ],
                    gradient_value,
                    preferred_element_type=jnp.float32,
                )
                for tap_index in range(3)
            ]
        )
        * scale_factor
    )


def borders_forward(receptive_field, dilation_step):
    return padded(receptive_field, (("seq", 1),), dilation_step)


def borders_backward(receptive_field, dilation_step):
    return padded(receptive_field, (("seq", 1),), dilation_step)


def kernel_reduction(terms):
    share = lax.psum_scatter(terms, "seq", scatter_dimension=1, tiled=True)
    return lax.psum(share, "dp")


def per_device(signal, first_kernel, second_kernel, cotangent):
    element_count = signal.shape[1]
    n_seq = lax.axis_size("seq")
    tokens_all = signal.shape[0] * lax.axis_size("dp") * element_count * n_seq
    scale_factor = 1.0 / math.sqrt(tokens_all)
    signal_float = signal.astype(jnp.float32)
    first_activation = gelu_tanh(signal_float).astype(jnp.bfloat16)
    first_margin = borders_forward(first_activation, FIRST_DILATION)
    hidden_state = (
        signal_float + convolve_forward(first_margin, first_kernel, FIRST_DILATION, element_count)
    ).astype(jnp.bfloat16)
    middle_float = hidden_state.astype(jnp.float32)
    second_activation = gelu_tanh(middle_float).astype(jnp.bfloat16)
    second_margin = borders_forward(second_activation, SECOND_DILATION)
    output = (
        middle_float
        + convolve_forward(second_margin, second_kernel, SECOND_DILATION, element_count)
    ).astype(jnp.bfloat16)
    upstream_padded = borders_backward(cotangent, SECOND_DILATION)
    second_backward = convolve_backward(
        upstream_padded, second_kernel, SECOND_DILATION, element_count
    )
    _, pull_b = jax.vjp(gelu_tanh, middle_float)
    middle_gradient = (cotangent.astype(jnp.float32) + pull_b(second_backward)[0]).astype(
        jnp.bfloat16
    )
    second_kernel_gradient = kernel_reduction(
        kernel_pieces(second_margin, cotangent, SECOND_DILATION, element_count, scale_factor)
    )
    middle_padded = borders_backward(middle_gradient, FIRST_DILATION)
    first_backward = convolve_backward(middle_padded, first_kernel, FIRST_DILATION, element_count)
    _, pull_a = jax.vjp(gelu_tanh, signal_float)
    grad_signal = (middle_gradient.astype(jnp.float32) + pull_a(first_backward)[0]).astype(
        jnp.bfloat16
    )
    first_kernel_gradient = kernel_reduction(
        kernel_pieces(first_margin, middle_gradient, FIRST_DILATION, element_count, scale_factor)
    )
    return (output, grad_signal, first_kernel_gradient, second_kernel_gradient)


def solution(mesh):
    placed = (P("dp", "seq", None), P(), P(), P("dp", "seq", None))
    return jax.shard_map(
        per_device,
        mesh=mesh,
        in_specs=placed,
        out_specs=(
            P("dp", "seq", None),
            P("dp", "seq", None),
            P(None, "seq", None),
            P(None, "seq", None),
        ),
        check_vma=False,
    )
```

profile of v0, /device:TPU:1, one launch (start us, length us, event | category | flops | bytes accessed | tf_op | source)
XLA Modules:
  0.0 572.3 jit_solution(10517159963988974399)
XLA Ops:
  7.2 0.0 copy-start.1
  7.2 0.0 copy-start
  7.2 0.0 reduce-scatter.3.cloned.1.call-start
  7.2 1.8 fusion.13
  9.0 4.4 collective-permute-start
  13.4 1.3 collective-permute-start.1
  14.7 0.0 copy-done
  14.8 1.3 collective-permute-start.4
  16.1 0.0 copy-start.4
  16.1 5.1 collective-permute-start.5
  21.2 0.0 copy-done.1
  21.2 2.4 fusion.52
  23.6 0.0 copy-done.4
  23.6 0.0 copy-start.5
  23.6 0.8 fusion.34
  24.4 0.0 collective-permute-done
  24.4 1.2 copy-done.5
  25.6 0.8 fusion.56
  26.4 0.0 collective-permute-done.1
  26.4 1.2 fusion.20
  27.6 0.0 copy-start.2
  27.6 0.0 collective-permute-done.4
  27.6 0.8 fusion.38
  28.5 0.0 collective-permute-done.5
  28.5 0.0 copy-done.2
  28.5 1.8 fusion.5
  30.3 1.0 convolution_bitcast_fusion.4
  31.3 0.8 convolution_bitcast_fusion.3
  32.1 0.8 convolution_bitcast_fusion.5
  32.9 3.2 maximum_multiply_fusion
  36.1 0.0 reduce-scatter.3.cloned.1.call-update
  36.2 0.0 reduce-scatter.5.cloned.1.call-start
  36.2 1.3 collective-permute-start.3
  37.5 4.4 collective-permute-start.2
  41.9 2.2 convolution_bitcast_fusion.1
  44.1 0.0 collective-permute-done.3
  44.1 0.8 convolution_bitcast_fusion
  45.0 0.0 collective-permute-done.2
  45.0 0.8 convolution_bitcast_fusion.2
  45.8 3.1 maximum_multiply_fusion.1
  48.9 0.0 copy-start.3
  48.9 0.0 reduce-scatter.5.cloned.1.call-update
  48.9 0.0 all-reduce.3.cloned.1.call-start
  49.0 1.1 copy-done.3
  50.1 0.0 copy-start.6
  50.1 3.7 fusion.36
  53.8 1.3 collective-permute-start.6
  55.1 5.3 collective-permute-start.7
  60.4 0.0 copy-done.6
  60.4 0.8 fusion.50
  61.2 3.2 fusion.40
  64.4 0.0 collective-permute-done.6
  64.4 0.8 fusion.54
  65.3 0.0 collective-permute-done.7
  65.3 2.7 fusion.9
  67.9 197.1 %reduce-scatter.3.cloned.1.call-done = f32[3,24,768]{2,1,0:T(8,128)} async-done(((f32[3,768,768]{2,1,0:T(8,128)}), f32[3,24,768]{2,1,0:T(8,128)}) %reduce-scatter.3.cloned.1.call-update) | async-done | bytes 221200 | tf_op jit(solution)/shard_map/reduce_scatter | solution.py:93
  265.0 229.6 %reduce-scatter.5.cloned.1.call-done = f32[3,24,768]{2,1,0:T(8,128)} async-done(((f32[3,768,768]{2,1,0:T(8,128)}), f32[3,24,768]{2,1,0:T(8,128)}) %reduce-scatter.5.cloned.1.call-update) | async-done | bytes 221200 | tf_op jit(solution)/shard_map/reduce_scatter | solution.py:93
  494.7 0.0 all-reduce.3.cloned.1.call-update
  494.7 3.9 fusion.21
  498.6 63.8 %all-reduce.3.cloned.1.call-done = (f32[3,24,768]{2,1,0:T(8,128)}, f32[3,24,768]{2,1,0:T(8,128)}) async-done(((f32[3,24,768]{2,1,0:T(8,128)}, f32[3,24,768]{2,1,0:T(8,128)}), (f32[3,24,768]{2,1,0:T(8,128)}, f32[3,24,768]{2,1,0:T(8,128)})) %all-reduce.3.cloned.1.call-update) | async-done | bytes 442384 | tf_op jit(solution)/shard_map/psum | solution.py:94
  562.5 1.6 copy.10
  564.1 1.6 copy.11
  (4 shorter events, 0.1 us)
Async XLA Ops:
  7.2 14.0 %copy-start.1 = (bf16[1,512,768]{2,1,0:T(8,128)(2,1)S(1)}, bf16[1,512,768]{2,1,0:T(8,128)(2,1)}, u32[]{:S(2)}) copy-start(bf16[1,512,768]{2,1,0:T(8,128)(2,1)} %param.4) | copy-start | bytes 2359300
  7.2 7.5 %copy-start = (bf16[1,512,768]{2,1,0:T(8,128)(2,1)S(1)}, bf16[1,512,768]{2,1,0:T(8,128)(2,1)}, u32[]{:S(2)}) copy-start(bf16[1,512,768]{2,1,0:T(8,128)(2,1)} %param.7) | copy-start | bytes 2359300
  7.2 257.9 %reduce-scatter.3.cloned.1.call-start = ((), (), s32[]{:S(2)}) async-start(), calls=%async_computation.2 | async-start | bytes 7299072 | tf_op jit(solution)/shard_map/reduce_scatter | solution.py:93
  9.0 15.4 %collective-permute-start = (bf16[1,64,768]{2,1,0:T(8,128)(2,1)S(1)}, bf16[1,64,768]{2,1,0:T(8,128)(2,1)S(1)}, u32[]{:S(2)}, u32[]{:S(2)}) collective-permute-start(bf16[1,64,768]{2,1,0:T(8,128)(2,1)S(1)} %get-tuple-element.13), channel_id=1, source_target_pairs={{0,8},{8,16},{16,24},{24,32},{32,40},{40,48},{48,56},{56,64},{64,7... | collective-permute-start | bytes 294920 | tf_op jit(solution)/shard_map/ppermute | solution.py:17
  13.4 12.9 %collective-permute-start.1 = (bf16[1,64,768]{2,1,0:T(8,128)(2,1)S(1)}, bf16[1,64,768]{2,1,0:T(8,128)(2,1)S(1)}, u32[]{:S(2)}, u32[]{:S(2)}) collective-permute-start(bf16[1,64,768]{2,1,0:T(8,128)(2,1)S(1)} %get-tuple-element.12), channel_id=1, source_target_pairs={{8,0},{16,8},{24,16},{32,24},{40,32},{48,40},{56,48},{64,56},{72,6... | collective-permute-start | bytes 294920 | tf_op jit(solution)/shard_map/ppermute | solution.py:20
  14.8 12.9 %collective-permute-start.4 = (bf16[1,128,768]{2,1,0:T(8,128)(2,1)S(1)}, bf16[1,128,768]{2,1,0:T(8,128)(2,1)S(1)}, u32[]{:S(2)}, u32[]{:S(2)}) collective-permute-start(bf16[1,128,768]{2,1,0:T(8,128)(2,1)S(1)} %get-tuple-element.9), channel_id=1, source_target_pairs={{8,0},{16,8},{24,16},{32,24},{40,32},{48,40},{56,48},{64,56},{72,6... | collective-permute-start | bytes 589832 | tf_op jit(solution)/shard_map/ppermute | solution.py:20
  16.1 7.5 %copy-start.4 = (bf16[3,768,768]{2,1,0:T(8,128)(2,1)S(1)}, bf16[3,768,768]{2,1,0:T(8,128)(2,1)}, u32[]{:S(2)}) copy-start(bf16[3,768,768]{2,1,0:T(8,128)(2,1)} %param.6) | copy-start | bytes 10616836
  16.1 12.4 %collective-permute-start.5 = (bf16[1,128,768]{2,1,0:T(8,128)(2,1)S(1)}, bf16[1,128,768]{2,1,0:T(8,128)(2,1)S(1)}, u32[]{:S(2)}, u32[]{:S(2)}) collective-permute-start(bf16[1,128,768]{2,1,0:T(8,128)(2,1)S(1)} %get-tuple-element.8), channel_id=1, source_target_pairs={{0,8},{8,16},{16,24},{24,32},{32,40},{40,48},{48,56},{56,64},{64,7... | collective-permute-start | bytes 589832 | tf_op jit(solution)/shard_map/ppermute | solution.py:17
  23.6 2.0 copy-start.5
  27.6 0.9 copy-start.2
  36.2 458.5 %reduce-scatter.5.cloned.1.call-start = ((), (), s32[]{:S(2)}) async-start(), calls=%async_computation.3 | async-start | bytes 7299072 | tf_op jit(solution)/shard_map/reduce_scatter | solution.py:93
  36.2 7.9 %collective-permute-start.3 = (bf16[1,128,768]{2,1,0:T(8,128)(2,1)S(1)}, bf16[1,128,768]{2,1,0:T(8,128)(2,1)S(1)}, u32[]{:S(2)}, u32[]{:S(2)}) collective-permute-start(bf16[1,128,768]{2,1,0:T(8,128)(2,1)S(1)} %get-tuple-element.10), channel_id=1, source_target_pairs={{8,0},{16,8},{24,16},{32,24},{40,32},{48,40},{56,48},{64,56},{72,6... | collective-permute-start | bytes 589832 | tf_op jit(solution)/shard_map/ppermute | solution.py:20
  37.5 7.4 %collective-permute-start.2 = (bf16[1,128,768]{2,1,0:T(8,128)(2,1)S(1)}, bf16[1,128,768]{2,1,0:T(8,128)(2,1)S(1)}, u32[]{:S(2)}, u32[]{:S(2)}) collective-permute-start(bf16[1,128,768]{2,1,0:T(8,128)(2,1)S(1)} %get-tuple-element.11), channel_id=1, source_target_pairs={{0,8},{8,16},{16,24},{24,32},{32,40},{40,48},{48,56},{56,64},{64,7... | collective-permute-start | bytes 589832 | tf_op jit(solution)/shard_map/ppermute | solution.py:17
  48.9 1.1 copy-start.3
  48.9 513.5 %all-reduce.3.cloned.1.call-start = ((), (), s32[]{:S(2)}) async-start(), calls=%async_computation.4 | async-start | bytes 884736 | tf_op jit(solution)/shard_map/psum | solution.py:94
  50.1 10.3 %copy-start.6 = (bf16[3,768,768]{2,1,0:T(8,128)(2,1)S(1)}, bf16[3,768,768]{2,1,0:T(8,128)(2,1)}, u32[]{:S(2)}) copy-start(bf16[3,768,768]{2,1,0:T(8,128)(2,1)} %param.5) | copy-start | bytes 10616836
  53.8 10.7 %collective-permute-start.6 = (bf16[1,64,768]{2,1,0:T(8,128)(2,1)S(1)}, bf16[1,64,768]{2,1,0:T(8,128)(2,1)S(1)}, u32[]{:S(2)}, u32[]{:S(2)}) collective-permute-start(bf16[1,64,768]{2,1,0:T(8,128)(2,1)S(1)} %get-tuple-element.7), channel_id=1, source_target_pairs={{8,0},{16,8},{24,16},{32,24},{40,32},{48,40},{56,48},{64,56},{72,6... | collective-permute-start | bytes 294920 | tf_op jit(solution)/shard_map/ppermute | solution.py:20
  55.1 10.2 %collective-permute-start.7 = (bf16[1,64,768]{2,1,0:T(8,128)(2,1)S(1)}, bf16[1,64,768]{2,1,0:T(8,128)(2,1)S(1)}, u32[]{:S(2)}, u32[]{:S(2)}) collective-permute-start(bf16[1,64,768]{2,1,0:T(8,128)(2,1)S(1)} %get-tuple-element.6), channel_id=1, source_target_pairs={{0,8},{8,16},{16,24},{24,32},{32,40},{40,48},{48,56},{56,64},{64,7... | collective-permute-start | bytes 294920 | tf_op jit(solution)/shard_map/ppermute | solution.py:17
Sparse Core Ops, SparseCore 0:
  36.3 228.7 reduce-scatter.2
  269.6 225.0 reduce-scatter.4
  497.2 65.2 all-reduce.2
where the time goes:
time: 574 us; the launch traced here: 572 us
  waiting for transfers between devices  491 us (86%)
  matrix products  29.3 us (5%)
  starting transfers between devices  24.5 us (4%)
  between operations  14.1 us (2%)
  other arithmetic  8.12 us (1%)
    reduce_scatter x2, waiting for transfers between devices, kernel_reduction(): share = lax.psum_scatter(terms, 'seq', scatter_dimension=1, tiled=True)  427 us
    psum x1, waiting for transfers between devices, kernel_reduction(): return lax.psum(share, 'dp')  63.8 us
    ppermute x4, starting transfers between devices, padded(): lax.ppermute(lax.slice_in_dim(block, block.shape[dim] - width, None, axis...  19.2 us
  transfers between devices with their start and end apart: 11, of which 3 were waited for; matrix products, arithmetic and copies ran while one was open for 5% of the time, Pallas kernels for 0%

commit v1 on v0

v1 whole, which is shorter than its diff:
```python
import math

import jax
import jax.numpy as jnp
from jax import lax
from jax.experimental import pallas as pl
from jax.experimental.pallas import tpu as pltpu
from jax.sharding import Mesh, PartitionSpec as P

FIRST = 64
SECOND = 128
CUBIC = 0.044715
ROOT = math.sqrt(2.0 / math.pi)
F32 = jnp.float32
BF16 = jnp.bfloat16


def gelu(v):
    return 0.5 * v * (1.0 + jnp.tanh(ROOT * (v + CUBIC * v * v * v)))


def gelu_both(v):
    square = v * v
    t = jnp.tanh(ROOT * v * (1.0 + CUBIC * square))
    half = 0.5 * (1.0 + t)
    slope = half + 0.5 * v * (1.0 - t * t) * (ROOT * (1.0 + 3.0 * CUBIC * square))
    return v * half, slope


def dot(a, b):
    return jnp.dot(a, b, preferred_element_type=F32)


def dot_nt(a, b):
    return lax.dot_general(a, b, (((1,), (1,)), ((), ())), preferred_element_type=F32)


def dot_tn(a, b):
    return lax.dot_general(a, b, (((0,), (0,)), ((), ())), preferred_element_type=F32)


def front_kernel(act, cot_ext, sig, cot, w1, w2, middle, act_b, grad_m, fwd, back):
    rows = sig.shape[0]
    total = dot(act[0:rows], w1[0])
    for k in (1, 2):
        total = total + dot(act[k * FIRST : k * FIRST + rows], w1[k])
    fwd[...] = total
    total = dot_nt(cot_ext[2 * SECOND : 2 * SECOND + rows], w2[0])
    for k in (1, 2):
        start = (2 - k) * SECOND
        total = total + dot_nt(cot_ext[start : start + rows], w2[k])
    back[...] = total

    @pl.loop(0, rows // 64)
    def _(i):
        at = pl.ds(pl.multiple_of(i * 64, 64), 64)
        mid = (sig[at].astype(F32) + fwd[at]).astype(BF16)
        middle[at] = mid
        value, slope = gelu_both(mid.astype(F32))
        act_b[at] = value.astype(BF16)
        grad_m[at] = (cot[at].astype(F32) + slope * back[at]).astype(BF16)


def front(act_ext, cot_ext, sig, cot, w1, w2):
    rows, ch = sig.shape
    tile = 256
    full = lambda a: pl.BlockSpec(a.shape, lambda n: (0, 0))
    cols = pl.BlockSpec((rows, tile), lambda n: (0, n))
    out = jax.ShapeDtypeStruct((rows, ch), BF16)
    return pl.pallas_call(
        front_kernel,
        grid=(ch // tile,),
        in_specs=[
            full(act_ext),
            full(cot_ext),
            cols,
            cols,
            pl.BlockSpec((3, ch, tile), lambda n: (0, 0, n)),
            pl.BlockSpec((3, tile, ch), lambda n: (0, n, 0)),
        ],
        out_specs=[cols, cols, cols],
        out_shape=[out, out, out],
        scratch_shapes=[pltpu.VMEM((rows, tile), F32), pltpu.VMEM((rows, tile), F32)],
        compiler_params=pltpu.CompilerParams(vmem_limit_bytes=40 << 20),
        cost_estimate=pl.CostEstimate(
            flops=12 * rows * ch * ch, transcendentals=rows * ch, bytes_accessed=14 * ch * ch
        ),
        name="front",
    )(act_ext, cot_ext, sig, cot, w1, w2)


def back_kernel(act_b, lo, hi, grad_m, mid, sig, gm, w1, w2, output, grad_s, a_ext, g_ext, fwd, bwd):
    rows = mid.shape[0]

    @pl.when(pl.program_id(0) == 0)
    def _():
        a_ext[0:SECOND] = lo[0:SECOND]
        a_ext[SECOND : SECOND + rows] = act_b[...]
        a_ext[SECOND + rows :] = hi[0:SECOND]
        g_ext[0:FIRST] = lo[SECOND:]
        g_ext[FIRST : FIRST + rows] = grad_m[...]
        g_ext[FIRST + rows :] = hi[SECOND:]

    total = dot(a_ext[0:rows], w2[0])
    for k in (1, 2):
        total = total + dot(a_ext[k * SECOND : k * SECOND + rows], w2[k])
    fwd[...] = total
    total = dot_nt(g_ext[2 * FIRST : 2 * FIRST + rows], w1[0])
    for k in (1, 2):
        start = (2 - k) * FIRST
        total = total + dot_nt(g_ext[start : start + rows], w1[k])
    bwd[...] = total

    @pl.loop(0, rows // 64)
    def _(i):
        at = pl.ds(pl.multiple_of(i * 64, 64), 64)
        output[at] = (mid[at].astype(F32) + fwd[at]).astype(BF16)
        _, slope = gelu_both(sig[at].astype(F32))
        grad_s[at] = (gm[at].astype(F32) + slope * bwd[at]).astype(BF16)


def back(act_b, lo, hi, grad_m, mid, sig, w1, w2):
    rows, ch = sig.shape
    tile = 256
    full = lambda a: pl.BlockSpec(a.shape, lambda n: (0, 0))
    cols = pl.BlockSpec((rows, tile), lambda n: (0, n))
    out = jax.ShapeDtypeStruct((rows, ch), BF16)
    return pl.pallas_call(
        back_kernel,
        grid=(ch // tile,),
        in_specs=[
            full(act_b),
            full(lo),
            full(hi),
            full(grad_m),
            cols,
            cols,
            cols,
            pl.BlockSpec((3, tile, ch), lambda n: (0, n, 0)),
            pl.BlockSpec((3, ch, tile), lambda n: (0, 0, n)),
        ],
        out_specs=[cols, cols],
        out_shape=[out, out],
        scratch_shapes=[
            pltpu.VMEM((rows + 2 * SECOND, ch), BF16),
            pltpu.VMEM((rows + 2 * FIRST, ch), BF16),
            pltpu.VMEM((rows, tile), F32),
            pltpu.VMEM((rows, tile), F32),
        ],
        compiler_params=pltpu.CompilerParams(vmem_limit_bytes=40 << 20),
        cost_estimate=pl.CostEstimate(
            flops=12 * rows * ch * ch, transcendentals=rows * ch, bytes_accessed=14 * ch * ch
        ),
        name="rear",
    )(act_b, lo, hi, grad_m, mid, sig, grad_m, w1, w2)


def weight_kernel(
    parts, core, act_b, act_ext, f_all, e_all, grad_t, cot_t, f_t, e_t, out
):
    nx, ny, nz, units = parts
    rows = act_b.shape[0]
    n = pl.program_id(0)

    def emit(left_own, left_far, right_own, right_far, left_at, right_at):
        for k in range(3):
            a, b = left_at(k), right_at(k)
            total = dot_tn(left_own[a : a + rows], right_own[b : b + rows])
            total = total + dot_tn(left_far[a : a + rows], right_far[b : b + rows])
            for j in range(2):
                tile = total[:, j * 128 : (j + 1) * 128].astype(BF16).reshape(nx, nz, 3, 8, 128)
                for g in range(3):
                    unit = k * 18 + (2 * n + j) * 3 + g
                    out[:, unit // units, :, unit % units] = tile[:, :, g]

    @pl.when(n == 0)
    def _():
        out[:, ny - 1, :, units - 2 :] = jnp.zeros((nx, nz, 2, 8, 128), BF16)

    @pl.when(core[0] == 0)
    def _():
        emit(act_b, f_all, cot_t, e_t, lambda k: 0, lambda k: (2 - k) * SECOND)

    @pl.when(core[0] != 0)
    def _():
        emit(act_ext, e_all, grad_t, f_t, lambda k: k * FIRST, lambda k: 0)


def weights(parts, core, act_b, act_ext, f_all, e_all, grad_m, cot_ext):
    rows, ch = act_b.shape
    tile = 256
    nx, ny, nz, units = parts
    full = lambda a: pl.BlockSpec(a.shape, lambda n: (0, 0))
    cols = lambda a: pl.BlockSpec((a.shape[0], tile), lambda n: (0, n))
    shape = (nx, ny, nz, units, 8, 128)
    return pl.pallas_call(
        lambda *refs: weight_kernel(parts, *refs),
        grid=(ch // tile,),
        in_specs=[
            pl.BlockSpec(memory_space=pltpu.SMEM),
            full(act_b),
            full(act_ext),
            full(f_all),
            full(e_all),
            cols(grad_m),
            cols(cot_ext),
            cols(f_all),
            cols(e_all),
        ],
        out_specs=pl.BlockSpec(shape, lambda n: (0,) * 6),
        out_shape=jax.ShapeDtypeStruct(shape, BF16),
        compiler_params=pltpu.CompilerParams(vmem_limit_bytes=48 << 20),
        cost_estimate=pl.CostEstimate(
            flops=12 * rows * ch * ch, transcendentals=0, bytes_accessed=12 * ch * ch
        ),
        name="weights",
    )(core, act_b, act_ext, f_all, e_all, grad_m, cot_ext, f_all, e_all)


def neighbours(low, high):
    axes = ("x", "z")
    count = lax.axis_size("x") * lax.axis_size("z")
    forward = [(i, i + 1) for i in range(count - 1)]
    backward = [(t, s) for s, t in forward]
    return lax.ppermute(high, axes, forward), lax.ppermute(low, axes, backward)


def per_device(signal, w1, w2, cotangent):
    sig, cot = signal[0], cotangent[0]
    rows, ch = sig.shape
    nx, ny, nz = (lax.axis_size(a) for a in ("x", "y", "z"))
    tokens = signal.shape[0] * ny * lax.axis_size("c") * rows * nx * nz
    scale = 1.0 / math.sqrt(tokens)
    groups = ch // (nx * nz) // 8
    count = 3 * (ch // 128) * groups
    units = -(-count // ny)
    core = lax.axis_index("c")

    lo, hi = neighbours(
        jnp.concatenate([sig[:FIRST], cot[:SECOND]]),
        jnp.concatenate([sig[rows - FIRST :], cot[rows - SECOND :]]),
    )
    act = lambda v: gelu(v.astype(F32)).astype(BF16)
    act_ext = jnp.concatenate([act(lo[:FIRST]), act(sig), act(hi[:FIRST])])
    cot_ext = jnp.concatenate([lo[FIRST:], cot, hi[FIRST:]])
    pad = cot_ext.shape[0] - act_ext.shape[0]
    swap = [(0, 1), (1, 0)]
    e_all = lax.ppermute(
        jnp.where(core == 0, jnp.pad(act_ext, ((0, pad), (0, 0))), cot_ext), "c", swap
    )
    mid, act_b, grad_m = front(act_ext, cot_ext, sig, cot, w1, w2)
    f_all = lax.ppermute(jnp.where(core == 0, grad_m, act_b), "c", swap)
    lo2, hi2 = neighbours(
        jnp.concatenate([act_b[:SECOND], grad_m[:FIRST]]),
        jnp.concatenate([act_b[rows - SECOND :], grad_m[rows - FIRST :]]),
    )
    parts = (nx, ny, nz, units)
    piece = weights(
        parts, core.astype(jnp.int32).reshape(1), act_b, act_ext, f_all, e_all, grad_m, cot_ext
    )
    output, grad_s = back(act_b, lo2, hi2, grad_m, mid, sig, w1, w2)

    got = lax.all_to_all(piece.reshape(nx * ny, nz, units, 8, 128), ("x", "y"), 0, 0, tiled=True)
    part = jnp.sum(got.astype(F32), axis=0).astype(BF16)
    got = lax.all_to_all(part, "z", 0, 0, tiled=True)
    part = jnp.sum(got.astype(F32), axis=0).astype(BF16)
    both = lax.all_to_all(
        jnp.broadcast_to(part[None], (2 * ny, units, 8, 128)), ("y", "c"), 0, 0, tiled=True
    )
    both = both.reshape(ny, 2, units, 8, 128)

    def assemble(layer):
        flat = both[:, layer].reshape(ny * units, 8, 128)[:count]
        flat = flat.reshape(3, ch // 128, groups, 8, 128).transpose(0, 2, 3, 1, 4)
        return flat.reshape(3, groups * 8, ch).astype(F32) * scale

    return output[None], grad_s[None], assemble(1), assemble(0)


def solution(mesh):
    fine = Mesh(mesh.devices.reshape(4, 8, 4, 2), ("x", "z", "y", "c"))
    placed = P(("y", "c"), ("x", "z"), None)
    split = P(None, ("x", "z"), None)
    return jax.shard_map(
        per_device,
        mesh=fine,
        in_specs=(placed, P(), P(), placed),
        out_specs=(placed, placed, split, split),
        check_vma=False,
    )
```

time: 574 us -> 146 us (0.25)
  the two profiles are of different devices: /device:TPU:1 before, /device:TPU:13 now
where the time goes in v1:
time: 146 us; the launch traced here: 145 us
  waiting for transfers between devices  64.4 us (44%)
  starting transfers between devices  43.4 us (30%)
  Pallas kernels  20.6 us (14%)
  local copies, waits for them, and re-layouts  10.8 us (7%)
  other arithmetic  5.31 us (4%)
    all_to_all x1, waiting for transfers between devices, per_device(): lax.all_to_all(piece.reshape(nx * ny, nz, units, 8, 128), ('x', 'y'), 0,...  48.5 us
    all_to_all x1, starting transfers between devices, per_device(): lax.all_to_all(jnp.broadcast_to(part[None], (2 * ny, units, 8, 128)), ('y...  15 us
    ppermute x2, starting transfers between devices, neighbours(): lax.ppermute(low, axes, backward)  9.38 us
    pallas_call x1, Pallas kernels, back(): pl.pallas_call(back_kernel, grid=(ch // tile,), in_specs=[full(act_b), fu...  7.21 us
    unnamed x16, local copies, waits for them, and re-layouts  7.16 us
    pallas_call x1, Pallas kernels, weights(): pl.pallas_call(lambda *refs: weight_kernel(parts, *refs), grid=(ch // til...  6.93 us
    all_to_all x1, starting transfers between devices, per_device(): lax.all_to_all(piece.reshape(nx * ny, nz, units, 8, 128), ('x', 'y'), 0,...  6.81 us
    pallas_call x1, Pallas kernels, front(): pl.pallas_call(front_kernel, grid=(ch // tile,), in_specs=[full(act_ext),...  6.46 us
  transfers between devices with their start and end apart: 9, of which 5 were waited for; matrix products, arithmetic and copies ran while one was open for 4% of the time, Pallas kernels for 9%

profile of v1, /device:TPU:13, one launch (start us, length us, event | category | flops | bytes accessed | tf_op | source)
XLA Modules:
  0.0 145.4 jit_solution(7135330589161536407)
XLA Ops:
  0.6 0.0 copy-start.1
  0.6 1.1 slice_bitcast_fusion.1
  1.8 1.0 slice_bitcast_fusion.3
  2.8 7.5 %collective-permute-start.1 = (bf16[192,768]{1,0:T(8,128)(2,1)S(1)}, bf16[192,768]{1,0:T(8,128)(2,1)S(1)}, u32[]{:S(2)}, u32[]{:S(2)}) collective-permute-start(bf16[192,768]{1,0:T(8,128)(2,1)S(1)} %pad_maximum_fusion.3), channel_id=1, source_target_pairs={{8,0},{16,8},{24,16},{32,24},{40,32},{48,40},{56,48},{64,56},{72,6... | collective-permute-start | bytes 884744 | tf_op jit(solution)/shard_map/ppermute | solution.py:225
  10.3 1.9 %collective-permute-start = (bf16[192,768]{1,0:T(8,128)(2,1)S(1)}, bf16[192,768]{1,0:T(8,128)(2,1)S(1)}, u32[]{:S(2)}, u32[]{:S(2)}) collective-permute-start(bf16[192,768]{1,0:T(8,128)(2,1)S(1)} %pad_maximum_fusion.2), channel_id=1, source_target_pairs={{0,8},{8,16},{16,24},{24,32},{32,40},{40,48},{48,56},{56,64},{64,7... | collective-permute-start | bytes 884744 | tf_op jit(solution)/shard_map/ppermute | solution.py:225
  12.2 0.0 copy-done.1
  12.2 0.5 fusion.1
  12.7 0.0 copy-start
  12.8 3.1 %collective-permute-done.1 = bf16[192,768]{1,0:T(8,128)(2,1)S(1)} collective-permute-done((bf16[192,768]{1,0:T(8,128)(2,1)S(1)}, bf16[192,768]{1,0:T(8,128)(2,1)S(1)}, u32[]{:S(2)}, u32[]{:S(2)}) %collective-permute-start.1) | collective-permute-done | bytes 294944 | tf_op jit(solution)/shard_map/ppermute | solution.py:225
  15.9 0.1 fusion.11
  16.0 5.9 %collective-permute-done = bf16[192,768]{1,0:T(8,128)(2,1)S(1)} collective-permute-done((bf16[192,768]{1,0:T(8,128)(2,1)S(1)}, bf16[192,768]{1,0:T(8,128)(2,1)S(1)}, u32[]{:S(2)}, u32[]{:S(2)}) %collective-permute-start) | collective-permute-done | bytes 294944 | tf_op jit(solution)/shard_map/ppermute | solution.py:225
  21.8 0.1 fusion.6
  21.9 0.1 pad_maximum_fusion.1.act.refs_2_
  22.0 0.0 copy-done
  22.0 0.0 copy-start.2
  22.0 0.3 pad_select_fusion
  22.3 2.0 %collective-permute-start.5 = (bf16[768,768]{1,0:T(8,128)(2,1)S(1)}, bf16[768,768]{1,0:T(8,128)(2,1)S(1)}, u32[]{:S(2)}, u32[]{:S(2)}) collective-permute-start(bf16[768,768]{1,0:T(8,128)(2,1)S(1)} %get-tuple-element.14), channel_id=1, source_target_pairs={{0,1},{1,0},{2,3},{3,2},{4,5},{5,4},{6,7},{7,6},{8,9},{9,8},{10,11... | collective-permute-start | bytes 3538952 | tf_op jit(solution)/shard_map/ppermute | solution.py:248
  24.3 0.0 copy-done.2
  24.3 0.0 copy-start.4
  24.3 2.0 %copy-done.4 = bf16[3,768,768]{2,1,0:T(8,128)(2,1)S(1)} copy-done((bf16[3,768,768]{2,1,0:T(8,128)(2,1)S(1)}, bf16[3,768,768]{2,1,0:T(8,128)(2,1)}, u32[]{:S(2)}) %copy-start.4) | copy-done | bytes 3538968
  26.3 6.5 %front.1 = (bf16[512,768]{1,0:T(8,128)(2,1)S(1)}, bf16[512,768]{1,0:T(8,128)(2,1)S(1)}, bf16[512,768]{1,0:T(8,128)(2,1)S(1)}) custom-call(bf16[640,768]{1,0:T(8,128)(2,1)S(1)} %pad_maximum_fusion.1.act.refs_2_, bf16[768,768]{1,0:T(8,128)(2,1)S(1)} %get-tuple-element.15.cot_ext.refs_6_, bf16[512,768]{1,0:T(8,128)(2,1)S(1)} %bitcast.30, ...), custom_call_target="tpu_custom_call" | custom-call | flops 3623878656 | bytes 8257536 | tf_op jit(solution)/shard_map/front/pallas_call | solution.py:70
  32.8 0.0 copy-start.6
  32.8 0.1 broadcast_select_fusion
  32.9 1.7 %collective-permute-start.4 = (bf16[512,768]{1,0:T(8,128)(2,1)S(1)}, bf16[512,768]{1,0:T(8,128)(2,1)S(1)}, u32[]{:S(2)}, u32[]{:S(2)}) collective-permute-start(bf16[512,768]{1,0:T(8,128)(2,1)S(1)} %broadcast_select_fusion), channel_id=1, source_target_pairs={{0,1},{1,0},{2,3},{3,2},{4,5},{5,4},{6,7},{7,6},{8,9},{9,8},{10,11... | collective-permute-start | bytes 2359304 | tf_op jit(solution)/shard_map/ppermute | solution.py:252
  34.5 1.9 %collective-permute-done.4.refs_3_.refs_7_ = bf16[512,768]{1,0:T(8,128)(2,1)S(1)} collective-permute-done((bf16[512,768]{1,0:T(8,128)(2,1)S(1)}, bf16[512,768]{1,0:T(8,128)(2,1)S(1)}, u32[]{:S(2)}, u32[]{:S(2)}) %collective-permute-start.4) | collective-permute-done | bytes 786464 | tf_op jit(solution)/shard_map/ppermute | solution.py:252
  36.5 0.0 collective-permute-done.5.refs_4_.refs_8_
  36.5 0.0 copy-done.6
  36.5 6.9 %weights.1 = bf16[4,4,8,14,8,128]{5,4,3,2,1,0:T(8,128)(2,1)} custom-call(s32[1]{0:T(128)} %bitcast.8.refs_0_, bf16[512,768]{1,0:T(8,128)(2,1)S(1)} %get-tuple-element.9.act_b.refs_1_, bf16[640,768]{1,0:T(8,128)(2,1)S(1)} %pad_maximum_fusion.1.act.refs_2_, bf16[512,768]{1,0:T(8,128)(2,1)S(1)} %collective-permute-done.4.refs_3_.refs_7_, ...), custom_call_target="tpu_custom_call" | custom-call | flops 3623878656 | bytes 7077888 | tf_op jit(solution)/shard_map/weights/pallas_call | solution.py:196
  43.4 6.8 %all-to-all-start = ((bf16[16,8,14,8,128]{4,3,2,1,0:T(8,128)(2,1)}), bf16[16,8,14,8,128]{4,3,2,1,0:T(8,128)(2,1)}, u32[]{:S(2)}, u32[]{:S(2)}) async-start(bf16[16,8,14,8,128]{4,3,2,1,0:T(8,128)(2,1)} %bitcast.32), calls=%async_computation | async-start | bytes 7340032 | tf_op jit(solution)/shard_map/all_to_all | solution.py:263
  50.3 1.9 %collective-permute-start.3 = (bf16[192,768]{1,0:T(8,128)(2,1)S(1)}, bf16[192,768]{1,0:T(8,128)(2,1)S(1)}, u32[]{:S(2)}, u32[]{:S(2)}) collective-permute-start(bf16[192,768]{1,0:T(8,128)(2,1)S(1)} %pad_maximum_fusion.5), channel_id=1, source_target_pairs={{8,0},{16,8},{24,16},{32,24},{40,32},{48,40},{56,48},{64,56},{72,6... | collective-permute-start | bytes 884744 | tf_op jit(solution)/shard_map/ppermute | solution.py:225
  52.2 48.5 %all-to-all-done = bf16[16,8,14,8,128]{4,3,2,1,0:T(8,128)(2,1)} async-done(((bf16[16,8,14,8,128]{4,3,2,1,0:T(8,128)(2,1)}), bf16[16,8,14,8,128]{4,3,2,1,0:T(8,128)(2,1)}, u32[]{:S(2)}, u32[]{:S(2)}) %all-to-all-start) | async-done | bytes 3670048 | tf_op jit(solution)/shard_map/all_to_all | solution.py:263
  100.7 3.3 %reduce_sum.24 = bf16[8,14,8,128]{3,2,1,0:T(8,128)(2,1)} reduce(bf16[16,8,14,8,128]{4,3,2,1,0:T(8,128)(2,1)} %all-to-all-done, bf16[]{:T(256)} %constant.5.clone.1), dimensions={0}, to_apply=%region_0.1 | reduce | flops 1720320 | bytes 3899394 | tf_op jit(solution)/shard_map/reduce_sum | solution.py:264
  104.0 3.4 %all-to-all-start.1 = ((bf16[8,14,8,128]{3,2,1,0:T(8,128)(2,1)}), bf16[8,14,8,128]{3,2,1,0:T(8,128)(2,1)S(1)}, u32[]{:S(2)}, u32[]{:S(2)}) async-start(bf16[8,14,8,128]{3,2,1,0:T(8,128)(2,1)} %reduce_sum.24), calls=%async_computation.1 | async-start | bytes 458752 | tf_op jit(solution)/shard_map/all_to_all | solution.py:265
  107.4 0.7 pad_maximum_fusion.4
  108.2 3.3 %collective-permute-start.2 = (bf16[192,768]{1,0:T(8,128)(2,1)}, bf16[192,768]{1,0:T(8,128)(2,1)S(1)}, u32[]{:S(2)}, u32[]{:S(2)}) collective-permute-start(bf16[192,768]{1,0:T(8,128)(2,1)} %pad_maximum_fusion.4), channel_id=1, source_target_pairs={{0,8},{8,16},{16,24},{24,32},{32,40},{40,48},{48,56},{56,64},{64,7... | collective-permute-start | bytes 884744 | tf_op jit(solution)/shard_map/ppermute | solution.py:225
  111.4 5.0 %all-to-all-done.1 = bf16[8,14,8,128]{3,2,1,0:T(8,128)(2,1)S(1)} async-done(((bf16[8,14,8,128]{3,2,1,0:T(8,128)(2,1)}), bf16[8,14,8,128]{3,2,1,0:T(8,128)(2,1)S(1)}, u32[]{:S(2)}, u32[]{:S(2)}) %all-to-all-start.1) | async-done | bytes 229408 | tf_op jit(solution)/shard_map/all_to_all | solution.py:265
  116.4 0.7 broadcast_in_dim.14
  117.1 15.0 %all-to-all-start.2 = ((bf16[8,14,8,128]{3,2,1,0:T(8,128)(2,1)}), bf16[8,14,8,128]{3,2,1,0:T(8,128)(2,1)S(1)}, u32[]{:S(2)}, u32[]{:S(2)}) async-start(bf16[8,14,8,128]{3,2,1,0:T(8,128)(2,1)} %broadcast_in_dim.14), calls=%async_computation.2 | async-start | bytes 458752 | tf_op jit(solution)/shard_map/all_to_all | solution.py:267
  132.1 0.0 collective-permute-done.3.hi
  132.2 0.0 collective-permute-done.2.lo
  132.2 0.0 copy-start.3
  132.2 2.0 %copy-done.3 = bf16[3,768,768]{2,1,0:T(8,128)(2,1)S(1)} copy-done((bf16[3,768,768]{2,1,0:T(8,128)(2,1)S(1)}, bf16[3,768,768]{2,1,0:T(8,128)(2,1)}, u32[]{:S(2)}) %copy-start.3) | copy-done | bytes 3538968
  134.2 0.0 copy-start.5
  134.2 2.0 %copy-done.5 = bf16[3,768,768]{2,1,0:T(8,128)(2,1)S(1)} copy-done((bf16[3,768,768]{2,1,0:T(8,128)(2,1)S(1)}, bf16[3,768,768]{2,1,0:T(8,128)(2,1)}, u32[]{:S(2)}) %copy-start.5) | copy-done | bytes 3538968
  136.2 0.0 copy-start.7
  136.2 1.1 copy-done.7
  137.3 7.2 %rear.1 = (bf16[512,768]{1,0:T(8,128)(2,1)}, bf16[512,768]{1,0:T(8,128)(2,1)}) custom-call(bf16[512,768]{1,0:T(8,128)(2,1)S(1)} %get-tuple-element.9.act_b.refs_1_, bf16[192,768]{1,0:T(8,128)(2,1)S(1)} %collective-permute-done.2.lo, bf16[192,768]{1,0:T(8,128)(2,1)S(1)} %collective-permute-done.3.hi, ...), custom_call_target="tpu_custom_call" | custom-call | flops 3623878656 | bytes 8257536 | tf_op jit(solution)/shard_map/rear/pallas_call | solution.py:128
  144.5 0.0 all-to-all-done.2
  144.6 0.8 copy_bitcast_fusion
  (11 shorter events, 0.2 us)
Async XLA Ops:
  0.6 11.6 %copy-start.1 = (bf16[1,512,768]{2,1,0:T(8,128)(2,1)S(1)}, bf16[1,512,768]{2,1,0:T(8,128)(2,1)}, u32[]{:S(2)}) copy-start(bf16[1,512,768]{2,1,0:T(8,128)(2,1)} %param.4) | copy-start | bytes 2359300
  2.8 13.1 %collective-permute-start.1 = (bf16[192,768]{1,0:T(8,128)(2,1)S(1)}, bf16[192,768]{1,0:T(8,128)(2,1)S(1)}, u32[]{:S(2)}, u32[]{:S(2)}) collective-permute-start(bf16[192,768]{1,0:T(8,128)(2,1)S(1)} %pad_maximum_fusion.3), channel_id=1, source_target_pairs={{8,0},{16,8},{24,16},{32,24},{40,32},{48,40},{56,48},{64,56},{72,6... | collective-permute-start | bytes 884744 | tf_op jit(solution)/shard_map/ppermute | solution.py:225
  10.3 11.6 %collective-permute-start = (bf16[192,768]{1,0:T(8,128)(2,1)S(1)}, bf16[192,768]{1,0:T(8,128)(2,1)S(1)}, u32[]{:S(2)}, u32[]{:S(2)}) collective-permute-start(bf16[192,768]{1,0:T(8,128)(2,1)S(1)} %pad_maximum_fusion.2), channel_id=1, source_target_pairs={{0,8},{8,16},{16,24},{24,32},{32,40},{40,48},{48,56},{56,64},{64,7... | collective-permute-start | bytes 884744 | tf_op jit(solution)/shard_map/ppermute | solution.py:225
  12.7 9.3 %copy-start = (bf16[1,512,768]{2,1,0:T(8,128)(2,1)S(1)}, bf16[1,512,768]{2,1,0:T(8,128)(2,1)}, u32[]{:S(2)}) copy-start(bf16[1,512,768]{2,1,0:T(8,128)(2,1)} %param.7) | copy-start | bytes 2359300
  22.0 2.3 %copy-start.2 = (bf16[3,768,768]{2,1,0:T(8,128)(2,1)S(1)}, bf16[3,768,768]{2,1,0:T(8,128)(2,1)}, u32[]{:S(2)}) copy-start(bf16[3,768,768]{2,1,0:T(8,128)(2,1)} %w1.3) | copy-start | bytes 10616836
  22.3 14.1 %collective-permute-start.5 = (bf16[768,768]{1,0:T(8,128)(2,1)S(1)}, bf16[768,768]{1,0:T(8,128)(2,1)S(1)}, u32[]{:S(2)}, u32[]{:S(2)}) collective-permute-start(bf16[768,768]{1,0:T(8,128)(2,1)S(1)} %get-tuple-element.14), channel_id=1, source_target_pairs={{0,1},{1,0},{2,3},{3,2},{4,5},{5,4},{6,7},{7,6},{8,9},{9,8},{10,11... | collective-permute-start | bytes 3538952 | tf_op jit(solution)/shard_map/ppermute | solution.py:248
  24.3 2.0 %copy-start.4 = (bf16[3,768,768]{2,1,0:T(8,128)(2,1)S(1)}, bf16[3,768,768]{2,1,0:T(8,128)(2,1)}, u32[]{:S(2)}) copy-start(bf16[3,768,768]{2,1,0:T(8,128)(2,1)} %w2.3) | copy-start | bytes 10616836
  32.8 3.7 %copy-start.6 = (bf16[512,768]{1,0:T(8,128)(2,1)}, bf16[512,768]{1,0:T(8,128)(2,1)S(1)}, u32[]{:S(2)}) copy-start(bf16[512,768]{1,0:T(8,128)(2,1)S(1)} %get-tuple-element.11.mid) | copy-start | bytes 2359300
  32.9 3.6 %collective-permute-start.4 = (bf16[512,768]{1,0:T(8,128)(2,1)S(1)}, bf16[512,768]{1,0:T(8,128)(2,1)S(1)}, u32[]{:S(2)}, u32[]{:S(2)}) collective-permute-start(bf16[512,768]{1,0:T(8,128)(2,1)S(1)} %broadcast_select_fusion), channel_id=1, source_target_pairs={{0,1},{1,0},{2,3},{3,2},{4,5},{5,4},{6,7},{7,6},{8,9},{9,8},{10,11... | collective-permute-start | bytes 2359304 | tf_op jit(solution)/shard_map/ppermute | solution.py:252
  43.4 57.3 %all-to-all-start = ((bf16[16,8,14,8,128]{4,3,2,1,0:T(8,128)(2,1)}), bf16[16,8,14,8,128]{4,3,2,1,0:T(8,128)(2,1)}, u32[]{:S(2)}, u32[]{:S(2)}) async-start(bf16[16,8,14,8,128]{4,3,2,1,0:T(8,128)(2,1)} %bitcast.32), calls=%async_computation | async-start | bytes 7340032 | tf_op jit(solution)/shard_map/all_to_all | solution.py:263
  50.3 81.9 %collective-permute-start.3 = (bf16[192,768]{1,0:T(8,128)(2,1)S(1)}, bf16[192,768]{1,0:T(8,128)(2,1)S(1)}, u32[]{:S(2)}, u32[]{:S(2)}) collective-permute-start(bf16[192,768]{1,0:T(8,128)(2,1)S(1)} %pad_maximum_fusion.5), channel_id=1, source_target_pairs={{8,0},{16,8},{24,16},{32,24},{40,32},{48,40},{56,48},{64,56},{72,6... | collective-permute-start | bytes 884744 | tf_op jit(solution)/shard_map/ppermute | solution.py:225
  104.0 12.4 %all-to-all-start.1 = ((bf16[8,14,8,128]{3,2,1,0:T(8,128)(2,1)}), bf16[8,14,8,128]{3,2,1,0:T(8,128)(2,1)S(1)}, u32[]{:S(2)}, u32[]{:S(2)}) async-start(bf16[8,14,8,128]{3,2,1,0:T(8,128)(2,1)} %reduce_sum.24), calls=%async_computation.1 | async-start | bytes 458752 | tf_op jit(solution)/shard_map/all_to_all | solution.py:265
  108.2 24.0 %collective-permute-start.2 = (bf16[192,768]{1,0:T(8,128)(2,1)}, bf16[192,768]{1,0:T(8,128)(2,1)S(1)}, u32[]{:S(2)}, u32[]{:S(2)}) collective-permute-start(bf16[192,768]{1,0:T(8,128)(2,1)} %pad_maximum_fusion.4), channel_id=1, source_target_pairs={{0,8},{8,16},{16,24},{24,32},{32,40},{40,48},{48,56},{56,64},{64,7... | collective-permute-start | bytes 884744 | tf_op jit(solution)/shard_map/ppermute | solution.py:225
  117.1 27.4 %all-to-all-start.2 = ((bf16[8,14,8,128]{3,2,1,0:T(8,128)(2,1)}), bf16[8,14,8,128]{3,2,1,0:T(8,128)(2,1)S(1)}, u32[]{:S(2)}, u32[]{:S(2)}) async-start(bf16[8,14,8,128]{3,2,1,0:T(8,128)(2,1)} %broadcast_in_dim.14), calls=%async_computation.2 | async-start | bytes 458752 | tf_op jit(solution)/shard_map/all_to_all | solution.py:267
  132.2 2.0 %copy-start.3 = (bf16[3,768,768]{2,1,0:T(8,128)(2,1)S(1)}, bf16[3,768,768]{2,1,0:T(8,128)(2,1)}, u32[]{:S(2)}) copy-start(bf16[3,768,768]{2,1,0:T(8,128)(2,1)} %w1.3) | copy-start | bytes 10616836
  134.2 2.0 %copy-start.5 = (bf16[3,768,768]{2,1,0:T(8,128)(2,1)S(1)}, bf16[3,768,768]{2,1,0:T(8,128)(2,1)}, u32[]{:S(2)}) copy-start(bf16[3,768,768]{2,1,0:T(8,128)(2,1)} %w2.3) | copy-start | bytes 10616836
  136.2 1.1 copy-start.7

commit v2 on v1

v2 whole, which is shorter than its diff:
```python
import math

import jax
import jax.numpy as jnp
from jax import lax
from jax.experimental import pallas as pl
from jax.experimental.pallas import tpu as pltpu
from jax.sharding import Mesh, PartitionSpec as P

FIRST = 64
SECOND = 128
CUBIC = 0.044715
ROOT = math.sqrt(2.0 / math.pi)
F32 = jnp.float32
BF16 = jnp.bfloat16


def gelu(v):
    return 0.5 * v * (1.0 + jnp.tanh(ROOT * (v + CUBIC * v * v * v)))


def gelu_both(v):
    square = v * v
    t = jnp.tanh(ROOT * v * (1.0 + CUBIC * square))
    half = 0.5 * (1.0 + t)
    slope = half + 0.5 * v * (1.0 - t * t) * (ROOT * (1.0 + 3.0 * CUBIC * square))
    return v * half, slope


def dot(a, b):
    return jnp.dot(a, b, preferred_element_type=F32)


def dot_nt(a, b):
    return lax.dot_general(a, b, (((1,), (1,)), ((), ())), preferred_element_type=F32)


def dot_tn(a, b):
    return lax.dot_general(a, b, (((0,), (0,)), ((), ())), preferred_element_type=F32)


def in_hbm(a):
    return pltpu.with_memory_space_constraint(a, pltpu.HBM)


def in_vmem(a):
    return pltpu.with_memory_space_constraint(a, pltpu.VMEM)


def edges(sig, cot):
    rows = sig.shape[0]

    def body(sig, cot, low, high, low_far, high_far, sems):
        pairs = []
        for first, last, skip_s, skip_c, take_s in (
            (low, high, 0, 0, FIRST),
            (low_far, high_far, FIRST, SECOND, SECOND),
        ):
            take_c = FIRST + SECOND - take_s
            pairs += [
                (sig, skip_s, first, 0, take_s),
                (cot, skip_c, first, take_s, take_c),
                (sig, rows - skip_s - take_s, last, 0, take_s),
                (cot, rows - skip_c - take_c, last, take_s, take_c),
            ]
        copies = [
            pltpu.make_async_copy(src.at[pl.ds(a, n)], dst.at[pl.ds(b, n)], sems.at[i])
            for i, (src, a, dst, b, n) in enumerate(pairs)
        ]
        for copy in copies:
            copy.start()
        for copy in copies:
            copy.wait()

    out = pltpu.VMEM((FIRST + SECOND, sig.shape[1]), BF16)
    return pl.pallas_call(
        body,
        in_specs=[pl.BlockSpec(memory_space=pl.ANY)] * 2,
        out_specs=[pl.BlockSpec(memory_space=pltpu.VMEM)] * 4,
        out_shape=[out] * 4,
        scratch_shapes=[pltpu.SemaphoreType.DMA((8,))],
        compiler_params=pltpu.CompilerParams(vmem_limit_bytes=2 << 20),
        name="edges",
    )(in_hbm(sig), in_hbm(cot))


def once(a):
    return pl.BlockSpec(a.shape, lambda n: (0, 0), pipeline_mode=pl.Buffered(1))


def three_taps(dots, left, weight, starts, rows):
    total = dots(left[starts[0] : starts[0] + rows], weight[0])
    for k in (1, 2):
        total = total + dots(left[starts[k] : starts[k] + rows], weight[k])
    return total


def front_kernel(core, act, cot_ext, sig, cot, w1, w2, middle, act_b, grad_m, swap, fwd, bwd):
    rows = sig.shape[0]
    fwd[...] = three_taps(dot, act, w1, [k * FIRST for k in range(3)], rows)
    bwd[...] = three_taps(dot_nt, cot_ext, w2, [(2 - k) * SECOND for k in range(3)], rows)

    @pl.loop(0, rows // 64)
    def _(i):
        at = pl.ds(pl.multiple_of(i * 64, 64), 64)
        mid = (sig[at].astype(F32) + fwd[at]).astype(BF16)
        middle[at] = mid
        value, slope = gelu_both(mid.astype(F32))
        grad = cot[at].astype(F32) + slope * bwd[at]
        act_b[at] = value.astype(BF16)
        grad_m[at] = grad.astype(BF16)
        swap[at] = jnp.where(core[0] == 0, grad, value).astype(BF16)


def front(core, act_ext, cot_ext, sig, cot, w1, w2):
    rows, ch = sig.shape
    tile = 256
    cols = pl.BlockSpec((rows, tile), lambda n: (0, n))
    out = jax.ShapeDtypeStruct((rows, ch), BF16)
    return pl.pallas_call(
        front_kernel,
        grid=(ch // tile,),
        in_specs=[
            pl.BlockSpec(memory_space=pltpu.SMEM),
            once(act_ext),
            once(cot_ext),
            cols,
            cols,
            pl.BlockSpec((3, ch, tile), lambda n: (0, 0, n)),
            pl.BlockSpec((3, tile, ch), lambda n: (0, n, 0)),
        ],
        out_specs=[cols] * 4,
        out_shape=[out] * 4,
        scratch_shapes=[pltpu.VMEM((rows, tile), F32), pltpu.VMEM((rows, tile), F32)],
        compiler_params=pltpu.CompilerParams(vmem_limit_bytes=16 << 20),
        cost_estimate=pl.CostEstimate(
            flops=12 * rows * ch * ch, transcendentals=rows * ch, bytes_accessed=14 * ch * ch
        ),
        name="front",
    )(core, act_ext, cot_ext, sig, cot, in_hbm(w1), in_hbm(w2))


def wing_kernel(inside, act, cot_ext, lo, hi, lo_far, hi_far, sig_t, cot_t, w1, w2, low, high, a_ext, c_ext):
    rows = act.shape[0] - 2 * FIRST

    @pl.when(pl.program_id(0) == 0)
    def _():
        far_low = gelu(lo_far[0:SECOND].astype(F32)).astype(BF16)
        far_high = gelu(hi_far[0:SECOND].astype(F32)).astype(BF16)
        a_ext[0, 0:SECOND] = far_low
        a_ext[0, SECOND:] = act[rows : rows + SECOND]
        a_ext[1, 0:FIRST] = far_low[FIRST:]
        a_ext[1, FIRST:SECOND] = act[0:FIRST]
        a_ext[1, SECOND : SECOND + FIRST] = act[rows + FIRST : rows + SECOND]
        a_ext[1, SECOND + FIRST :] = far_high[0:FIRST]
        a_ext[2, 0:SECOND] = act[0:SECOND]
        a_ext[2, SECOND:] = far_high
        c_ext[2, 0:FIRST] = lo_far[SECOND:]
        c_ext[2, FIRST:] = cot_ext[rows : rows + FIRST]
        c_ext[1, 0:FIRST] = cot_ext[FIRST:SECOND]
        c_ext[1, FIRST:] = cot_ext[rows + SECOND : rows + SECOND + FIRST]
        c_ext[0, 0:FIRST] = cot_ext[SECOND + FIRST : 2 * SECOND]
        c_ext[0, FIRST:] = hi_far[SECOND:]

    total = dot(a_ext[0], w1[0])
    for k in (1, 2):
        total = total + dot(a_ext[k], w1[k])
    mid = (sig_t[...].astype(F32) + total).astype(BF16).astype(F32)
    value, slope = gelu_both(mid)
    total = dot_nt(c_ext[0], w2[0])
    for k in (1, 2):
        total = total + dot_nt(c_ext[k], w2[k])
    slope = slope[SECOND - FIRST : SECOND + FIRST]
    grad = cot_t[...].astype(F32) + slope * total
    low[0:SECOND] = jnp.where(inside[0] > 0, value[0:SECOND], 0.0).astype(BF16)
    low[SECOND:] = jnp.where(inside[0] > 0, grad[0:FIRST], 0.0).astype(BF16)
    high[0:SECOND] = jnp.where(inside[1] > 0, value[SECOND:], 0.0).astype(BF16)
    high[SECOND:] = jnp.where(inside[1] > 0, grad[FIRST:], 0.0).astype(BF16)


def wings(inside, act_ext, cot_ext, lo, hi, lo_far, hi_far, w1, w2):
    ch = act_ext.shape[1]
    tile = 256
    size = FIRST + SECOND
    sig_t = jnp.concatenate([lo_far[FIRST:SECOND], lo[:FIRST], hi[:FIRST], hi_far[: SECOND - FIRST]])
    cot_t = jnp.concatenate([lo[FIRST + SECOND - FIRST :], hi[FIRST : 2 * FIRST]])
    cols = lambda a: pl.BlockSpec((a.shape[0], tile), lambda n: (0, n))
    out = jax.ShapeDtypeStruct((size, ch), BF16)
    return pl.pallas_call(
        wing_kernel,
        grid=(ch // tile,),
        in_specs=[
            pl.BlockSpec(memory_space=pltpu.SMEM),
            *[once(a) for a in (act_ext, cot_ext, lo, hi, lo_far, hi_far)],
            cols(sig_t),
            cols(cot_t),
            pl.BlockSpec((3, ch, tile), lambda n: (0, 0, n)),
            pl.BlockSpec((3, tile, ch), lambda n: (0, n, 0)),
        ],
        out_specs=[cols(out), cols(out)],
        out_shape=[out, out],
        scratch_shapes=[
            pltpu.VMEM((3, 2 * SECOND, ch), BF16),
            pltpu.VMEM((3, 2 * FIRST, ch), BF16),
        ],
        compiler_params=pltpu.CompilerParams(vmem_limit_bytes=16 << 20),
        cost_estimate=pl.CostEstimate(
            flops=6 * (2 * SECOND + 2 * FIRST) * ch * ch,
            transcendentals=4 * SECOND * ch,
            bytes_accessed=12 * ch * ch,
        ),
        name="wings",
    )(inside, act_ext, cot_ext, lo, hi, lo_far, hi_far, sig_t, cot_t, w1, w2)


def back_kernel(act_b, lo, hi, grad_m, mid, sig, gm, w1, w2, output, grad_s, a_ext, g_ext, fwd, bwd):
    rows = mid.shape[0]

    @pl.when(pl.program_id(0) == 0)
    def _():
        a_ext[0:SECOND] = lo[0:SECOND]
        a_ext[SECOND : SECOND + rows] = act_b[...]
        a_ext[SECOND + rows :] = hi[0:SECOND]
        g_ext[0:FIRST] = lo[SECOND:]
        g_ext[FIRST : FIRST + rows] = grad_m[...]
        g_ext[FIRST + rows :] = hi[SECOND:]

    total = dot(a_ext[0:rows], w2[0])
    for k in (1, 2):
        total = total + dot(a_ext[k * SECOND : k * SECOND + rows], w2[k])
    fwd[...] = total
    total = dot_nt(g_ext[2 * FIRST : 2 * FIRST + rows], w1[0])
    for k in (1, 2):
        start = (2 - k) * FIRST
        total = total + dot_nt(g_ext[start : start + rows], w1[k])
    bwd[...] = total

    @pl.loop(0, rows // 64)
    def _(i):
        at = pl.ds(pl.multiple_of(i * 64, 64), 64)
        output[at] = (mid[at].astype(F32) + fwd[at]).astype(BF16)
        _, slope = gelu_both(sig[at].astype(F32))
        grad_s[at] = (gm[at].astype(F32) + slope * bwd[at]).astype(BF16)


def back(act_b, lo, hi, grad_m, mid, sig, w1, w2):
    rows, ch = sig.shape
    tile = 256
    cols = pl.BlockSpec((rows, tile), lambda n: (0, n))
    out = jax.ShapeDtypeStruct((rows, ch), BF16)
    return pl.pallas_call(
        back_kernel,
        grid=(ch // tile,),
        in_specs=[
            once(act_b),
            once(lo),
            once(hi),
            once(grad_m),
            cols,
            cols,
            cols,
            pl.BlockSpec((3, tile, ch), lambda n: (0, n, 0)),
            pl.BlockSpec((3, ch, tile), lambda n: (0, 0, n)),
        ],
        out_specs=[cols, cols],
        out_shape=[out, out],
        scratch_shapes=[
            pltpu.VMEM((rows + 2 * SECOND, ch), BF16),
            pltpu.VMEM((rows + 2 * FIRST, ch), BF16),
            pltpu.VMEM((rows, tile), F32),
            pltpu.VMEM((rows, tile), F32),
        ],
        compiler_params=pltpu.CompilerParams(vmem_limit_bytes=16 << 20),
        cost_estimate=pl.CostEstimate(
            flops=12 * rows * ch * ch, transcendentals=rows * ch, bytes_accessed=14 * ch * ch
        ),
        name="rear",
    )(act_b, lo, hi, grad_m, mid, sig, grad_m, w1, w2)


def weight_kernel(parts, lead_x, core, act_b, act_ext, f_all, far_act, right_l2, far_l2, right_l1, far_l1, out):
    nx, ny, nz, units = parts
    rows = act_b.shape[0]

    def emit(left_own, left_far, right_own, right_far, left_at, right_at):
        for k in range(3):
            a, b = left_at(k), right_at(k)
            total = dot_tn(left_own[a : a + rows], right_own[b : b + rows])
            total = total + dot_tn(left_far[a : a + rows], right_far[b : b + rows])
            for j in range(3):
                tile = total[:, j * 128 : (j + 1) * 128].astype(BF16).reshape(nx, nz, 3, 8, 128)
                for g in range(3):
                    unit = k * 9 + j * 3 + g
                    y, i = unit // units, unit % units
                    if lead_x:
                        out[:, y, :, i] = tile[:, :, g]
                    else:
                        out[y, :, :, i] = tile[:, :, g]

    blank = jnp.zeros((nx, nz, 8, 128), BF16)
    if lead_x:
        out[:, ny - 1, :, units - 1] = blank
    else:
        out[ny - 1, :, :, units - 1] = blank

    @pl.when(core[0] == 0)
    def _():
        emit(act_b, f_all, right_l2, far_l2, lambda k: 0, lambda k: (2 - k) * SECOND)

    @pl.when(core[0] != 0)
    def _():
        emit(act_ext, far_act, right_l1, far_l1, lambda k: k * FIRST, lambda k: 0)


def weights(parts, half, core, act_b, act_ext, f_all, far_act, far_cot, grad_m, cot_ext):
    rows, ch = act_b.shape
    tile = ch // 2
    nx, ny, nz, units = parts
    cols = lambda a: pl.BlockSpec(
        (a.shape[0], tile), lambda n: (0, half), pipeline_mode=pl.Buffered(1)
    )
    shape = ((nx, ny) if half == 0 else (ny, nx)) + (nz, units, 8, 128)
    return pl.pallas_call(
        lambda *refs: weight_kernel(parts, half == 0, *refs),
        grid=(1,),
        in_specs=[
            pl.BlockSpec(memory_space=pltpu.SMEM),
            once(act_b),
            once(act_ext),
            once(f_all),
            once(far_act),
            cols(cot_ext),
            cols(far_cot),
            cols(grad_m),
            cols(f_all),
        ],
        out_specs=pl.BlockSpec(shape, lambda n: (0,) * 6),
        out_shape=pltpu.VMEM(shape, BF16),
        compiler_params=pltpu.CompilerParams(vmem_limit_bytes=16 << 20),
        cost_estimate=pl.CostEstimate(
            flops=6 * rows * ch * ch, transcendentals=0, bytes_accessed=6 * ch * ch
        ),
        name="weights",
    )(core, act_b, act_ext, f_all, far_act, cot_ext, far_cot, grad_m, f_all)


def exchange(data, axis, order):
    n = lax.axis_size(axis)
    rest = data.shape[1:]
    total = None
    for k in (0, 1, n - 1, *range(2, n - 1)):
        chunk = lax.dynamic_slice(
            data, (order[k],) + (0,) * len(rest), (1,) + rest, allow_negative_indices=False
        ).reshape(rest)
        if k:
            chunk = lax.ppermute(chunk, axis, [(i, (i + k) % n) for i in range(n)])
        chunk = chunk.astype(F32)
        total = chunk if total is None else total + chunk
    return total.astype(BF16)


def order_of(axis):
    n = lax.axis_size(axis)
    me = lax.axis_index(axis).astype(jnp.int32)
    return [jnp.where(me + k < n, me + k, me + k - n) for k in range(n)]


def neighbours(low, high):
    axes = ("x", "z")
    count = lax.axis_size("x") * lax.axis_size("z")
    forward = [(i, i + 1) for i in range(count - 1)]
    backward = [(t, s) for s, t in forward]
    return lax.ppermute(high, axes, forward), lax.ppermute(low, axes, backward)


def per_device(signal, w1, w2, cotangent):
    sig, cot = signal[0], cotangent[0]
    rows, ch = sig.shape
    nx, ny, nz = (lax.axis_size(a) for a in ("x", "y", "z"))
    tokens = signal.shape[0] * ny * lax.axis_size("c") * rows * nx * nz
    scale = 1.0 / math.sqrt(tokens)
    units = -(-27 // ny)
    core = lax.axis_index("c").astype(jnp.int32).reshape(1)
    place = lax.axis_index("x") * nz + lax.axis_index("z")
    inside = jnp.stack([place > 0, place < nx * nz - 1]).astype(jnp.int32)

    order_x, order_y = order_of("x"), order_of("y")
    sig, cot, core, inside, order_x, order_y = lax.optimization_barrier(
        (sig, cot, core, inside, order_x, order_y)
    )

    low, high, low_far, high_far = edges(sig, cot)
    lo, hi = neighbours(low, high)
    lo_far, hi_far = neighbours(low_far, high_far)
    act = lambda v: gelu(v.astype(F32)).astype(BF16)
    act_ext = jnp.concatenate([act(lo[:FIRST]), act(sig), act(hi[:FIRST])])
    cot_ext = jnp.concatenate([lo[FIRST:], cot, hi[FIRST:]])
    swap = lambda a: lax.ppermute(a, "c", [(0, 1), (1, 0)])
    far_act, far_cot = swap(act_ext), swap(cot_ext)
    mid, act_b, grad_m, give = front(core, act_ext, cot_ext, sig, cot, w1, w2)
    f_all = swap(give)
    parts = (nx, ny, nz, units)
    near = weights(parts, 0, core, act_b, act_ext, f_all, far_act, far_cot, grad_m, cot_ext)
    far = weights(parts, 1, core, act_b, act_ext, f_all, far_act, far_cot, grad_m, cot_ext)
    far, inside = lax.optimization_barrier((far, inside))
    near = exchange(near, "x", order_x)
    far = exchange(far, "y", order_y)
    lo2, hi2 = wings(inside, act_ext, cot_ext, lo, hi, lo_far, hi_far, w1, w2)
    output, grad_s = back(act_b, lo2, hi2, grad_m, mid, sig, w1, w2)
    near, far, output, grad_s = lax.optimization_barrier((near, far, output, grad_s))
    part = jnp.stack([exchange(near, "y", order_y), exchange(far, "x", order_x)], axis=1)

    got = lax.all_to_all(part, "z", 0, 0, tiled=True)
    part = jnp.sum(got.astype(F32), axis=0).astype(BF16)
    both = lax.all_to_all(
        jnp.broadcast_to(part[None], (2 * ny,) + part.shape), ("y", "c"), 0, 0, tiled=True
    )
    both = both.reshape((ny, 2) + part.shape).astype(F32) * scale

    def assemble(layer):
        flat = both[:, layer].transpose(1, 0, 2, 3, 4).reshape(2, ny * units, 8, 128)[:, :27]
        flat = flat.reshape(2, 3, ch // 256, 3, 8, 128).transpose(1, 3, 4, 0, 2, 5)
        return flat.reshape(3, 24, ch)

    return output[None], grad_s[None], assemble(1), assemble(0)


def solution(mesh):
    fine = Mesh(mesh.devices.reshape(4, 8, 4, 2), ("x", "z", "y", "c"))
    placed = P(("y", "c"), ("x", "z"), None)
    split = P(None, ("x", "z"), None)
    return jax.shard_map(
        per_device,
        mesh=fine,
        in_specs=(placed, P(), P(), placed),
        out_specs=(placed, placed, split, split),
        check_vma=False,
    )
```

time: 146 us -> 111 us (0.76)
  the two profiles are of different devices: /device:TPU:13 before, /device:TPU:1 now
where the time goes in v2:
time: 111 us
  starting transfers between devices  33.2 us (30%)
  blocking collectives  28.9 us (26%)
  Pallas kernels  26.2 us (24%)
  waiting for transfers between devices  17.6 us (16%)
  local copies, waits for them, and re-layouts  1.96 us (2%)
  other arithmetic  1.67 us (2%)
    ppermute x12, starting transfers between devices, exchange(): chunk = lax.ppermute(chunk, axis, [(i, (i + k) % n) for i in range(n)])  18.7 us
    all_to_all x1, blocking collectives, per_device(): lax.all_to_all(jnp.broadcast_to(part[None], (2 * ny,) + part.shape), ('y'...  15.6 us
    ppermute x12, waiting for transfers between devices, exchange(): chunk = lax.ppermute(chunk, axis, [(i, (i + k) % n) for i in range(n)])  13.3 us
    all_to_all x1, blocking collectives, per_device(): got = lax.all_to_all(part, 'z', 0, 0, tiled=True)  13.3 us
    ppermute x2, starting transfers between devices, neighbours(): lax.ppermute(high, axes, forward)  8.69 us
    pallas_call x1, Pallas kernels, front(): pl.pallas_call(front_kernel, grid=(ch // tile,), in_specs=[pl.BlockSpec(m...  7.71 us
    pallas_call x1, Pallas kernels, back(): pl.pallas_call(back_kernel, grid=(ch // tile,), in_specs=[once(act_b), on...  7.21 us
    pallas_call x2, Pallas kernels, weights(): pl.pallas_call(lambda *refs: weight_kernel(parts, half == 0, *refs), grid...  5.87 us
  transfers between devices with their start and end apart: 19, of which 7 were waited for; matrix products, arithmetic and copies ran while one was open for 1% of the time, Pallas kernels for 20%

profile of v2, /device:TPU:1, one launch (start us, length us, event | category | flops | bytes accessed | tf_op | source)
XLA Modules:
  0.0 110.5 jit_solution(1580086166356189106)
XLA Ops:
  0.6 0.0 copy-start.2
  0.7 0.1 add_convert_fusion.inside
  0.8 1.5 %edges.1 = (bf16[192,768]{1,0:T(8,128)(2,1)S(1)}, bf16[192,768]{1,0:T(8,128)(2,1)S(1)}, bf16[192,768]{1,0:T(8,128)(2,1)S(1)}, bf16[192,768]{1,0:T(8,128)(2,1)S(1)}) custom-call(bf16[512,768]{1,0:T(8,128)(2,1)} %bitcast.66, bf16[512,768]{1,0:T(8,128)(2,1)} %bitcast.70), custom_call_target="tpu_custom_call" | custom-call | tf_op jit(solution)/shard_map/edges/pallas_call | solution.py:76
  2.2 0.0 copy-start.3
  2.2 4.5 %collective-permute-start = (bf16[192,768]{1,0:T(8,128)(2,1)S(1)}, bf16[192,768]{1,0:T(8,128)(2,1)S(1)}, u32[]{:S(2)}, u32[]{:S(2)}) collective-permute-start(bf16[192,768]{1,0:T(8,128)(2,1)S(1)} %get-tuple-element.37), channel_id=1, source_target_pairs={{0,8},{8,16},{16,24},{24,32},{32,40},{40,48},{48,56},{56,64},{64,7... | collective-permute-start | bytes 884744 | tf_op jit(solution)/shard_map/ppermute | solution.py:373
  6.8 1.3 %collective-permute-start.1 = (bf16[192,768]{1,0:T(8,128)(2,1)S(1)}, bf16[192,768]{1,0:T(8,128)(2,1)S(1)}, u32[]{:S(2)}, u32[]{:S(2)}) collective-permute-start(bf16[192,768]{1,0:T(8,128)(2,1)S(1)} %get-tuple-element.38), channel_id=1, source_target_pairs={{8,0},{16,8},{24,16},{32,24},{40,32},{48,40},{56,48},{64,56},{72,6... | collective-permute-start | bytes 884744 | tf_op jit(solution)/shard_map/ppermute | solution.py:373
  8.1 4.2 %collective-permute-start.11 = (bf16[192,768]{1,0:T(8,128)(2,1)S(1)}, bf16[192,768]{1,0:T(8,128)(2,1)S(1)}, u32[]{:S(2)}, u32[]{:S(2)}) collective-permute-start(bf16[192,768]{1,0:T(8,128)(2,1)S(1)} %get-tuple-element.53), channel_id=1, source_target_pairs={{0,8},{8,16},{16,24},{24,32},{32,40},{40,48},{48,56},{56,64},{64,7... | collective-permute-start | bytes 884744 | tf_op jit(solution)/shard_map/ppermute | solution.py:373
  12.3 1.3 %collective-permute-start.12 = (bf16[192,768]{1,0:T(8,128)(2,1)S(1)}, bf16[192,768]{1,0:T(8,128)(2,1)S(1)}, u32[]{:S(2)}, u32[]{:S(2)}) collective-permute-start(bf16[192,768]{1,0:T(8,128)(2,1)S(1)} %get-tuple-element.54), channel_id=1, source_target_pairs={{8,0},{16,8},{24,16},{32,24},{40,32},{48,40},{56,48},{64,56},{72,6... | collective-permute-start | bytes 884744 | tf_op jit(solution)/shard_map/ppermute | solution.py:373
  13.6 0.0 copy-done.2
  13.6 0.5 fusion.1
  14.1 0.0 collective-permute-done.lo
  14.1 2.4 %collective-permute-done.1.hi = bf16[192,768]{1,0:T(8,128)(2,1)S(1)} collective-permute-done((bf16[192,768]{1,0:T(8,128)(2,1)S(1)}, bf16[192,768]{1,0:T(8,128)(2,1)S(1)}, u32[]{:S(2)}, u32[]{:S(2)}) %collective-permute-start.1) | collective-permute-done | bytes 294944 | tf_op jit(solution)/shard_map/ppermute | solution.py:373
  16.6 0.1 pad_maximum_fusion.cot_ext.refs_5_
  16.7 2.5 %collective-permute-start.4 = (bf16[768,768]{1,0:T(8,128)(2,1)S(1)}, bf16[768,768]{1,0:T(8,128)(2,1)S(1)}, u32[]{:S(2)}, u32[]{:S(2)}) collective-permute-start(bf16[768,768]{1,0:T(8,128)(2,1)S(1)} %pad_maximum_fusion.cot_ext.refs_5_), channel_id=1, source_target_pairs={{0,1},{1,0},{2,3},{3,2},{4,5},{5,4},{6,7},{7,6},{8,9},{9,8},{10,11... | collective-permute-start | bytes 3538952 | tf_op jit(solution)/shard_map/ppermute | solution.py:398
  19.2 0.1 fusion.18
  19.3 0.1 fusion.23
  19.4 0.1 pad_maximum_fusion.1.act.refs_2_
  19.5 0.1 collective-permute-start.3
  19.6 7.7 %front.1 = (bf16[512,768]{1,0:T(8,128)(2,1)S(1)}, bf16[512,768]{1,0:T(8,128)(2,1)S(1)}, bf16[512,768]{1,0:T(8,128)(2,1)S(1)}, bf16[512,768]{1,0:T(8,128)(2,1)S(1)}) custom-call(s32[1]{0:T(128)} %bitcast.2.core.refs_0_, bf16[640,768]{1,0:T(8,128)(2,1)S(1)} %pad_maximum_fusion.1.act.refs_2_, bf16[768,768]{1,0:T(8,128)(2,1)S(1)} %pad_maximum_fusion.cot_ext.refs_5_, ...), custom_call_target="tpu_custom_call" | custom-call | flops 3623878656 | bytes 8257536 | tf_op jit(solution)/shard_map/front/pallas_call | solution.py:120
  27.3 0.6 collective-permute-start.2
  27.8 0.0 collective-permute-done.11.lo_far
  27.9 0.0 collective-permute-done.12.hi_far
  28.0 1.8 %collective-permute-done.2.refs_3_.refs_8_ = bf16[512,768]{1,0:T(8,128)(2,1)S(1)} collective-permute-done((bf16[512,768]{1,0:T(8,128)(2,1)S(1)}, bf16[512,768]{1,0:T(8,128)(2,1)S(1)}, u32[]{:S(2)}, u32[]{:S(2)}) %collective-permute-start.2) | collective-permute-done | bytes 786464 | tf_op jit(solution)/shard_map/ppermute | solution.py:398
  29.8 0.0 collective-permute-done.3.refs_4_
  29.8 0.0 collective-permute-done.4.refs_6_
  29.8 2.8 %weights.3 = bf16[4,4,8,7,8,128]{5,4,3,2,1,0:T(8,128)(2,1)S(1)} custom-call(s32[1]{0:T(128)} %bitcast.2.core.refs_0_, bf16[512,768]{1,0:T(8,128)(2,1)S(1)} %get-tuple-element.39.refs_1_.act_b, bf16[640,768]{1,0:T(8,128)(2,1)S(1)} %pad_maximum_fusion.1.act.refs_2_, bf16[512,768]{1,0:T(8,128)(2,1)S(1)} %collective-permute-done.2.refs_3_.refs_8_, ...), custom_call_target="tpu_custom_call" | custom-call | flops 1811939328 | bytes 3538944 | tf_op jit(solution)/shard_map/weights/pallas_call | solution.py:323
  32.6 0.1 dynamic-slice_bitcast_fusion.2
  32.7 3.0 %collective-permute-start.10 = (bf16[4,8,7,8,128]{4,3,2,1,0:T(8,128)(2,1)S(1)}, bf16[4,8,7,8,128]{4,3,2,1,0:T(8,128)(2,1)S(1)}, u32[]{:S(2)}, u32[]{:S(2)}) collective-permute-start(bf16[4,8,7,8,128]{4,3,2,1,0:T(8,128)(2,1)S(1)} %get-tuple-element.65), channel_id=1, source_target_pairs={{0,4},{2,6},{4,0},{6,2},{1,5},{3,7},{5,1},{7,3},{8,12},{10,14},{12... | collective-permute-start | bytes 1376264 | tf_op jit(solution)/shard_map/ppermute | solution.py:356
  35.8 0.5 collective-permute-start.8
  36.2 2.3 %collective-permute-start.9 = (bf16[4,8,7,8,128]{4,3,2,1,0:T(8,128)(2,1)S(1)}, bf16[4,8,7,8,128]{4,3,2,1,0:T(8,128)(2,1)S(1)}, u32[]{:S(2)}, u32[]{:S(2)}) collective-permute-start(bf16[4,8,7,8,128]{4,3,2,1,0:T(8,128)(2,1)S(1)} %get-tuple-element.66), channel_id=1, source_target_pairs={{0,6},{2,0},{4,2},{6,4},{1,7},{3,1},{5,3},{7,5},{8,14},{10,8},{12,... | collective-permute-start | bytes 1376264 | tf_op jit(solution)/shard_map/ppermute | solution.py:356
  38.5 3.0 %weights.2 = bf16[4,4,8,7,8,128]{5,4,3,2,1,0:T(8,128)(2,1)S(1)} custom-call(s32[1]{0:T(128)} %bitcast.2.core.refs_0_, bf16[512,768]{1,0:T(8,128)(2,1)S(1)} %get-tuple-element.39.refs_1_.act_b, bf16[640,768]{1,0:T(8,128)(2,1)S(1)} %pad_maximum_fusion.1.act.refs_2_, bf16[512,768]{1,0:T(8,128)(2,1)S(1)} %collective-permute-done.2.refs_3_.refs_8_, ...), custom_call_target="tpu_custom_call" | custom-call | flops 1811939328 | bytes 3538944 | tf_op jit(solution)/shard_map/weights/pallas_call | solution.py:323
  41.6 0.1 dynamic-slice_bitcast_fusion.5
  41.7 4.4 %collective-permute-start.5 = (bf16[4,8,7,8,128]{4,3,2,1,0:T(8,128)(2,1)S(1)}, bf16[4,8,7,8,128]{4,3,2,1,0:T(8,128)(2,1)S(1)}, u32[]{:S(2)}, u32[]{:S(2)}) collective-permute-start(bf16[4,8,7,8,128]{4,3,2,1,0:T(8,128)(2,1)S(1)} %get-tuple-element.67), channel_id=1, source_target_pairs={{0,64},{64,128},{128,192},{192,0},{1,65},{65,129},{129,193},{193,1... | collective-permute-start | bytes 1376264 | tf_op jit(solution)/shard_map/ppermute | solution.py:356
  46.1 1.6 %collective-permute-start.6 = (bf16[4,8,7,8,128]{4,3,2,1,0:T(8,128)(2,1)S(1)}, bf16[4,8,7,8,128]{4,3,2,1,0:T(8,128)(2,1)S(1)}, u32[]{:S(2)}, u32[]{:S(2)}) collective-permute-start(bf16[4,8,7,8,128]{4,3,2,1,0:T(8,128)(2,1)S(1)} %get-tuple-element.69), channel_id=1, source_target_pairs={{0,192},{64,0},{128,64},{192,128},{1,193},{65,1},{129,65},{193,129... | collective-permute-start | bytes 1376264 | tf_op jit(solution)/shard_map/ppermute | solution.py:356
  47.7 0.0 copy-done
  47.7 4.0 %wings.1 = (bf16[192,768]{1,0:T(8,128)(2,1)S(1)}, bf16[192,768]{1,0:T(8,128)(2,1)S(1)}) custom-call(s32[2]{0:T(128)S(1)} %add_convert_fusion.inside, bf16[640,768]{1,0:T(8,128)(2,1)S(1)} %pad_maximum_fusion.1.act.refs_2_, bf16[768,768]{1,0:T(8,128)(2,1)S(1)} %pad_maximum_fusion.cot_ext.refs_5_, bf16[192,768]{1,0:T(8,128)(2,1)S(1)} %collective-permute-done.lo, ...), custom_call_target="tpu_custom_call" | custom-call | flops 1358954496 | bytes 7077888 | tf_op jit(solution)/shard_map/wings/pallas_call | solution.py:189
  51.7 0.0 collective-permute-done.10
  51.7 1.4 %collective-permute-start.7 = (bf16[4,8,7,8,128]{4,3,2,1,0:T(8,128)(2,1)S(1)}, bf16[4,8,7,8,128]{4,3,2,1,0:T(8,128)(2,1)S(1)}, u32[]{:S(2)}, u32[]{:S(2)}) collective-permute-start(bf16[4,8,7,8,128]{4,3,2,1,0:T(8,128)(2,1)S(1)} %get-tuple-element.68), channel_id=1, source_target_pairs={{0,128},{64,192},{128,0},{192,64},{1,129},{65,193},{129,1},{193,65... | collective-permute-start | bytes 1376264 | tf_op jit(solution)/shard_map/ppermute | solution.py:356
  53.2 7.2 %rear.1 = (bf16[512,768]{1,0:T(8,128)(2,1)}, bf16[512,768]{1,0:T(8,128)(2,1)}) custom-call(bf16[512,768]{1,0:T(8,128)(2,1)S(1)} %get-tuple-element.39.refs_1_.act_b, bf16[192,768]{1,0:T(8,128)(2,1)S(1)} %get-tuple-element.55.lo, bf16[192,768]{1,0:T(8,128)(2,1)S(1)} %get-tuple-element.56.hi, bf16[512,768]{1,0:T(8,128)(2,1)S(1)} %get-tuple-element.41.refs_7_.grad_m.gm, ...), custom_call_target="tpu_custom_call" | custom-call | flops 3623878656 | bytes 8257536 | tf_op jit(solution)/shard_map/rear/pallas_call | solution.py:251
  60.4 0.0 collective-permute-done.8
  60.4 0.0 collective-permute-done.9
  60.4 0.2 fusion.7
  60.6 0.0 collective-permute-done.5
  60.6 0.0 collective-permute-done.6
  60.6 7.3 %collective-permute-done.7 = bf16[4,8,7,8,128]{4,3,2,1,0:T(8,128)(2,1)S(1)} collective-permute-done((bf16[4,8,7,8,128]{4,3,2,1,0:T(8,128)(2,1)S(1)}, bf16[4,8,7,8,128]{4,3,2,1,0:T(8,128)(2,1)S(1)}, u32[]{:S(2)}, u32[]{:S(2)}) %collective-permute-start.7) | collective-permute-done | bytes 458784 | tf_op jit(solution)/shard_map/ppermute | solution.py:356
  68.0 0.2 fusion.10
  68.3 0.1 collective-permute-start.13
  68.3 2.7 %collective-permute-start.14 = (bf16[8,7,8,128]{3,2,1,0:T(8,128)(2,1)S(1)}, bf16[8,7,8,128]{3,2,1,0:T(8,128)(2,1)S(1)}, u32[]{:S(2)}, u32[]{:S(2)}) collective-permute-start(bf16[8,7,8,128]{3,2,1,0:T(8,128)(2,1)S(1)} %get-tuple-element.74), channel_id=1, source_target_pairs={{0,6},{2,0},{4,2},{6,4},{1,7},{3,1},{5,3},{7,5},{8,14},{10,8},{12,... | collective-permute-start | bytes 344072 | tf_op jit(solution)/shard_map/ppermute | solution.py:356
  71.0 0.0 collective-permute-start.15
  71.0 0.7 collective-permute-start.16
  71.7 2.1 %collective-permute-start.17 = (bf16[8,7,8,128]{3,2,1,0:T(8,128)(2,1)S(1)}, bf16[8,7,8,128]{3,2,1,0:T(8,128)(2,1)S(1)}, u32[]{:S(2)}, u32[]{:S(2)}) collective-permute-start(bf16[8,7,8,128]{3,2,1,0:T(8,128)(2,1)S(1)} %get-tuple-element.77), channel_id=1, source_target_pairs={{0,192},{64,0},{128,64},{192,128},{1,193},{65,1},{129,65},{193,129... | collective-permute-start | bytes 344072 | tf_op jit(solution)/shard_map/ppermute | solution.py:356
  73.8 0.0 collective-permute-done.13
  73.8 0.0 collective-permute-start.18
  73.8 0.2 collective-permute-done.14
  74.0 2.3 %collective-permute-done.15 = bf16[8,7,8,128]{3,2,1,0:T(8,128)(2,1)S(1)} collective-permute-done((bf16[8,7,8,128]{3,2,1,0:T(8,128)(2,1)S(1)}, bf16[8,7,8,128]{3,2,1,0:T(8,128)(2,1)S(1)}, u32[]{:S(2)}, u32[]{:S(2)}) %collective-permute-start.15) | collective-permute-done | bytes 114720 | tf_op jit(solution)/shard_map/ppermute | solution.py:356
  76.3 0.1 fusion.27
  76.3 0.0 collective-permute-done.16
  76.3 0.4 collective-permute-done.17
  76.8 3.1 %collective-permute-done.18 = bf16[8,7,8,128]{3,2,1,0:T(8,128)(2,1)S(1)} collective-permute-done((bf16[8,7,8,128]{3,2,1,0:T(8,128)(2,1)S(1)}, bf16[8,7,8,128]{3,2,1,0:T(8,128)(2,1)S(1)}, u32[]{:S(2)}, u32[]{:S(2)}) %collective-permute-start.18) | collective-permute-done | bytes 114720 | tf_op jit(solution)/shard_map/ppermute | solution.py:356
  79.9 0.1 fusion.28
  80.0 13.3 %all_to_all.10 = bf16[8,2,7,8,128]{4,3,2,1,0:T(8,128)(2,1)S(1)} all-to-all(bf16[8,2,7,8,128]{4,3,2,1,0:T(8,128)(2,1)S(1)} %copy.12), channel_id=1, replica_groups=mesh['x'=4,'z'=8,'y'=4,'c'=2] {'z'}, dimensions={0} | all-to-all | bytes 458752 | tf_op jit(solution)/shard_map/all_to_all | solution.py:413
  93.4 15.6 %all_to_all.11 = bf16[8,2,7,8,128]{4,3,2,1,0:T(8,128)(2,1)S(1)} all-to-all(bf16[8,2,7,8,128]{4,3,2,1,0:T(8,128)(2,1)S(1)} %broadcast_in_dim.14), channel_id=1, replica_groups=mesh['x'=4,'z'=8,'y'=4,'c'=2] {'y','c'}, dimensions={0} | all-to-all | bytes 458752 | tf_op jit(solution)/shard_map/all_to_all | solution.py:415
  109.1 0.7 copy.14
  109.8 0.7 copy.16
  (24 shorter events, 0.4 us)
Async XLA Ops:
  0.6 12.9 %copy-start.2 = (bf16[1,512,768]{2,1,0:T(8,128)(2,1)S(1)}, bf16[1,512,768]{2,1,0:T(8,128)(2,1)}, u32[]{:S(2)}) copy-start(bf16[1,512,768]{2,1,0:T(8,128)(2,1)} %param.4) | copy-start | bytes 2359300
  2.2 14.4 %copy-start.3 = (bf16[1,512,768]{2,1,0:T(8,128)(2,1)S(1)}, bf16[1,512,768]{2,1,0:T(8,128)(2,1)}, u32[]{:S(2)}) copy-start(bf16[1,512,768]{2,1,0:T(8,128)(2,1)} %param.7) | copy-start | bytes 2359300
  2.2 11.9 %collective-permute-start = (bf16[192,768]{1,0:T(8,128)(2,1)S(1)}, bf16[192,768]{1,0:T(8,128)(2,1)S(1)}, u32[]{:S(2)}, u32[]{:S(2)}) collective-permute-start(bf16[192,768]{1,0:T(8,128)(2,1)S(1)} %get-tuple-element.37), channel_id=1, source_target_pairs={{0,8},{8,16},{16,24},{24,32},{32,40},{40,48},{48,56},{56,64},{64,7... | collective-permute-start | bytes 884744 | tf_op jit(solution)/shard_map/ppermute | solution.py:373
  6.8 9.8 %collective-permute-start.1 = (bf16[192,768]{1,0:T(8,128)(2,1)S(1)}, bf16[192,768]{1,0:T(8,128)(2,1)S(1)}, u32[]{:S(2)}, u32[]{:S(2)}) collective-permute-start(bf16[192,768]{1,0:T(8,128)(2,1)S(1)} %get-tuple-element.38), channel_id=1, source_target_pairs={{8,0},{16,8},{24,16},{32,24},{40,32},{48,40},{56,48},{64,56},{72,6... | collective-permute-start | bytes 884744 | tf_op jit(solution)/shard_map/ppermute | solution.py:373
  8.1 19.8 %collective-permute-start.11 = (bf16[192,768]{1,0:T(8,128)(2,1)S(1)}, bf16[192,768]{1,0:T(8,128)(2,1)S(1)}, u32[]{:S(2)}, u32[]{:S(2)}) collective-permute-start(bf16[192,768]{1,0:T(8,128)(2,1)S(1)} %get-tuple-element.53), channel_id=1, source_target_pairs={{0,8},{8,16},{16,24},{24,32},{32,40},{40,48},{48,56},{56,64},{64,7... | collective-permute-start | bytes 884744 | tf_op jit(solution)/shard_map/ppermute | solution.py:373
  12.3 15.6 %collective-permute-start.12 = (bf16[192,768]{1,0:T(8,128)(2,1)S(1)}, bf16[192,768]{1,0:T(8,128)(2,1)S(1)}, u32[]{:S(2)}, u32[]{:S(2)}) collective-permute-start(bf16[192,768]{1,0:T(8,128)(2,1)S(1)} %get-tuple-element.54), channel_id=1, source_target_pairs={{8,0},{16,8},{24,16},{32,24},{40,32},{48,40},{56,48},{64,56},{72,6... | collective-permute-start | bytes 884744 | tf_op jit(solution)/shard_map/ppermute | solution.py:373
  16.7 13.1 %collective-permute-start.4 = (bf16[768,768]{1,0:T(8,128)(2,1)S(1)}, bf16[768,768]{1,0:T(8,128)(2,1)S(1)}, u32[]{:S(2)}, u32[]{:S(2)}) collective-permute-start(bf16[768,768]{1,0:T(8,128)(2,1)S(1)} %pad_maximum_fusion.cot_ext.refs_5_), channel_id=1, source_target_pairs={{0,1},{1,0},{2,3},{3,2},{4,5},{5,4},{6,7},{7,6},{8,9},{9,8},{10,11... | collective-permute-start | bytes 3538952 | tf_op jit(solution)/shard_map/ppermute | solution.py:398
  19.5 10.3 %collective-permute-start.3 = (bf16[640,768]{1,0:T(8,128)(2,1)S(1)}, bf16[640,768]{1,0:T(8,128)(2,1)S(1)}, u32[]{:S(2)}, u32[]{:S(2)}) collective-permute-start(bf16[640,768]{1,0:T(8,128)(2,1)S(1)} %pad_maximum_fusion.1.act.refs_2_), channel_id=1, source_target_pairs={{0,1},{1,0},{2,3},{3,2},{4,5},{5,4},{6,7},{7,6},{8,9},{9,8},{10,11... | collective-permute-start | bytes 2949128 | tf_op jit(solution)/shard_map/ppermute | solution.py:398
  27.3 2.5 %collective-permute-start.2 = (bf16[512,768]{1,0:T(8,128)(2,1)S(1)}, bf16[512,768]{1,0:T(8,128)(2,1)S(1)}, u32[]{:S(2)}, u32[]{:S(2)}) collective-permute-start(bf16[512,768]{1,0:T(8,128)(2,1)S(1)} %get-tuple-element.40), channel_id=1, source_target_pairs={{0,1},{1,0},{2,3},{3,2},{4,5},{5,4},{6,7},{7,6},{8,9},{9,8},{10,11... | collective-permute-start | bytes 2359304 | tf_op jit(solution)/shard_map/ppermute | solution.py:398
  32.7 19.0 %collective-permute-start.10 = (bf16[4,8,7,8,128]{4,3,2,1,0:T(8,128)(2,1)S(1)}, bf16[4,8,7,8,128]{4,3,2,1,0:T(8,128)(2,1)S(1)}, u32[]{:S(2)}, u32[]{:S(2)}) collective-permute-start(bf16[4,8,7,8,128]{4,3,2,1,0:T(8,128)(2,1)S(1)} %get-tuple-element.65), channel_id=1, source_target_pairs={{0,4},{2,6},{4,0},{6,2},{1,5},{3,7},{5,1},{7,3},{8,12},{10,14},{12... | collective-permute-start | bytes 1376264 | tf_op jit(solution)/shard_map/ppermute | solution.py:356
  35.8 24.6 %collective-permute-start.8 = (bf16[4,8,7,8,128]{4,3,2,1,0:T(8,128)(2,1)S(1)}, bf16[4,8,7,8,128]{4,3,2,1,0:T(8,128)(2,1)S(1)}, u32[]{:S(2)}, u32[]{:S(2)}) collective-permute-start(bf16[4,8,7,8,128]{4,3,2,1,0:T(8,128)(2,1)S(1)} %get-tuple-element.64), channel_id=1, source_target_pairs={{0,2},{2,4},{4,6},{6,0},{1,3},{3,5},{5,7},{7,1},{8,10},{10,12},{12... | collective-permute-start | bytes 1376264 | tf_op jit(solution)/shard_map/ppermute | solution.py:356
  36.2 24.1 %collective-permute-start.9 = (bf16[4,8,7,8,128]{4,3,2,1,0:T(8,128)(2,1)S(1)}, bf16[4,8,7,8,128]{4,3,2,1,0:T(8,128)(2,1)S(1)}, u32[]{:S(2)}, u32[]{:S(2)}) collective-permute-start(bf16[4,8,7,8,128]{4,3,2,1,0:T(8,128)(2,1)S(1)} %get-tuple-element.66), channel_id=1, source_target_pairs={{0,6},{2,0},{4,2},{6,4},{1,7},{3,1},{5,3},{7,5},{8,14},{10,8},{12,... | collective-permute-start | bytes 1376264 | tf_op jit(solution)/shard_map/ppermute | solution.py:356
  38.5 9.2 %copy-start = (bf16[3,768,768]{2,1,0:T(8,128)(2,1)S(1)}, bf16[3,768,768]{2,1,0:T(8,128)(2,1)}, u32[]{:S(2)}) copy-start(bf16[3,768,768]{2,1,0:T(8,128)(2,1)} %w1.5) | copy-start | bytes 10616836
  38.5 9.2 %copy-start.1 = (bf16[3,768,768]{2,1,0:T(8,128)(2,1)S(1)}, bf16[3,768,768]{2,1,0:T(8,128)(2,1)}, u32[]{:S(2)}) copy-start(bf16[3,768,768]{2,1,0:T(8,128)(2,1)} %w2.5) | copy-start | bytes 10616836
  41.7 18.9 %collective-permute-start.5 = (bf16[4,8,7,8,128]{4,3,2,1,0:T(8,128)(2,1)S(1)}, bf16[4,8,7,8,128]{4,3,2,1,0:T(8,128)(2,1)S(1)}, u32[]{:S(2)}, u32[]{:S(2)}) collective-permute-start(bf16[4,8,7,8,128]{4,3,2,1,0:T(8,128)(2,1)S(1)} %get-tuple-element.67), channel_id=1, source_target_pairs={{0,64},{64,128},{128,192},{192,0},{1,65},{65,129},{129,193},{193,1... | collective-permute-start | bytes 1376264 | tf_op jit(solution)/shard_map/ppermute | solution.py:356
  46.1 14.6 %collective-permute-start.6 = (bf16[4,8,7,8,128]{4,3,2,1,0:T(8,128)(2,1)S(1)}, bf16[4,8,7,8,128]{4,3,2,1,0:T(8,128)(2,1)S(1)}, u32[]{:S(2)}, u32[]{:S(2)}) collective-permute-start(bf16[4,8,7,8,128]{4,3,2,1,0:T(8,128)(2,1)S(1)} %get-tuple-element.69), channel_id=1, source_target_pairs={{0,192},{64,0},{128,64},{192,128},{1,193},{65,1},{129,65},{193,129... | collective-permute-start | bytes 1376264 | tf_op jit(solution)/shard_map/ppermute | solution.py:356
  51.7 16.3 %collective-permute-start.7 = (bf16[4,8,7,8,128]{4,3,2,1,0:T(8,128)(2,1)S(1)}, bf16[4,8,7,8,128]{4,3,2,1,0:T(8,128)(2,1)S(1)}, u32[]{:S(2)}, u32[]{:S(2)}) collective-permute-start(bf16[4,8,7,8,128]{4,3,2,1,0:T(8,128)(2,1)S(1)} %get-tuple-element.68), channel_id=1, source_target_pairs={{0,128},{64,192},{128,0},{192,64},{1,129},{65,193},{129,1},{193,65... | collective-permute-start | bytes 1376264 | tf_op jit(solution)/shard_map/ppermute | solution.py:356
  68.3 5.5 %collective-permute-start.13 = (bf16[8,7,8,128]{3,2,1,0:T(8,128)(2,1)S(1)}, bf16[8,7,8,128]{3,2,1,0:T(8,128)(2,1)S(1)}, u32[]{:S(2)}, u32[]{:S(2)}) collective-permute-start(bf16[8,7,8,128]{3,2,1,0:T(8,128)(2,1)S(1)} %get-tuple-element.72), channel_id=1, source_target_pairs={{0,2},{2,4},{4,6},{6,0},{1,3},{3,5},{5,7},{7,1},{8,10},{10,12},{12... | collective-permute-start | bytes 344072 | tf_op jit(solution)/shard_map/ppermute | solution.py:356
  68.3 5.6 %collective-permute-start.14 = (bf16[8,7,8,128]{3,2,1,0:T(8,128)(2,1)S(1)}, bf16[8,7,8,128]{3,2,1,0:T(8,128)(2,1)S(1)}, u32[]{:S(2)}, u32[]{:S(2)}) collective-permute-start(bf16[8,7,8,128]{3,2,1,0:T(8,128)(2,1)S(1)} %get-tuple-element.74), channel_id=1, source_target_pairs={{0,6},{2,0},{4,2},{6,4},{1,7},{3,1},{5,3},{7,5},{8,14},{10,8},{12,... | collective-permute-start | bytes 344072 | tf_op jit(solution)/shard_map/ppermute | solution.py:356
  71.0 5.3 %collective-permute-start.15 = (bf16[8,7,8,128]{3,2,1,0:T(8,128)(2,1)S(1)}, bf16[8,7,8,128]{3,2,1,0:T(8,128)(2,1)S(1)}, u32[]{:S(2)}, u32[]{:S(2)}) collective-permute-start(bf16[8,7,8,128]{3,2,1,0:T(8,128)(2,1)S(1)} %get-tuple-element.73), channel_id=1, source_target_pairs={{0,4},{2,6},{4,0},{6,2},{1,5},{3,7},{5,1},{7,3},{8,12},{10,14},{12... | collective-permute-start | bytes 344072 | tf_op jit(solution)/shard_map/ppermute | solution.py:356
  71.0 5.3 %collective-permute-start.16 = (bf16[8,7,8,128]{3,2,1,0:T(8,128)(2,1)S(1)}, bf16[8,7,8,128]{3,2,1,0:T(8,128)(2,1)S(1)}, u32[]{:S(2)}, u32[]{:S(2)}) collective-permute-start(bf16[8,7,8,128]{3,2,1,0:T(8,128)(2,1)S(1)} %get-tuple-element.75), channel_id=1, source_target_pairs={{0,64},{64,128},{128,192},{192,0},{1,65},{65,129},{129,193},{193,1... | collective-permute-start | bytes 344072 | tf_op jit(solution)/shard_map/ppermute | solution.py:356
  71.7 5.1 %collective-permute-start.17 = (bf16[8,7,8,128]{3,2,1,0:T(8,128)(2,1)S(1)}, bf16[8,7,8,128]{3,2,1,0:T(8,128)(2,1)S(1)}, u32[]{:S(2)}, u32[]{:S(2)}) collective-permute-start(bf16[8,7,8,128]{3,2,1,0:T(8,128)(2,1)S(1)} %get-tuple-element.77), channel_id=1, source_target_pairs={{0,192},{64,0},{128,64},{192,128},{1,193},{65,1},{129,65},{193,129... | collective-permute-start | bytes 344072 | tf_op jit(solution)/shard_map/ppermute | solution.py:356
  73.8 6.1 %collective-permute-start.18 = (bf16[8,7,8,128]{3,2,1,0:T(8,128)(2,1)S(1)}, bf16[8,7,8,128]{3,2,1,0:T(8,128)(2,1)S(1)}, u32[]{:S(2)}, u32[]{:S(2)}) collective-permute-start(bf16[8,7,8,128]{3,2,1,0:T(8,128)(2,1)S(1)} %get-tuple-element.76), channel_id=1, source_target_pairs={{0,128},{64,192},{128,0},{192,64},{1,129},{65,193},{129,1},{193,65... | collective-permute-start | bytes 344072 | tf_op jit(solution)/shard_map/ppermute | solution.py:356

commit v3 on v2

--- a/solution.py
+++ b/solution.py
@@ -2,6 +2,7 @@
 
 import jax
 import jax.numpy as jnp
+import numpy as np
 from jax import lax
 from jax.experimental import pallas as pl
 from jax.experimental.pallas import tpu as pltpu
@@ -278,50 +279,52 @@
     )(act_b, lo, hi, grad_m, mid, sig, grad_m, w1, w2)
 
 
-def weight_kernel(parts, lead_x, core, act_b, act_ext, f_all, far_act, right_l2, far_l2, right_l1, far_l1, out):
+def weight_kernel(parts, core, act_b, act_ext, f_all, far_act, right_l2, far_l2, right_l1, far_l1, out):
     nx, ny, nz, units = parts
     rows = act_b.shape[0]
-
-    def emit(left_own, left_far, right_own, right_far, left_at, right_at):
+    tiles = right_l2.shape[1] // 128
+    count = 9 * tiles
+
+    def emit(left_own, left_far, right_own, right_far, left_at, right_at, lead_x):
         for k in range(3):
             a, b = left_at(k), right_at(k)
             total = dot_tn(left_own[a : a + rows], right_own[b : b + rows])
             total = total + dot_tn(left_far[a : a + rows], right_far[b : b + rows])
-            for j in range(3):
+            for j in range(tiles):
                 tile = total[:, j * 128 : (j + 1) * 128].astype(BF16).reshape(nx, nz, 3, 8, 128)
                 for g in range(3):
-                    unit = k * 9 + j * 3 + g
+                    unit = (k * tiles + j) * 3 + g
                     y, i = unit // units, unit % units
                     if lead_x:
                         out[:, y, :, i] = tile[:, :, g]
                     else:
                         out[y, :, :, i] = tile[:, :, g]
-
-    blank = jnp.zeros((nx, nz, 8, 128), BF16)
-    if lead_x:
-        out[:, ny - 1, :, units - 1] = blank
-    else:
-        out[ny - 1, :, :, units - 1] = blank
+        for unit in range(count, ny * units):
+            y, i = unit // units, unit % units
+            blank = jnp.zeros((nx, nz, 8, 128), BF16)
+            if lead_x:
+                out[:, y, :, i] = blank
+            else:
+                out[y, :, :, i] = blank
 
     @pl.when(core[0] == 0)
     def _():
-        emit(act_b, f_all, right_l2, far_l2, lambda k: 0, lambda k: (2 - k) * SECOND)
+        emit(act_b, f_all, right_l2, far_l2, lambda k: 0, lambda k: (2 - k) * SECOND, True)
 
     @pl.when(core[0] != 0)
     def _():
-        emit(act_ext, far_act, right_l1, far_l1, lambda k: k * FIRST, lambda k: 0)
-
-
-def weights(parts, half, core, act_b, act_ext, f_all, far_act, far_cot, grad_m, cot_ext):
+        emit(act_ext, far_act, right_l1, far_l1, lambda k: k * FIRST, lambda k: 0, False)
+
+
+def weights(parts, start, width, core, act_b, act_ext, f_all, far_act, far_cot, grad_m, cot_ext):
     rows, ch = act_b.shape
-    tile = ch // 2
     nx, ny, nz, units = parts
     cols = lambda a: pl.BlockSpec(
-        (a.shape[0], tile), lambda n: (0, half), pipeline_mode=pl.Buffered(1)
+        (a.shape[0], width), lambda n: (0, start // width), pipeline_mode=pl.Buffered(1)
     )
-    shape = ((nx, ny) if half == 0 else (ny, nx)) + (nz, units, 8, 128)
+    shape = (nx, ny, nz, units, 8, 128)
     return pl.pallas_call(
-        lambda *refs: weight_kernel(parts, half == 0, *refs),
+        lambda *refs: weight_kernel(parts, *refs),
         grid=(1,),
         in_specs=[
             pl.BlockSpec(memory_space=pltpu.SMEM),
@@ -336,32 +339,42 @@
         ],
         out_specs=pl.BlockSpec(shape, lambda n: (0,) * 6),
         out_shape=pltpu.VMEM(shape, BF16),
-        compiler_params=pltpu.CompilerParams(vmem_limit_bytes=16 << 20),
+        compiler_params=pltpu.CompilerParams(vmem_limit_bytes=20 << 20),
         cost_estimate=pl.CostEstimate(
-            flops=6 * rows * ch * ch, transcendentals=0, bytes_accessed=6 * ch * ch
+            flops=12 * rows * ch * width, transcendentals=0, bytes_accessed=12 * ch * width
         ),
         name="weights",
     )(core, act_b, act_ext, f_all, far_act, cot_ext, far_cot, grad_m, f_all)
 
 
-def exchange(data, axis, order):
-    n = lax.axis_size(axis)
+def exchange(data, order, core_axis):
+    axes = ("x", "z", "y", "c")
+    sizes = [lax.axis_size(a) for a in axes]
+    n = data.shape[0]
     rest = data.shape[1:]
+
+    def pairs(k):
+        found = []
+        for i in range(math.prod(sizes)):
+            place = list(np.unravel_index(i, sizes))
+            at = axes.index(core_axis[place[3]])
+            place[at] = (place[at] + k) % n
+            found.append((i, int(np.ravel_multi_index(place, sizes))))
+        return found
+
     total = None
     for k in (0, 1, n - 1, *range(2, n - 1)):
         chunk = lax.dynamic_slice(
             data, (order[k],) + (0,) * len(rest), (1,) + rest, allow_negative_indices=False
         ).reshape(rest)
         if k:
-            chunk = lax.ppermute(chunk, axis, [(i, (i + k) % n) for i in range(n)])
+            chunk = lax.ppermute(chunk, axes, pairs(k))
         chunk = chunk.astype(F32)
         total = chunk if total is None else total + chunk
     return total.astype(BF16)
 
 
-def order_of(axis):
-    n = lax.axis_size(axis)
-    me = lax.axis_index(axis).astype(jnp.int32)
+def order_of(me, n):
     return [jnp.where(me + k < n, me + k, me + k - n) for k in range(n)]
 
 
@@ -379,14 +392,18 @@
     nx, ny, nz = (lax.axis_size(a) for a in ("x", "y", "z"))
     tokens = signal.shape[0] * ny * lax.axis_size("c") * rows * nx * nz
     scale = 1.0 / math.sqrt(tokens)
-    units = -(-27 // ny)
+    splits = [(0, 512), (512, 256)]
+    sizes = [9 * width // 128 for _, width in splits]
+    units = [-(-size // ny) for size in sizes]
     core = lax.axis_index("c").astype(jnp.int32).reshape(1)
     place = lax.axis_index("x") * nz + lax.axis_index("z")
     inside = jnp.stack([place > 0, place < nx * nz - 1]).astype(jnp.int32)
 
-    order_x, order_y = order_of("x"), order_of("y")
-    sig, cot, core, inside, order_x, order_y = lax.optimization_barrier(
-        (sig, cot, core, inside, order_x, order_y)
+    at_x, at_y = (lax.axis_index(a).astype(jnp.int32) for a in ("x", "y"))
+    order_a = order_of(jnp.where(core[0] == 0, at_x, at_y), nx)
+    order_b = order_of(jnp.where(core[0] == 0, at_y, at_x), ny)
+    sig, cot, core, inside, order_a, order_b = lax.optimization_barrier(
+        (sig, cot, core, inside, order_a, order_b)
     )
 
     low, high, low_far, high_far = edges(sig, cot)
@@ -399,16 +416,16 @@
     far_act, far_cot = swap(act_ext), swap(cot_ext)
     mid, act_b, grad_m, give = front(core, act_ext, cot_ext, sig, cot, w1, w2)
     f_all = swap(give)
-    parts = (nx, ny, nz, units)
-    near = weights(parts, 0, core, act_b, act_ext, f_all, far_act, far_cot, grad_m, cot_ext)
-    far = weights(parts, 1, core, act_b, act_ext, f_all, far_act, far_cot, grad_m, cot_ext)
-    far, inside = lax.optimization_barrier((far, inside))
-    near = exchange(near, "x", order_x)
-    far = exchange(far, "y", order_y)
+    pieces = [
+        weights((nx, ny, nz, u), *split, core, act_b, act_ext, f_all, far_act, far_cot, grad_m, cot_ext)
+        for split, u in zip(splits, units)
+    ]
+    pieces[-1], inside = lax.optimization_barrier((pieces[-1], inside))
+    pieces = [exchange(piece, order_a, "xy") for piece in pieces]
     lo2, hi2 = wings(inside, act_ext, cot_ext, lo, hi, lo_far, hi_far, w1, w2)
     output, grad_s = back(act_b, lo2, hi2, grad_m, mid, sig, w1, w2)
-    near, far, output, grad_s = lax.optimization_barrier((near, far, output, grad_s))
-    part = jnp.stack([exchange(near, "y", order_y), exchange(far, "x", order_x)], axis=1)
+    pieces, output, grad_s = lax.optimization_barrier((pieces, output, grad_s))
+    part = exchange(jnp.concatenate(pieces, axis=2), order_b, "yx")
 
     got = lax.all_to_all(part, "z", 0, 0, tiled=True)
     part = jnp.sum(got.astype(F32), axis=0).astype(BF16)
@@ -418,9 +435,13 @@
     both = both.reshape((ny, 2) + part.shape).astype(F32) * scale
 
     def assemble(layer):
-        flat = both[:, layer].transpose(1, 0, 2, 3, 4).reshape(2, ny * units, 8, 128)[:, :27]
-        flat = flat.reshape(2, 3, ch // 256, 3, 8, 128).transpose(1, 3, 4, 0, 2, 5)
-        return flat.reshape(3, 24, ch)
+        found, at = [], 0
+        for (_, width), size, u in zip(splits, sizes, units):
+            flat = both[:, layer, at : at + u].reshape(ny * u, 8, 128)[:size]
+            flat = flat.reshape(3, width // 128, 3, 8, 128).transpose(0, 2, 3, 1, 4)
+            found.append(flat.reshape(3, 24, width))
+            at += u
+        return jnp.concatenate(found, axis=2)
 
     return output[None], grad_s[None], assemble(1), assemble(0)
 

time: 111 us -> 100 us (0.901)
  waiting for transfers between devices: 17.6 us -> 12.9 us
  starting transfers between devices: 33.2 us -> 30.1 us
  local copies, waits for them, and re-layouts: 1.96 us -> 0.62 us
  Pallas kernels: 26.2 us -> 24.9 us
    ppermute x12 -> x9, waiting for transfers between devices: 13.3 us -> 8.69 us  [exchange(): chunk = lax.ppermute(chunk, axes, pairs(k))]
    ppermute x12 -> x9, starting transfers between devices: 18.7 us -> 15.6 us  [exchange(): chunk = lax.ppermute(chunk, axes, pairs(k))]
    transpose x5 -> x4, local copies, waits for them, and re-layouts: 1.47 us -> 0.04 us  [assemble(): flat = flat.reshape(3, width // 128, 3, 8, 128).transpose(0, 2, 3, 1, 4)]
    pallas_call x2, Pallas kernels: 5.87 us -> 4.5 us  [weights(): pl.pallas_call(lambda *refs: weight_kernel(parts, *refs), grid=(1,), in_s...]
  transfers between devices with their start and end apart: 19 -> 16, of which waited for: 7 -> 7; matrix products, arithmetic and copies ran while one was open for 1% -> 1% of each run, Pallas kernels for 20% -> 22%
where the time goes in v3:
time: 100 us
  starting transfers between devices  30.1 us (30%)
  blocking collectives  28 us (28%)
  Pallas kernels  24.9 us (25%)
  waiting for transfers between devices  12.9 us (13%)
  other arithmetic  2.42 us (2%)
  between operations  1.07 us (1%)
    ppermute x9, starting transfers between devices, exchange(): chunk = lax.ppermute(chunk, axes, pairs(k))  15.6 us
    all_to_all x1, blocking collectives, per_device(): lax.all_to_all(jnp.broadcast_to(part[None], (2 * ny,) + part.shape), ('y'...  14.9 us
    all_to_all x1, blocking collectives, per_device(): got = lax.all_to_all(part, 'z', 0, 0, tiled=True)  13.2 us
    ppermute x2, starting transfers between devices, neighbours(): lax.ppermute(high, axes, forward)  8.69 us
    ppermute x9, waiting for transfers between devices, exchange(): chunk = lax.ppermute(chunk, axes, pairs(k))  8.69 us
    pallas_call x1, Pallas kernels, front(): pl.pallas_call(front_kernel, grid=(ch // tile,), in_specs=[pl.BlockSpec(m...  7.71 us
    pallas_call x1, Pallas kernels, back(): pl.pallas_call(back_kernel, grid=(ch // tile,), in_specs=[once(act_b), on...  7.24 us
    pallas_call x2, Pallas kernels, weights(): pl.pallas_call(lambda *refs: weight_kernel(parts, *refs), grid=(1,), in_s...  4.5 us
  transfers between devices with their start and end apart: 16, of which 7 were waited for; matrix products, arithmetic and copies ran while one was open for 1% of the time, Pallas kernels for 22%

profile of v3, /device:TPU:1, one launch (start us, length us, event | category | flops | bytes accessed | tf_op | source)
XLA Modules:
  0.0 100.0 jit_solution(8634742985989951961)
XLA Ops:
  0.6 0.0 copy-start.2
  0.7 0.1 add_convert_fusion.inside
  0.8 1.5 %edges.1 = (bf16[192,768]{1,0:T(8,128)(2,1)S(1)}, bf16[192,768]{1,0:T(8,128)(2,1)S(1)}, bf16[192,768]{1,0:T(8,128)(2,1)S(1)}, bf16[192,768]{1,0:T(8,128)(2,1)S(1)}) custom-call(bf16[512,768]{1,0:T(8,128)(2,1)} %bitcast.61, bf16[512,768]{1,0:T(8,128)(2,1)} %bitcast.65), custom_call_target="tpu_custom_call" | custom-call | tf_op jit(solution)/shard_map/edges/pallas_call | solution.py:77
  2.2 0.0 copy-start.3
  2.3 4.5 %collective-permute-start = (bf16[192,768]{1,0:T(8,128)(2,1)S(1)}, bf16[192,768]{1,0:T(8,128)(2,1)S(1)}, u32[]{:S(2)}, u32[]{:S(2)}) collective-permute-start(bf16[192,768]{1,0:T(8,128)(2,1)S(1)} %get-tuple-element.37), channel_id=1, source_target_pairs={{0,8},{8,16},{16,24},{24,32},{32,40},{40,48},{48,56},{56,64},{64,7... | collective-permute-start | bytes 884744 | tf_op jit(solution)/shard_map/ppermute | solution.py:386
  6.8 1.3 %collective-permute-start.1 = (bf16[192,768]{1,0:T(8,128)(2,1)S(1)}, bf16[192,768]{1,0:T(8,128)(2,1)S(1)}, u32[]{:S(2)}, u32[]{:S(2)}) collective-permute-start(bf16[192,768]{1,0:T(8,128)(2,1)S(1)} %get-tuple-element.38), channel_id=1, source_target_pairs={{8,0},{16,8},{24,16},{32,24},{40,32},{48,40},{56,48},{64,56},{72,6... | collective-permute-start | bytes 884744 | tf_op jit(solution)/shard_map/ppermute | solution.py:386
  8.1 4.2 %collective-permute-start.11 = (bf16[192,768]{1,0:T(8,128)(2,1)S(1)}, bf16[192,768]{1,0:T(8,128)(2,1)S(1)}, u32[]{:S(2)}, u32[]{:S(2)}) collective-permute-start(bf16[192,768]{1,0:T(8,128)(2,1)S(1)} %get-tuple-element.49), channel_id=1, source_target_pairs={{0,8},{8,16},{16,24},{24,32},{32,40},{40,48},{48,56},{56,64},{64,7... | collective-permute-start | bytes 884744 | tf_op jit(solution)/shard_map/ppermute | solution.py:386
  12.3 1.3 %collective-permute-start.12 = (bf16[192,768]{1,0:T(8,128)(2,1)S(1)}, bf16[192,768]{1,0:T(8,128)(2,1)S(1)}, u32[]{:S(2)}, u32[]{:S(2)}) collective-permute-start(bf16[192,768]{1,0:T(8,128)(2,1)S(1)} %get-tuple-element.50), channel_id=1, source_target_pairs={{8,0},{16,8},{24,16},{32,24},{40,32},{48,40},{56,48},{64,56},{72,6... | collective-permute-start | bytes 884744 | tf_op jit(solution)/shard_map/ppermute | solution.py:386
  13.6 0.0 copy-done.2
  13.6 0.5 fusion.1
  14.1 0.0 collective-permute-done.lo
  14.2 2.4 %collective-permute-done.1.hi = bf16[192,768]{1,0:T(8,128)(2,1)S(1)} collective-permute-done((bf16[192,768]{1,0:T(8,128)(2,1)S(1)}, bf16[192,768]{1,0:T(8,128)(2,1)S(1)}, u32[]{:S(2)}, u32[]{:S(2)}) %collective-permute-start.1) | collective-permute-done | bytes 294944 | tf_op jit(solution)/shard_map/ppermute | solution.py:386
  16.6 0.0 copy-done.3
  16.6 0.1 pad_maximum_fusion.cot_ext.refs_5_
  16.7 2.5 %collective-permute-start.4 = (bf16[768,768]{1,0:T(8,128)(2,1)S(1)}, bf16[768,768]{1,0:T(8,128)(2,1)S(1)}, u32[]{:S(2)}, u32[]{:S(2)}) collective-permute-start(bf16[768,768]{1,0:T(8,128)(2,1)S(1)} %pad_maximum_fusion.cot_ext.refs_5_), channel_id=1, source_target_pairs={{0,1},{1,0},{2,3},{3,2},{4,5},{5,4},{6,7},{7,6},{8,9},{9,8},{10,11... | collective-permute-start | bytes 3538952 | tf_op jit(solution)/shard_map/ppermute | solution.py:415
  19.2 0.1 fusion.15
  19.3 0.1 fusion.20
  19.4 0.1 pad_maximum_fusion.1.act.refs_2_
  19.5 0.1 collective-permute-start.3
  19.6 7.7 %front.1 = (bf16[512,768]{1,0:T(8,128)(2,1)S(1)}, bf16[512,768]{1,0:T(8,128)(2,1)S(1)}, bf16[512,768]{1,0:T(8,128)(2,1)S(1)}, bf16[512,768]{1,0:T(8,128)(2,1)S(1)}) custom-call(s32[1]{0:T(128)} %bitcast.2.core.refs_0_, bf16[640,768]{1,0:T(8,128)(2,1)S(1)} %pad_maximum_fusion.1.act.refs_2_, bf16[768,768]{1,0:T(8,128)(2,1)S(1)} %pad_maximum_fusion.cot_ext.refs_5_, ...), custom_call_target="tpu_custom_call" | custom-call | flops 3623878656 | bytes 8257536 | tf_op jit(solution)/shard_map/front/pallas_call | solution.py:121
  27.3 0.6 collective-permute-start.2
  27.8 0.0 collective-permute-done.11.lo_far
  27.9 0.0 collective-permute-done.12.hi_far
  28.0 1.8 %collective-permute-done.2.refs_3_.refs_8_ = bf16[512,768]{1,0:T(8,128)(2,1)S(1)} collective-permute-done((bf16[512,768]{1,0:T(8,128)(2,1)S(1)}, bf16[512,768]{1,0:T(8,128)(2,1)S(1)}, u32[]{:S(2)}, u32[]{:S(2)}) %collective-permute-start.2) | collective-permute-done | bytes 786464 | tf_op jit(solution)/shard_map/ppermute | solution.py:415
  29.8 0.0 collective-permute-done.3.refs_4_
  29.8 0.0 collective-permute-done.4.refs_6_
  29.8 1.5 %weights.3 = bf16[4,4,8,5,8,128]{5,4,3,2,1,0:T(8,128)(2,1)S(1)} custom-call(s32[1]{0:T(128)} %bitcast.2.core.refs_0_, bf16[512,768]{1,0:T(8,128)(2,1)S(1)} %get-tuple-element.39.refs_1_.act_b, bf16[640,768]{1,0:T(8,128)(2,1)S(1)} %pad_maximum_fusion.1.act.refs_2_, bf16[512,768]{1,0:T(8,128)(2,1)S(1)} %collective-permute-done.2.refs_3_.refs_8_, ...), custom_call_target="tpu_custom_call" | custom-call | flops 1207959552 | bytes 2359296 | tf_op jit(solution)/shard_map/weights/pallas_call | solution.py:326
  31.3 0.1 dynamic-slice_bitcast_fusion.5
  31.4 3.0 %collective-permute-start.10 = (bf16[4,8,5,8,128]{4,3,2,1,0:T(8,128)(2,1)S(1)}, bf16[4,8,5,8,128]{4,3,2,1,0:T(8,128)(2,1)S(1)}, u32[]{:S(2)}, u32[]{:S(2)}) collective-permute-start(bf16[4,8,5,8,128]{4,3,2,1,0:T(8,128)(2,1)S(1)} %get-tuple-element.68), channel_id=1, source_target_pairs={{0,128},{1,5},{2,130},{3,7},{4,132},{5,1},{6,134},{7,3},{8,136},{9... | collective-permute-start | bytes 983048 | tf_op jit(solution)/shard_map/ppermute | solution.py:371
  34.4 0.4 collective-permute-start.8
  34.8 2.3 %collective-permute-start.9 = (bf16[4,8,5,8,128]{4,3,2,1,0:T(8,128)(2,1)S(1)}, bf16[4,8,5,8,128]{4,3,2,1,0:T(8,128)(2,1)S(1)}, u32[]{:S(2)}, u32[]{:S(2)}) collective-permute-start(bf16[4,8,5,8,128]{4,3,2,1,0:T(8,128)(2,1)S(1)} %get-tuple-element.69), channel_id=1, source_target_pairs={{0,192},{1,7},{2,194},{3,1},{4,196},{5,3},{6,198},{7,5},{8,200},{9... | collective-permute-start | bytes 983048 | tf_op jit(solution)/shard_map/ppermute | solution.py:371
  37.1 0.0 copy-start.1
  37.1 3.0 %weights.2 = bf16[4,4,8,9,8,128]{5,4,3,2,1,0:T(8,128)(2,1)S(1)} custom-call(s32[1]{0:T(128)} %bitcast.2.core.refs_0_, bf16[512,768]{1,0:T(8,128)(2,1)S(1)} %get-tuple-element.39.refs_1_.act_b, bf16[640,768]{1,0:T(8,128)(2,1)S(1)} %pad_maximum_fusion.1.act.refs_2_, bf16[512,768]{1,0:T(8,128)(2,1)S(1)} %collective-permute-done.2.refs_3_.refs_8_, ...), custom_call_target="tpu_custom_call" | custom-call | flops 2415919104 | bytes 4718592 | tf_op jit(solution)/shard_map/weights/pallas_call | solution.py:326
  40.1 0.0 copy-start
  40.1 0.1 dynamic-slice_bitcast_fusion.2
  40.2 0.1 collective-permute-start.5
  40.3 2.7 %collective-permute-start.6 = (bf16[4,8,9,8,128]{4,3,2,1,0:T(8,128)(2,1)S(1)}, bf16[4,8,9,8,128]{4,3,2,1,0:T(8,128)(2,1)S(1)}, u32[]{:S(2)}, u32[]{:S(2)}) collective-permute-start(bf16[4,8,9,8,128]{4,3,2,1,0:T(8,128)(2,1)S(1)} %get-tuple-element.66), channel_id=1, source_target_pairs={{0,192},{1,7},{2,194},{3,1},{4,196},{5,3},{6,198},{7,5},{8,200},{9... | collective-permute-start | bytes 1769480 | tf_op jit(solution)/shard_map/ppermute | solution.py:371
  43.0 0.0 copy-done.1
  43.0 0.0 copy-done
  43.0 4.0 %wings.1 = (bf16[192,768]{1,0:T(8,128)(2,1)S(1)}, bf16[192,768]{1,0:T(8,128)(2,1)S(1)}) custom-call(s32[2]{0:T(128)S(1)} %add_convert_fusion.inside, bf16[640,768]{1,0:T(8,128)(2,1)S(1)} %pad_maximum_fusion.1.act.refs_2_, bf16[768,768]{1,0:T(8,128)(2,1)S(1)} %pad_maximum_fusion.cot_ext.refs_5_, bf16[192,768]{1,0:T(8,128)(2,1)S(1)} %collective-permute-done.lo, ...), custom_call_target="tpu_custom_call" | custom-call | flops 1358954496 | bytes 7077888 | tf_op jit(solution)/shard_map/wings/pallas_call | solution.py:190
  47.0 0.0 collective-permute-done.10
  47.0 0.1 collective-permute-start.7
  47.1 7.2 %rear.1 = (bf16[512,768]{1,0:T(8,128)(2,1)}, bf16[512,768]{1,0:T(8,128)(2,1)}) custom-call(bf16[512,768]{1,0:T(8,128)(2,1)S(1)} %get-tuple-element.39.refs_1_.act_b, bf16[192,768]{1,0:T(8,128)(2,1)S(1)} %get-tuple-element.51.lo, bf16[192,768]{1,0:T(8,128)(2,1)S(1)} %get-tuple-element.52.hi, bf16[512,768]{1,0:T(8,128)(2,1)S(1)} %get-tuple-element.41.refs_7_.grad_m.gm, ...), custom_call_target="tpu_custom_call" | custom-call | flops 3623878656 | bytes 8257536 | tf_op jit(solution)/shard_map/rear/pallas_call | solution.py:252
  54.3 0.0 collective-permute-done.8
  54.3 0.0 collective-permute-done.9
  54.3 0.2 fusion.10
  54.5 0.0 collective-permute-done.5
  54.5 1.6 %collective-permute-done.6 = bf16[4,8,9,8,128]{4,3,2,1,0:T(8,128)(2,1)S(1)} collective-permute-done((bf16[4,8,9,8,128]{4,3,2,1,0:T(8,128)(2,1)S(1)}, bf16[4,8,9,8,128]{4,3,2,1,0:T(8,128)(2,1)S(1)}, u32[]{:S(2)}, u32[]{:S(2)}) %collective-permute-start.6) | collective-permute-done | bytes 589856 | tf_op jit(solution)/shard_map/ppermute | solution.py:371
  56.1 1.5 %collective-permute-done.7 = bf16[4,8,9,8,128]{4,3,2,1,0:T(8,128)(2,1)S(1)} collective-permute-done((bf16[4,8,9,8,128]{4,3,2,1,0:T(8,128)(2,1)S(1)}, bf16[4,8,9,8,128]{4,3,2,1,0:T(8,128)(2,1)S(1)}, u32[]{:S(2)}, u32[]{:S(2)}) %collective-permute-start.7) | collective-permute-done | bytes 589856 | tf_op jit(solution)/shard_map/ppermute | solution.py:371
  57.6 0.3 fusion.7
  58.0 0.1 constant_dynamic-update-slice_fusion
  58.0 0.1 dynamic-slice_bitcast_fusion.8
  58.1 4.1 %collective-permute-start.13 = (bf16[8,14,8,128]{3,2,1,0:T(8,128)(2,1)S(1)}, bf16[8,14,8,128]{3,2,1,0:T(8,128)(2,1)S(1)}, u32[]{:S(2)}, u32[]{:S(2)}) collective-permute-start(bf16[8,14,8,128]{3,2,1,0:T(8,128)(2,1)S(1)} %get-tuple-element.70), channel_id=1, source_target_pairs={{0,2},{1,65},{2,4},{3,67},{4,6},{5,69},{6,0},{7,71},{8,10},{9,73},... | collective-permute-start | bytes 688136 | tf_op jit(solution)/shard_map/ppermute | solution.py:371
  62.2 1.6 %collective-permute-start.14 = (bf16[8,14,8,128]{3,2,1,0:T(8,128)(2,1)S(1)}, bf16[8,14,8,128]{3,2,1,0:T(8,128)(2,1)S(1)}, u32[]{:S(2)}, u32[]{:S(2)}) collective-permute-start(bf16[8,14,8,128]{3,2,1,0:T(8,128)(2,1)S(1)} %get-tuple-element.72), channel_id=1, source_target_pairs={{0,6},{1,193},{2,0},{3,195},{4,2},{5,197},{6,4},{7,199},{8,14},{9,... | collective-permute-start | bytes 688136 | tf_op jit(solution)/shard_map/ppermute | solution.py:371
  63.8 1.4 %collective-permute-start.15 = (bf16[8,14,8,128]{3,2,1,0:T(8,128)(2,1)S(1)}, bf16[8,14,8,128]{3,2,1,0:T(8,128)(2,1)S(1)}, u32[]{:S(2)}, u32[]{:S(2)}) collective-permute-start(bf16[8,14,8,128]{3,2,1,0:T(8,128)(2,1)S(1)} %get-tuple-element.71), channel_id=1, source_target_pairs={{0,4},{1,129},{2,6},{3,131},{4,0},{5,133},{6,2},{7,135},{8,12},{9,... | collective-permute-start | bytes 688136 | tf_op jit(solution)/shard_map/ppermute | solution.py:371
  65.2 2.0 %collective-permute-done.13 = bf16[8,14,8,128]{3,2,1,0:T(8,128)(2,1)S(1)} collective-permute-done((bf16[8,14,8,128]{3,2,1,0:T(8,128)(2,1)S(1)}, bf16[8,14,8,128]{3,2,1,0:T(8,128)(2,1)S(1)}, u32[]{:S(2)}, u32[]{:S(2)}) %collective-permute-start.13) | collective-permute-done | bytes 229408 | tf_op jit(solution)/shard_map/ppermute | solution.py:371
  67.2 2.1 %collective-permute-done.14 = bf16[8,14,8,128]{3,2,1,0:T(8,128)(2,1)S(1)} collective-permute-done((bf16[8,14,8,128]{3,2,1,0:T(8,128)(2,1)S(1)}, bf16[8,14,8,128]{3,2,1,0:T(8,128)(2,1)S(1)}, u32[]{:S(2)}, u32[]{:S(2)}) %collective-permute-start.14) | collective-permute-done | bytes 229408 | tf_op jit(solution)/shard_map/ppermute | solution.py:371
  69.3 1.5 %collective-permute-done.15 = bf16[8,14,8,128]{3,2,1,0:T(8,128)(2,1)S(1)} collective-permute-done((bf16[8,14,8,128]{3,2,1,0:T(8,128)(2,1)S(1)}, bf16[8,14,8,128]{3,2,1,0:T(8,128)(2,1)S(1)}, u32[]{:S(2)}, u32[]{:S(2)}) %collective-permute-start.15) | collective-permute-done | bytes 229408 | tf_op jit(solution)/shard_map/ppermute | solution.py:371
  70.8 0.1 fusion.13
  70.9 13.2 %all_to_all.10 = bf16[8,14,8,128]{3,2,1,0:T(8,128)(2,1)S(1)} all-to-all(bf16[8,14,8,128]{3,2,1,0:T(8,128)(2,1)S(1)} %fusion.13), channel_id=1, replica_groups=mesh['x'=4,'z'=8,'y'=4,'c'=2] {'z'}, dimensions={0} | all-to-all | bytes 458752 | tf_op jit(solution)/shard_map/all_to_all | solution.py:430
  84.2 14.9 %all_to_all.11 = bf16[8,14,8,128]{3,2,1,0:T(8,128)(2,1)S(1)} all-to-all(bf16[8,14,8,128]{3,2,1,0:T(8,128)(2,1)S(1)} %broadcast_in_dim.14), channel_id=1, replica_groups=mesh['x'=4,'z'=8,'y'=4,'c'=2] {'y','c'}, dimensions={0} | all-to-all | bytes 458752 | tf_op jit(solution)/shard_map/all_to_all | solution.py:432
  99.2 0.8 pad_maximum_fusion.3
  (20 shorter events, 0.4 us)
Async XLA Ops:
  0.6 12.9 %copy-start.2 = (bf16[1,512,768]{2,1,0:T(8,128)(2,1)S(1)}, bf16[1,512,768]{2,1,0:T(8,128)(2,1)}, u32[]{:S(2)}) copy-start(bf16[1,512,768]{2,1,0:T(8,128)(2,1)} %param.4) | copy-start | bytes 2359300
  2.2 14.4 %copy-start.3 = (bf16[1,512,768]{2,1,0:T(8,128)(2,1)S(1)}, bf16[1,512,768]{2,1,0:T(8,128)(2,1)}, u32[]{:S(2)}) copy-start(bf16[1,512,768]{2,1,0:T(8,128)(2,1)} %param.7) | copy-start | bytes 2359300
  2.3 11.9 %collective-permute-start = (bf16[192,768]{1,0:T(8,128)(2,1)S(1)}, bf16[192,768]{1,0:T(8,128)(2,1)S(1)}, u32[]{:S(2)}, u32[]{:S(2)}) collective-permute-start(bf16[192,768]{1,0:T(8,128)(2,1)S(1)} %get-tuple-element.37), channel_id=1, source_target_pairs={{0,8},{8,16},{16,24},{24,32},{32,40},{40,48},{48,56},{56,64},{64,7... | collective-permute-start | bytes 884744 | tf_op jit(solution)/shard_map/ppermute | solution.py:386
  6.8 9.8 %collective-permute-start.1 = (bf16[192,768]{1,0:T(8,128)(2,1)S(1)}, bf16[192,768]{1,0:T(8,128)(2,1)S(1)}, u32[]{:S(2)}, u32[]{:S(2)}) collective-permute-start(bf16[192,768]{1,0:T(8,128)(2,1)S(1)} %get-tuple-element.38), channel_id=1, source_target_pairs={{8,0},{16,8},{24,16},{32,24},{40,32},{48,40},{56,48},{64,56},{72,6... | collective-permute-start | bytes 884744 | tf_op jit(solution)/shard_map/ppermute | solution.py:386
  8.1 19.8 %collective-permute-start.11 = (bf16[192,768]{1,0:T(8,128)(2,1)S(1)}, bf16[192,768]{1,0:T(8,128)(2,1)S(1)}, u32[]{:S(2)}, u32[]{:S(2)}) collective-permute-start(bf16[192,768]{1,0:T(8,128)(2,1)S(1)} %get-tuple-element.49), channel_id=1, source_target_pairs={{0,8},{8,16},{16,24},{24,32},{32,40},{40,48},{48,56},{56,64},{64,7... | collective-permute-start | bytes 884744 | tf_op jit(solution)/shard_map/ppermute | solution.py:386
  12.3 15.6 %collective-permute-start.12 = (bf16[192,768]{1,0:T(8,128)(2,1)S(1)}, bf16[192,768]{1,0:T(8,128)(2,1)S(1)}, u32[]{:S(2)}, u32[]{:S(2)}) collective-permute-start(bf16[192,768]{1,0:T(8,128)(2,1)S(1)} %get-tuple-element.50), channel_id=1, source_target_pairs={{8,0},{16,8},{24,16},{32,24},{40,32},{48,40},{56,48},{64,56},{72,6... | collective-permute-start | bytes 884744 | tf_op jit(solution)/shard_map/ppermute | solution.py:386
  16.7 13.1 %collective-permute-start.4 = (bf16[768,768]{1,0:T(8,128)(2,1)S(1)}, bf16[768,768]{1,0:T(8,128)(2,1)S(1)}, u32[]{:S(2)}, u32[]{:S(2)}) collective-permute-start(bf16[768,768]{1,0:T(8,128)(2,1)S(1)} %pad_maximum_fusion.cot_ext.refs_5_), channel_id=1, source_target_pairs={{0,1},{1,0},{2,3},{3,2},{4,5},{5,4},{6,7},{7,6},{8,9},{9,8},{10,11... | collective-permute-start | bytes 3538952 | tf_op jit(solution)/shard_map/ppermute | solution.py:415
  19.5 10.3 %collective-permute-start.3 = (bf16[640,768]{1,0:T(8,128)(2,1)S(1)}, bf16[640,768]{1,0:T(8,128)(2,1)S(1)}, u32[]{:S(2)}, u32[]{:S(2)}) collective-permute-start(bf16[640,768]{1,0:T(8,128)(2,1)S(1)} %pad_maximum_fusion.1.act.refs_2_), channel_id=1, source_target_pairs={{0,1},{1,0},{2,3},{3,2},{4,5},{5,4},{6,7},{7,6},{8,9},{9,8},{10,11... | collective-permute-start | bytes 2949128 | tf_op jit(solution)/shard_map/ppermute | solution.py:415
  27.3 2.5 %collective-permute-start.2 = (bf16[512,768]{1,0:T(8,128)(2,1)S(1)}, bf16[512,768]{1,0:T(8,128)(2,1)S(1)}, u32[]{:S(2)}, u32[]{:S(2)}) collective-permute-start(bf16[512,768]{1,0:T(8,128)(2,1)S(1)} %get-tuple-element.40), channel_id=1, source_target_pairs={{0,1},{1,0},{2,3},{3,2},{4,5},{5,4},{6,7},{7,6},{8,9},{9,8},{10,11... | collective-permute-start | bytes 2359304 | tf_op jit(solution)/shard_map/ppermute | solution.py:415
  31.4 15.6 %collective-permute-start.10 = (bf16[4,8,5,8,128]{4,3,2,1,0:T(8,128)(2,1)S(1)}, bf16[4,8,5,8,128]{4,3,2,1,0:T(8,128)(2,1)S(1)}, u32[]{:S(2)}, u32[]{:S(2)}) collective-permute-start(bf16[4,8,5,8,128]{4,3,2,1,0:T(8,128)(2,1)S(1)} %get-tuple-element.68), channel_id=1, source_target_pairs={{0,128},{1,5},{2,130},{3,7},{4,132},{5,1},{6,134},{7,3},{8,136},{9... | collective-permute-start | bytes 983048 | tf_op jit(solution)/shard_map/ppermute | solution.py:371
  34.4 19.9 %collective-permute-start.8 = (bf16[4,8,5,8,128]{4,3,2,1,0:T(8,128)(2,1)S(1)}, bf16[4,8,5,8,128]{4,3,2,1,0:T(8,128)(2,1)S(1)}, u32[]{:S(2)}, u32[]{:S(2)}) collective-permute-start(bf16[4,8,5,8,128]{4,3,2,1,0:T(8,128)(2,1)S(1)} %get-tuple-element.67), channel_id=1, source_target_pairs={{0,64},{1,3},{2,66},{3,5},{4,68},{5,7},{6,70},{7,1},{8,72},{9,11},... | collective-permute-start | bytes 983048 | tf_op jit(solution)/shard_map/ppermute | solution.py:371
  34.8 19.5 %collective-permute-start.9 = (bf16[4,8,5,8,128]{4,3,2,1,0:T(8,128)(2,1)S(1)}, bf16[4,8,5,8,128]{4,3,2,1,0:T(8,128)(2,1)S(1)}, u32[]{:S(2)}, u32[]{:S(2)}) collective-permute-start(bf16[4,8,5,8,128]{4,3,2,1,0:T(8,128)(2,1)S(1)} %get-tuple-element.69), channel_id=1, source_target_pairs={{0,192},{1,7},{2,194},{3,1},{4,196},{5,3},{6,198},{7,5},{8,200},{9... | collective-permute-start | bytes 983048 | tf_op jit(solution)/shard_map/ppermute | solution.py:371
  37.1 5.9 %copy-start.1 = (bf16[3,768,768]{2,1,0:T(8,128)(2,1)S(1)}, bf16[3,768,768]{2,1,0:T(8,128)(2,1)}, u32[]{:S(2)}) copy-start(bf16[3,768,768]{2,1,0:T(8,128)(2,1)} %w2.5) | copy-start | bytes 10616836
  40.1 2.9 %copy-start = (bf16[3,768,768]{2,1,0:T(8,128)(2,1)S(1)}, bf16[3,768,768]{2,1,0:T(8,128)(2,1)}, u32[]{:S(2)}) copy-start(bf16[3,768,768]{2,1,0:T(8,128)(2,1)} %w1.5) | copy-start | bytes 10616836
  40.2 14.3 %collective-permute-start.5 = (bf16[4,8,9,8,128]{4,3,2,1,0:T(8,128)(2,1)S(1)}, bf16[4,8,9,8,128]{4,3,2,1,0:T(8,128)(2,1)S(1)}, u32[]{:S(2)}, u32[]{:S(2)}) collective-permute-start(bf16[4,8,9,8,128]{4,3,2,1,0:T(8,128)(2,1)S(1)} %get-tuple-element.64), channel_id=1, source_target_pairs={{0,64},{1,3},{2,66},{3,5},{4,68},{5,7},{6,70},{7,1},{8,72},{9,11},... | collective-permute-start | bytes 1769480 | tf_op jit(solution)/shard_map/ppermute | solution.py:371
  40.3 15.8 %collective-permute-start.6 = (bf16[4,8,9,8,128]{4,3,2,1,0:T(8,128)(2,1)S(1)}, bf16[4,8,9,8,128]{4,3,2,1,0:T(8,128)(2,1)S(1)}, u32[]{:S(2)}, u32[]{:S(2)}) collective-permute-start(bf16[4,8,9,8,128]{4,3,2,1,0:T(8,128)(2,1)S(1)} %get-tuple-element.66), channel_id=1, source_target_pairs={{0,192},{1,7},{2,194},{3,1},{4,196},{5,3},{6,198},{7,5},{8,200},{9... | collective-permute-start | bytes 1769480 | tf_op jit(solution)/shard_map/ppermute | solution.py:371
  47.0 10.6 %collective-permute-start.7 = (bf16[4,8,9,8,128]{4,3,2,1,0:T(8,128)(2,1)S(1)}, bf16[4,8,9,8,128]{4,3,2,1,0:T(8,128)(2,1)S(1)}, u32[]{:S(2)}, u32[]{:S(2)}) collective-permute-start(bf16[4,8,9,8,128]{4,3,2,1,0:T(8,128)(2,1)S(1)} %get-tuple-element.65), channel_id=1, source_target_pairs={{0,128},{1,5},{2,130},{3,7},{4,132},{5,1},{6,134},{7,3},{8,136},{9... | collective-permute-start | bytes 1769480 | tf_op jit(solution)/shard_map/ppermute | solution.py:371
  58.1 9.1 %collective-permute-start.13 = (bf16[8,14,8,128]{3,2,1,0:T(8,128)(2,1)S(1)}, bf16[8,14,8,128]{3,2,1,0:T(8,128)(2,1)S(1)}, u32[]{:S(2)}, u32[]{:S(2)}) collective-permute-start(bf16[8,14,8,128]{3,2,1,0:T(8,128)(2,1)S(1)} %get-tuple-element.70), channel_id=1, source_target_pairs={{0,2},{1,65},{2,4},{3,67},{4,6},{5,69},{6,0},{7,71},{8,10},{9,73},... | collective-permute-start | bytes 688136 | tf_op jit(solution)/shard_map/ppermute | solution.py:371
  62.2 7.1 %collective-permute-start.14 = (bf16[8,14,8,128]{3,2,1,0:T(8,128)(2,1)S(1)}, bf16[8,14,8,128]{3,2,1,0:T(8,128)(2,1)S(1)}, u32[]{:S(2)}, u32[]{:S(2)}) collective-permute-start(bf16[8,14,8,128]{3,2,1,0:T(8,128)(2,1)S(1)} %get-tuple-element.72), channel_id=1, source_target_pairs={{0,6},{1,193},{2,0},{3,195},{4,2},{5,197},{6,4},{7,199},{8,14},{9,... | collective-permute-start | bytes 688136 | tf_op jit(solution)/shard_map/ppermute | solution.py:371
  63.8 7.0 %collective-permute-start.15 = (bf16[8,14,8,128]{3,2,1,0:T(8,128)(2,1)S(1)}, bf16[8,14,8,128]{3,2,1,0:T(8,128)(2,1)S(1)}, u32[]{:S(2)}, u32[]{:S(2)}) collective-permute-start(bf16[8,14,8,128]{3,2,1,0:T(8,128)(2,1)S(1)} %get-tuple-element.71), channel_id=1, source_target_pairs={{0,4},{1,129},{2,6},{3,131},{4,0},{5,133},{6,2},{7,135},{8,12},{9,... | collective-permute-start | bytes 688136 | tf_op jit(solution)/shard_map/ppermute | solution.py:371

commit v4 on v3

--- a/solution.py
+++ b/solution.py
@@ -89,25 +89,25 @@
     return pl.BlockSpec(a.shape, lambda n: (0, 0), pipeline_mode=pl.Buffered(1))
 
 
-def three_taps(dots, left, weight, starts, rows):
-    total = dots(left[starts[0] : starts[0] + rows], weight[0])
+CHUNK = 256
+
+
+def three_taps(dots, left, weight, starts, at):
+    total = dots(left[starts[0] + at : starts[0] + at + CHUNK], weight[0])
     for k in (1, 2):
-        total = total + dots(left[starts[k] : starts[k] + rows], weight[k])
+        total = total + dots(left[starts[k] + at : starts[k] + at + CHUNK], weight[k])
     return total
 
 
-def front_kernel(core, act, cot_ext, sig, cot, w1, w2, middle, act_b, grad_m, swap, fwd, bwd):
-    rows = sig.shape[0]
-    fwd[...] = three_taps(dot, act, w1, [k * FIRST for k in range(3)], rows)
-    bwd[...] = three_taps(dot_nt, cot_ext, w2, [(2 - k) * SECOND for k in range(3)], rows)
-
-    @pl.loop(0, rows // 64)
-    def _(i):
-        at = pl.ds(pl.multiple_of(i * 64, 64), 64)
-        mid = (sig[at].astype(F32) + fwd[at]).astype(BF16)
+def front_kernel(core, act, cot_ext, sig, cot, w1, w2, middle, act_b, grad_m, swap):
+    for i in range(0, sig.shape[0], CHUNK):
+        at = slice(i, i + CHUNK)
+        fwd = three_taps(dot, act, w1, [k * FIRST for k in range(3)], i)
+        bwd = three_taps(dot_nt, cot_ext, w2, [(2 - k) * SECOND for k in range(3)], i)
+        mid = (sig[at].astype(F32) + fwd).astype(BF16)
         middle[at] = mid
         value, slope = gelu_both(mid.astype(F32))
-        grad = cot[at].astype(F32) + slope * bwd[at]
+        grad = cot[at].astype(F32) + slope * bwd
         act_b[at] = value.astype(BF16)
         grad_m[at] = grad.astype(BF16)
         swap[at] = jnp.where(core[0] == 0, grad, value).astype(BF16)
@@ -132,7 +132,6 @@
         ],
         out_specs=[cols] * 4,
         out_shape=[out] * 4,
-        scratch_shapes=[pltpu.VMEM((rows, tile), F32), pltpu.VMEM((rows, tile), F32)],
         compiler_params=pltpu.CompilerParams(vmem_limit_bytes=16 << 20),
         cost_estimate=pl.CostEstimate(
             flops=12 * rows * ch * ch, transcendentals=rows * ch, bytes_accessed=14 * ch * ch
@@ -214,7 +213,7 @@
     )(inside, act_ext, cot_ext, lo, hi, lo_far, hi_far, sig_t, cot_t, w1, w2)
 
 
-def back_kernel(act_b, lo, hi, grad_m, mid, sig, gm, w1, w2, output, grad_s, a_ext, g_ext, fwd, bwd):
+def back_kernel(act_b, lo, hi, grad_m, mid, sig, gm, w1, w2, output, grad_s, a_ext, g_ext):
     rows = mid.shape[0]
 
     @pl.when(pl.program_id(0) == 0)
@@ -226,22 +225,13 @@
         g_ext[FIRST : FIRST + rows] = grad_m[...]
         g_ext[FIRST + rows :] = hi[SECOND:]
 
-    total = dot(a_ext[0:rows], w2[0])
-    for k in (1, 2):
-        total = total + dot(a_ext[k * SECOND : k * SECOND + rows], w2[k])
-    fwd[...] = total
-    total = dot_nt(g_ext[2 * FIRST : 2 * FIRST + rows], w1[0])
-    for k in (1, 2):
-        start = (2 - k) * FIRST
-        total = total + dot_nt(g_ext[start : start + rows], w1[k])
-    bwd[...] = total
-
-    @pl.loop(0, rows // 64)
-    def _(i):
-        at = pl.ds(pl.multiple_of(i * 64, 64), 64)
-        output[at] = (mid[at].astype(F32) + fwd[at]).astype(BF16)
+    for i in range(0, rows, CHUNK):
+        at = slice(i, i + CHUNK)
+        fwd = three_taps(dot, a_ext, w2, [k * SECOND for k in range(3)], i)
+        bwd = three_taps(dot_nt, g_ext, w1, [(2 - k) * FIRST for k in range(3)], i)
+        output[at] = (mid[at].astype(F32) + fwd).astype(BF16)
         _, slope = gelu_both(sig[at].astype(F32))
-        grad_s[at] = (gm[at].astype(F32) + slope * bwd[at]).astype(BF16)
+        grad_s[at] = (gm[at].astype(F32) + slope * bwd).astype(BF16)
 
 
 def back(act_b, lo, hi, grad_m, mid, sig, w1, w2):
@@ -268,8 +258,6 @@
         scratch_shapes=[
             pltpu.VMEM((rows + 2 * SECOND, ch), BF16),
             pltpu.VMEM((rows + 2 * FIRST, ch), BF16),
-            pltpu.VMEM((rows, tile), F32),
-            pltpu.VMEM((rows, tile), F32),
         ],
         compiler_params=pltpu.CompilerParams(vmem_limit_bytes=16 << 20),
         cost_estimate=pl.CostEstimate(
@@ -347,7 +335,7 @@
     )(core, act_b, act_ext, f_all, far_act, cot_ext, far_cot, grad_m, f_all)
 
 
-def exchange(data, order, core_axis):
+def exchange(data, order, core_axis, token=None):
     axes = ("x", "z", "y", "c")
     sizes = [lax.axis_size(a) for a in axes]
     n = data.shape[0]
@@ -363,15 +351,17 @@
         return found
 
     total = None
-    for k in (0, 1, n - 1, *range(2, n - 1)):
+    for k in (0, *range(2, n - 1), 1, n - 1):
         chunk = lax.dynamic_slice(
             data, (order[k],) + (0,) * len(rest), (1,) + rest, allow_negative_indices=False
         ).reshape(rest)
         if k:
             chunk = lax.ppermute(chunk, axes, pairs(k))
+        if k == 2 and token is not None:
+            chunk, token = lax.optimization_barrier((chunk, token))
         chunk = chunk.astype(F32)
         total = chunk if total is None else total + chunk
-    return total.astype(BF16)
+    return total.astype(BF16), token
 
 
 def order_of(me, n):
@@ -420,12 +410,13 @@
         weights((nx, ny, nz, u), *split, core, act_b, act_ext, f_all, far_act, far_cot, grad_m, cot_ext)
         for split, u in zip(splits, units)
     ]
-    pieces[-1], inside = lax.optimization_barrier((pieces[-1], inside))
-    pieces = [exchange(piece, order_a, "xy") for piece in pieces]
+    wide, _ = exchange(pieces[0], order_a, "xy")
+    narrow, inside = exchange(pieces[1], order_a, "xy", inside)
+    pieces = [wide, narrow]
     lo2, hi2 = wings(inside, act_ext, cot_ext, lo, hi, lo_far, hi_far, w1, w2)
     output, grad_s = back(act_b, lo2, hi2, grad_m, mid, sig, w1, w2)
     pieces, output, grad_s = lax.optimization_barrier((pieces, output, grad_s))
-    part = exchange(jnp.concatenate(pieces, axis=2), order_b, "yx")
+    part, _ = exchange(jnp.concatenate(pieces, axis=2), order_b, "yx")
 
     got = lax.all_to_all(part, "z", 0, 0, tiled=True)
     part = jnp.sum(got.astype(F32), axis=0).astype(BF16)

time: 100 us -> 98.1 us (0.981)
  Pallas kernels: 24.9 us -> 23 us
  waiting for transfers between devices: 12.9 us -> 11.6 us
    ppermute x9, waiting for transfers between devices: 8.69 us -> 7.42 us  [exchange(): chunk = lax.ppermute(chunk, axes, pairs(k))]
    pallas_call x1, Pallas kernels: 7.24 us -> 6.1 us  [back(): pl.pallas_call(back_kernel, grid=(ch // tile,), in_specs=[once(act_b), on...]
  transfers between devices with their start and end apart: 16 -> 16, of which waited for: 7 -> 6; matrix products, arithmetic and copies ran while one was open for 1% -> 1% of each run, Pallas kernels for 22% -> 20%
where the time goes in v4:
time: 98.1 us; the launch traced here: 97.9 us
  starting transfers between devices  30.9 us (31%)
  blocking collectives  28.2 us (29%)
  Pallas kernels  23 us (23%)
  waiting for transfers between devices  11.6 us (12%)
  other arithmetic  2.43 us (2%)
  between operations  1.06 us (1%)
    ppermute x9, starting transfers between devices, exchange(): chunk = lax.ppermute(chunk, axes, pairs(k))  16.4 us
    all_to_all x1, blocking collectives, per_device(): lax.all_to_all(jnp.broadcast_to(part[None], (2 * ny,) + part.shape), ('y'...  15.2 us
    all_to_all x1, blocking collectives, per_device(): got = lax.all_to_all(part, 'z', 0, 0, tiled=True)  13.1 us
    ppermute x2, starting transfers between devices, neighbours(): lax.ppermute(high, axes, forward)  8.69 us
    ppermute x9, waiting for transfers between devices, exchange(): chunk = lax.ppermute(chunk, axes, pairs(k))  7.42 us
    pallas_call x1, Pallas kernels, front(): pl.pallas_call(front_kernel, grid=(ch // tile,), in_specs=[pl.BlockSpec(m...  6.99 us
    pallas_call x1, Pallas kernels, back(): pl.pallas_call(back_kernel, grid=(ch // tile,), in_specs=[once(act_b), on...  6.1 us
    pallas_call x2, Pallas kernels, weights(): pl.pallas_call(lambda *refs: weight_kernel(parts, *refs), grid=(1,), in_s...  4.5 us
  transfers between devices with their start and end apart: 16, of which 6 were waited for; matrix products, arithmetic and copies ran while one was open for 1% of the time, Pallas kernels for 20%

profile of v4, /device:TPU:1, one launch (start us, length us, event | category | flops | bytes accessed | tf_op | source)
XLA Modules:
  0.0 97.9 jit_solution(14348941840973934123)
XLA Ops:
  0.6 0.0 copy-start.2
  0.7 0.1 add_convert_fusion.inside
  0.8 1.5 %edges.1 = (bf16[192,768]{1,0:T(8,128)(2,1)S(1)}, bf16[192,768]{1,0:T(8,128)(2,1)S(1)}, bf16[192,768]{1,0:T(8,128)(2,1)S(1)}, bf16[192,768]{1,0:T(8,128)(2,1)S(1)}) custom-call(bf16[512,768]{1,0:T(8,128)(2,1)} %bitcast.61, bf16[512,768]{1,0:T(8,128)(2,1)} %bitcast.65), custom_call_target="tpu_custom_call" | custom-call | tf_op jit(solution)/shard_map/edges/pallas_call | solution.py:77
  2.2 0.0 copy-start.3
  2.3 4.5 %collective-permute-start = (bf16[192,768]{1,0:T(8,128)(2,1)S(1)}, bf16[192,768]{1,0:T(8,128)(2,1)S(1)}, u32[]{:S(2)}, u32[]{:S(2)}) collective-permute-start(bf16[192,768]{1,0:T(8,128)(2,1)S(1)} %get-tuple-element.37), channel_id=1, source_target_pairs={{0,8},{8,16},{16,24},{24,32},{32,40},{40,48},{48,56},{56,64},{64,7... | collective-permute-start | bytes 884744 | tf_op jit(solution)/shard_map/ppermute | solution.py:376
  6.8 1.3 %collective-permute-start.1 = (bf16[192,768]{1,0:T(8,128)(2,1)S(1)}, bf16[192,768]{1,0:T(8,128)(2,1)S(1)}, u32[]{:S(2)}, u32[]{:S(2)}) collective-permute-start(bf16[192,768]{1,0:T(8,128)(2,1)S(1)} %get-tuple-element.38), channel_id=1, source_target_pairs={{8,0},{16,8},{24,16},{32,24},{40,32},{48,40},{56,48},{64,56},{72,6... | collective-permute-start | bytes 884744 | tf_op jit(solution)/shard_map/ppermute | solution.py:376
  8.1 4.2 %collective-permute-start.11 = (bf16[192,768]{1,0:T(8,128)(2,1)S(1)}, bf16[192,768]{1,0:T(8,128)(2,1)S(1)}, u32[]{:S(2)}, u32[]{:S(2)}) collective-permute-start(bf16[192,768]{1,0:T(8,128)(2,1)S(1)} %get-tuple-element.49), channel_id=1, source_target_pairs={{0,8},{8,16},{16,24},{24,32},{32,40},{40,48},{48,56},{56,64},{64,7... | collective-permute-start | bytes 884744 | tf_op jit(solution)/shard_map/ppermute | solution.py:376
  12.3 1.3 %collective-permute-start.12 = (bf16[192,768]{1,0:T(8,128)(2,1)S(1)}, bf16[192,768]{1,0:T(8,128)(2,1)S(1)}, u32[]{:S(2)}, u32[]{:S(2)}) collective-permute-start(bf16[192,768]{1,0:T(8,128)(2,1)S(1)} %get-tuple-element.50), channel_id=1, source_target_pairs={{8,0},{16,8},{24,16},{32,24},{40,32},{48,40},{56,48},{64,56},{72,6... | collective-permute-start | bytes 884744 | tf_op jit(solution)/shard_map/ppermute | solution.py:376
  13.6 0.0 copy-done.2
  13.6 0.5 fusion.1
  14.1 0.0 collective-permute-done.lo
  14.2 2.4 %collective-permute-done.1.hi = bf16[192,768]{1,0:T(8,128)(2,1)S(1)} collective-permute-done((bf16[192,768]{1,0:T(8,128)(2,1)S(1)}, bf16[192,768]{1,0:T(8,128)(2,1)S(1)}, u32[]{:S(2)}, u32[]{:S(2)}) %collective-permute-start.1) | collective-permute-done | bytes 294944 | tf_op jit(solution)/shard_map/ppermute | solution.py:376
  16.6 0.0 copy-done.3
  16.6 0.1 pad_maximum_fusion.cot_ext.refs_5_
  16.7 2.5 %collective-permute-start.4 = (bf16[768,768]{1,0:T(8,128)(2,1)S(1)}, bf16[768,768]{1,0:T(8,128)(2,1)S(1)}, u32[]{:S(2)}, u32[]{:S(2)}) collective-permute-start(bf16[768,768]{1,0:T(8,128)(2,1)S(1)} %pad_maximum_fusion.cot_ext.refs_5_), channel_id=1, source_target_pairs={{0,1},{1,0},{2,3},{3,2},{4,5},{5,4},{6,7},{7,6},{8,9},{9,8},{10,11... | collective-permute-start | bytes 3538952 | tf_op jit(solution)/shard_map/ppermute | solution.py:405
  19.2 0.1 fusion.15
  19.3 0.1 fusion.20
  19.4 0.1 pad_maximum_fusion.1.act.refs_2_
  19.5 0.1 collective-permute-start.3
  19.6 7.0 %front.1 = (bf16[512,768]{1,0:T(8,128)(2,1)S(1)}, bf16[512,768]{1,0:T(8,128)(2,1)S(1)}, bf16[512,768]{1,0:T(8,128)(2,1)S(1)}, bf16[512,768]{1,0:T(8,128)(2,1)S(1)}) custom-call(s32[1]{0:T(128)} %bitcast.2.core.refs_0_, bf16[640,768]{1,0:T(8,128)(2,1)S(1)} %pad_maximum_fusion.1.act.refs_2_, bf16[768,768]{1,0:T(8,128)(2,1)S(1)} %pad_maximum_fusion.cot_ext.refs_5_, ...), custom_call_target="tpu_custom_call" | custom-call | flops 3623878656 | bytes 8257536 | tf_op jit(solution)/shard_map/front/pallas_call | solution.py:121
  26.6 0.6 collective-permute-start.2
  27.1 0.0 collective-permute-done.11.lo_far
  27.1 0.0 collective-permute-done.12.hi_far
  27.3 1.8 %collective-permute-done.2.refs_3_.refs_8_ = bf16[512,768]{1,0:T(8,128)(2,1)S(1)} collective-permute-done((bf16[512,768]{1,0:T(8,128)(2,1)S(1)}, bf16[512,768]{1,0:T(8,128)(2,1)S(1)}, u32[]{:S(2)}, u32[]{:S(2)}) %collective-permute-start.2) | collective-permute-done | bytes 786464 | tf_op jit(solution)/shard_map/ppermute | solution.py:405
  29.0 0.0 collective-permute-done.3.refs_4_
  29.0 0.0 collective-permute-done.4.refs_6_
  29.1 1.5 %weights.3 = bf16[4,4,8,5,8,128]{5,4,3,2,1,0:T(8,128)(2,1)S(1)} custom-call(s32[1]{0:T(128)} %bitcast.2.core.refs_0_, bf16[512,768]{1,0:T(8,128)(2,1)S(1)} %get-tuple-element.39.refs_1_.act_b, bf16[640,768]{1,0:T(8,128)(2,1)S(1)} %pad_maximum_fusion.1.act.refs_2_, bf16[512,768]{1,0:T(8,128)(2,1)S(1)} %collective-permute-done.2.refs_3_.refs_8_, ...), custom_call_target="tpu_custom_call" | custom-call | flops 1207959552 | bytes 2359296 | tf_op jit(solution)/shard_map/weights/pallas_call | solution.py:314
  30.6 0.1 dynamic-slice_bitcast_fusion.5
  30.7 3.0 %collective-permute-start.8 = (bf16[4,8,5,8,128]{4,3,2,1,0:T(8,128)(2,1)S(1)}, bf16[4,8,5,8,128]{4,3,2,1,0:T(8,128)(2,1)S(1)}, u32[]{:S(2)}, u32[]{:S(2)}) collective-permute-start(bf16[4,8,5,8,128]{4,3,2,1,0:T(8,128)(2,1)S(1)} %get-tuple-element.67), channel_id=1, source_target_pairs={{0,128},{1,5},{2,130},{3,7},{4,132},{5,1},{6,134},{7,3},{8,136},{9... | collective-permute-start | bytes 983048 | tf_op jit(solution)/shard_map/ppermute | solution.py:359
  33.7 0.8 collective-permute-start.10
  34.5 0.7 collective-permute-start.9
  35.1 0.0 copy-start.1
  35.2 3.0 %weights.2 = bf16[4,4,8,9,8,128]{5,4,3,2,1,0:T(8,128)(2,1)S(1)} custom-call(s32[1]{0:T(128)} %bitcast.2.core.refs_0_, bf16[512,768]{1,0:T(8,128)(2,1)S(1)} %get-tuple-element.39.refs_1_.act_b, bf16[640,768]{1,0:T(8,128)(2,1)S(1)} %pad_maximum_fusion.1.act.refs_2_, bf16[512,768]{1,0:T(8,128)(2,1)S(1)} %collective-permute-done.2.refs_3_.refs_8_, ...), custom_call_target="tpu_custom_call" | custom-call | flops 2415919104 | bytes 4718592 | tf_op jit(solution)/shard_map/weights/pallas_call | solution.py:314
  38.1 0.0 copy-start
  38.1 0.1 dynamic-slice_bitcast_fusion.2
  38.3 0.8 collective-permute-start.5
  39.1 1.8 %collective-permute-start.6 = (bf16[4,8,9,8,128]{4,3,2,1,0:T(8,128)(2,1)S(1)}, bf16[4,8,9,8,128]{4,3,2,1,0:T(8,128)(2,1)S(1)}, u32[]{:S(2)}, u32[]{:S(2)}) collective-permute-start(bf16[4,8,9,8,128]{4,3,2,1,0:T(8,128)(2,1)S(1)} %get-tuple-element.66), channel_id=1, source_target_pairs={{0,64},{1,3},{2,66},{3,5},{4,68},{5,7},{6,70},{7,1},{8,72},{9,11},... | collective-permute-start | bytes 1769480 | tf_op jit(solution)/shard_map/ppermute | solution.py:359
  41.0 0.0 collective-permute-done.8
  41.0 0.8 collective-permute-start.7
  41.8 0.0 copy-done.1
  41.8 0.0 copy-done
  41.8 4.0 %wings.1 = (bf16[192,768]{1,0:T(8,128)(2,1)S(1)}, bf16[192,768]{1,0:T(8,128)(2,1)S(1)}) custom-call(s32[2]{0:T(128)S(1)} %add_convert_fusion.inside, bf16[640,768]{1,0:T(8,128)(2,1)S(1)} %pad_maximum_fusion.1.act.refs_2_, bf16[768,768]{1,0:T(8,128)(2,1)S(1)} %pad_maximum_fusion.cot_ext.refs_5_, bf16[192,768]{1,0:T(8,128)(2,1)S(1)} %collective-permute-done.lo, ...), custom_call_target="tpu_custom_call" | custom-call | flops 1358954496 | bytes 7077888 | tf_op jit(solution)/shard_map/wings/pallas_call | solution.py:189
  45.8 0.0 collective-permute-done.10
  45.8 0.0 collective-permute-done.9
  45.8 0.2 fusion.10
  46.0 6.1 %rear.1 = (bf16[512,768]{1,0:T(8,128)(2,1)}, bf16[512,768]{1,0:T(8,128)(2,1)}) custom-call(bf16[512,768]{1,0:T(8,128)(2,1)S(1)} %get-tuple-element.39.refs_1_.act_b, bf16[192,768]{1,0:T(8,128)(2,1)S(1)} %get-tuple-element.51.lo, bf16[192,768]{1,0:T(8,128)(2,1)S(1)} %get-tuple-element.52.hi, bf16[512,768]{1,0:T(8,128)(2,1)S(1)} %get-tuple-element.41.refs_7_.grad_m.gm, ...), custom_call_target="tpu_custom_call" | custom-call | flops 3623878656 | bytes 8257536 | tf_op jit(solution)/shard_map/rear/pallas_call | solution.py:242
  52.1 0.0 collective-permute-done.5
  52.1 3.1 %collective-permute-done.6 = bf16[4,8,9,8,128]{4,3,2,1,0:T(8,128)(2,1)S(1)} collective-permute-done((bf16[4,8,9,8,128]{4,3,2,1,0:T(8,128)(2,1)S(1)}, bf16[4,8,9,8,128]{4,3,2,1,0:T(8,128)(2,1)S(1)}, u32[]{:S(2)}, u32[]{:S(2)}) %collective-permute-start.6) | collective-permute-done | bytes 589856 | tf_op jit(solution)/shard_map/ppermute | solution.py:359
  55.2 0.0 collective-permute-done.7
  55.2 0.3 fusion.7
  55.6 0.1 constant_dynamic-update-slice_fusion
  55.7 0.1 dynamic-slice_bitcast_fusion.8
  55.7 5.8 %collective-permute-start.13 = (bf16[8,14,8,128]{3,2,1,0:T(8,128)(2,1)S(1)}, bf16[8,14,8,128]{3,2,1,0:T(8,128)(2,1)S(1)}, u32[]{:S(2)}, u32[]{:S(2)}) collective-permute-start(bf16[8,14,8,128]{3,2,1,0:T(8,128)(2,1)S(1)} %get-tuple-element.70), channel_id=1, source_target_pairs={{0,4},{1,129},{2,6},{3,131},{4,0},{5,133},{6,2},{7,135},{8,12},{9,... | collective-permute-start | bytes 688136 | tf_op jit(solution)/shard_map/ppermute | solution.py:359
  61.5 0.8 collective-permute-start.14
  62.3 1.9 %collective-permute-start.15 = (bf16[8,14,8,128]{3,2,1,0:T(8,128)(2,1)S(1)}, bf16[8,14,8,128]{3,2,1,0:T(8,128)(2,1)S(1)}, u32[]{:S(2)}, u32[]{:S(2)}) collective-permute-start(bf16[8,14,8,128]{3,2,1,0:T(8,128)(2,1)S(1)} %get-tuple-element.71), channel_id=1, source_target_pairs={{0,6},{1,193},{2,0},{3,195},{4,2},{5,197},{6,4},{7,199},{8,14},{9,... | collective-permute-start | bytes 688136 | tf_op jit(solution)/shard_map/ppermute | solution.py:359
  64.2 0.7 collective-permute-done.13
  64.9 3.0 %collective-permute-done.14 = bf16[8,14,8,128]{3,2,1,0:T(8,128)(2,1)S(1)} collective-permute-done((bf16[8,14,8,128]{3,2,1,0:T(8,128)(2,1)S(1)}, bf16[8,14,8,128]{3,2,1,0:T(8,128)(2,1)S(1)}, u32[]{:S(2)}, u32[]{:S(2)}) %collective-permute-start.14) | collective-permute-done | bytes 229408 | tf_op jit(solution)/shard_map/ppermute | solution.py:359
  67.9 0.6 collective-permute-done.15
  68.4 0.1 fusion.13
  68.6 13.1 %all_to_all.10 = bf16[8,14,8,128]{3,2,1,0:T(8,128)(2,1)S(1)} all-to-all(bf16[8,14,8,128]{3,2,1,0:T(8,128)(2,1)S(1)} %fusion.13), channel_id=1, replica_groups=mesh['x'=4,'z'=8,'y'=4,'c'=2] {'z'}, dimensions={0} | all-to-all | bytes 458752 | tf_op jit(solution)/shard_map/all_to_all | solution.py:421
  81.7 15.2 %all_to_all.11 = bf16[8,14,8,128]{3,2,1,0:T(8,128)(2,1)S(1)} all-to-all(bf16[8,14,8,128]{3,2,1,0:T(8,128)(2,1)S(1)} %broadcast_in_dim.14), channel_id=1, replica_groups=mesh['x'=4,'z'=8,'y'=4,'c'=2] {'y','c'}, dimensions={0} | all-to-all | bytes 458752 | tf_op jit(solution)/shard_map/all_to_all | solution.py:423
  97.1 0.8 pad_maximum_fusion.3
  (20 shorter events, 0.4 us)
Async XLA Ops:
  0.6 12.9 %copy-start.2 = (bf16[1,512,768]{2,1,0:T(8,128)(2,1)S(1)}, bf16[1,512,768]{2,1,0:T(8,128)(2,1)}, u32[]{:S(2)}) copy-start(bf16[1,512,768]{2,1,0:T(8,128)(2,1)} %param.4) | copy-start | bytes 2359300
  2.2 14.4 %copy-start.3 = (bf16[1,512,768]{2,1,0:T(8,128)(2,1)S(1)}, bf16[1,512,768]{2,1,0:T(8,128)(2,1)}, u32[]{:S(2)}) copy-start(bf16[1,512,768]{2,1,0:T(8,128)(2,1)} %param.7) | copy-start | bytes 2359300
  2.3 11.9 %collective-permute-start = (bf16[192,768]{1,0:T(8,128)(2,1)S(1)}, bf16[192,768]{1,0:T(8,128)(2,1)S(1)}, u32[]{:S(2)}, u32[]{:S(2)}) collective-permute-start(bf16[192,768]{1,0:T(8,128)(2,1)S(1)} %get-tuple-element.37), channel_id=1, source_target_pairs={{0,8},{8,16},{16,24},{24,32},{32,40},{40,48},{48,56},{56,64},{64,7... | collective-permute-start | bytes 884744 | tf_op jit(solution)/shard_map/ppermute | solution.py:376
  6.8 9.8 %collective-permute-start.1 = (bf16[192,768]{1,0:T(8,128)(2,1)S(1)}, bf16[192,768]{1,0:T(8,128)(2,1)S(1)}, u32[]{:S(2)}, u32[]{:S(2)}) collective-permute-start(bf16[192,768]{1,0:T(8,128)(2,1)S(1)} %get-tuple-element.38), channel_id=1, source_target_pairs={{8,0},{16,8},{24,16},{32,24},{40,32},{48,40},{56,48},{64,56},{72,6... | collective-permute-start | bytes 884744 | tf_op jit(solution)/shard_map/ppermute | solution.py:376
  8.1 19.1 %collective-permute-start.11 = (bf16[192,768]{1,0:T(8,128)(2,1)S(1)}, bf16[192,768]{1,0:T(8,128)(2,1)S(1)}, u32[]{:S(2)}, u32[]{:S(2)}) collective-permute-start(bf16[192,768]{1,0:T(8,128)(2,1)S(1)} %get-tuple-element.49), channel_id=1, source_target_pairs={{0,8},{8,16},{16,24},{24,32},{32,40},{40,48},{48,56},{56,64},{64,7... | collective-permute-start | bytes 884744 | tf_op jit(solution)/shard_map/ppermute | solution.py:376
  12.3 14.9 %collective-permute-start.12 = (bf16[192,768]{1,0:T(8,128)(2,1)S(1)}, bf16[192,768]{1,0:T(8,128)(2,1)S(1)}, u32[]{:S(2)}, u32[]{:S(2)}) collective-permute-start(bf16[192,768]{1,0:T(8,128)(2,1)S(1)} %get-tuple-element.50), channel_id=1, source_target_pairs={{8,0},{16,8},{24,16},{32,24},{40,32},{48,40},{56,48},{64,56},{72,6... | collective-permute-start | bytes 884744 | tf_op jit(solution)/shard_map/ppermute | solution.py:376
  16.7 12.3 %collective-permute-start.4 = (bf16[768,768]{1,0:T(8,128)(2,1)S(1)}, bf16[768,768]{1,0:T(8,128)(2,1)S(1)}, u32[]{:S(2)}, u32[]{:S(2)}) collective-permute-start(bf16[768,768]{1,0:T(8,128)(2,1)S(1)} %pad_maximum_fusion.cot_ext.refs_5_), channel_id=1, source_target_pairs={{0,1},{1,0},{2,3},{3,2},{4,5},{5,4},{6,7},{7,6},{8,9},{9,8},{10,11... | collective-permute-start | bytes 3538952 | tf_op jit(solution)/shard_map/ppermute | solution.py:405
  19.5 9.6 %collective-permute-start.3 = (bf16[640,768]{1,0:T(8,128)(2,1)S(1)}, bf16[640,768]{1,0:T(8,128)(2,1)S(1)}, u32[]{:S(2)}, u32[]{:S(2)}) collective-permute-start(bf16[640,768]{1,0:T(8,128)(2,1)S(1)} %pad_maximum_fusion.1.act.refs_2_), channel_id=1, source_target_pairs={{0,1},{1,0},{2,3},{3,2},{4,5},{5,4},{6,7},{7,6},{8,9},{9,8},{10,11... | collective-permute-start | bytes 2949128 | tf_op jit(solution)/shard_map/ppermute | solution.py:405
  26.6 2.5 %collective-permute-start.2 = (bf16[512,768]{1,0:T(8,128)(2,1)S(1)}, bf16[512,768]{1,0:T(8,128)(2,1)S(1)}, u32[]{:S(2)}, u32[]{:S(2)}) collective-permute-start(bf16[512,768]{1,0:T(8,128)(2,1)S(1)} %get-tuple-element.40), channel_id=1, source_target_pairs={{0,1},{1,0},{2,3},{3,2},{4,5},{5,4},{6,7},{7,6},{8,9},{9,8},{10,11... | collective-permute-start | bytes 2359304 | tf_op jit(solution)/shard_map/ppermute | solution.py:405
  30.7 10.3 %collective-permute-start.8 = (bf16[4,8,5,8,128]{4,3,2,1,0:T(8,128)(2,1)S(1)}, bf16[4,8,5,8,128]{4,3,2,1,0:T(8,128)(2,1)S(1)}, u32[]{:S(2)}, u32[]{:S(2)}) collective-permute-start(bf16[4,8,5,8,128]{4,3,2,1,0:T(8,128)(2,1)S(1)} %get-tuple-element.67), channel_id=1, source_target_pairs={{0,128},{1,5},{2,130},{3,7},{4,132},{5,1},{6,134},{7,3},{8,136},{9... | collective-permute-start | bytes 983048 | tf_op jit(solution)/shard_map/ppermute | solution.py:359
  33.7 12.1 %collective-permute-start.10 = (bf16[4,8,5,8,128]{4,3,2,1,0:T(8,128)(2,1)S(1)}, bf16[4,8,5,8,128]{4,3,2,1,0:T(8,128)(2,1)S(1)}, u32[]{:S(2)}, u32[]{:S(2)}) collective-permute-start(bf16[4,8,5,8,128]{4,3,2,1,0:T(8,128)(2,1)S(1)} %get-tuple-element.68), channel_id=1, source_target_pairs={{0,192},{1,7},{2,194},{3,1},{4,196},{5,3},{6,198},{7,5},{8,200},{9... | collective-permute-start | bytes 983048 | tf_op jit(solution)/shard_map/ppermute | solution.py:359
  34.5 11.3 %collective-permute-start.9 = (bf16[4,8,5,8,128]{4,3,2,1,0:T(8,128)(2,1)S(1)}, bf16[4,8,5,8,128]{4,3,2,1,0:T(8,128)(2,1)S(1)}, u32[]{:S(2)}, u32[]{:S(2)}) collective-permute-start(bf16[4,8,5,8,128]{4,3,2,1,0:T(8,128)(2,1)S(1)} %get-tuple-element.69), channel_id=1, source_target_pairs={{0,64},{1,3},{2,66},{3,5},{4,68},{5,7},{6,70},{7,1},{8,72},{9,11},... | collective-permute-start | bytes 983048 | tf_op jit(solution)/shard_map/ppermute | solution.py:359
  35.1 6.7 %copy-start.1 = (bf16[3,768,768]{2,1,0:T(8,128)(2,1)S(1)}, bf16[3,768,768]{2,1,0:T(8,128)(2,1)}, u32[]{:S(2)}) copy-start(bf16[3,768,768]{2,1,0:T(8,128)(2,1)} %w2.5) | copy-start | bytes 10616836
  38.1 3.7 %copy-start = (bf16[3,768,768]{2,1,0:T(8,128)(2,1)S(1)}, bf16[3,768,768]{2,1,0:T(8,128)(2,1)}, u32[]{:S(2)}) copy-start(bf16[3,768,768]{2,1,0:T(8,128)(2,1)} %w1.5) | copy-start | bytes 10616836
  38.3 13.8 %collective-permute-start.5 = (bf16[4,8,9,8,128]{4,3,2,1,0:T(8,128)(2,1)S(1)}, bf16[4,8,9,8,128]{4,3,2,1,0:T(8,128)(2,1)S(1)}, u32[]{:S(2)}, u32[]{:S(2)}) collective-permute-start(bf16[4,8,9,8,128]{4,3,2,1,0:T(8,128)(2,1)S(1)} %get-tuple-element.64), channel_id=1, source_target_pairs={{0,128},{1,5},{2,130},{3,7},{4,132},{5,1},{6,134},{7,3},{8,136},{9... | collective-permute-start | bytes 1769480 | tf_op jit(solution)/shard_map/ppermute | solution.py:359
  39.1 16.1 %collective-permute-start.6 = (bf16[4,8,9,8,128]{4,3,2,1,0:T(8,128)(2,1)S(1)}, bf16[4,8,9,8,128]{4,3,2,1,0:T(8,128)(2,1)S(1)}, u32[]{:S(2)}, u32[]{:S(2)}) collective-permute-start(bf16[4,8,9,8,128]{4,3,2,1,0:T(8,128)(2,1)S(1)} %get-tuple-element.66), channel_id=1, source_target_pairs={{0,64},{1,3},{2,66},{3,5},{4,68},{5,7},{6,70},{7,1},{8,72},{9,11},... | collective-permute-start | bytes 1769480 | tf_op jit(solution)/shard_map/ppermute | solution.py:359
  41.0 14.3 %collective-permute-start.7 = (bf16[4,8,9,8,128]{4,3,2,1,0:T(8,128)(2,1)S(1)}, bf16[4,8,9,8,128]{4,3,2,1,0:T(8,128)(2,1)S(1)}, u32[]{:S(2)}, u32[]{:S(2)}) collective-permute-start(bf16[4,8,9,8,128]{4,3,2,1,0:T(8,128)(2,1)S(1)} %get-tuple-element.65), channel_id=1, source_target_pairs={{0,192},{1,7},{2,194},{3,1},{4,196},{5,3},{6,198},{7,5},{8,200},{9... | collective-permute-start | bytes 1769480 | tf_op jit(solution)/shard_map/ppermute | solution.py:359
  55.7 9.2 %collective-permute-start.13 = (bf16[8,14,8,128]{3,2,1,0:T(8,128)(2,1)S(1)}, bf16[8,14,8,128]{3,2,1,0:T(8,128)(2,1)S(1)}, u32[]{:S(2)}, u32[]{:S(2)}) collective-permute-start(bf16[8,14,8,128]{3,2,1,0:T(8,128)(2,1)S(1)} %get-tuple-element.70), channel_id=1, source_target_pairs={{0,4},{1,129},{2,6},{3,131},{4,0},{5,133},{6,2},{7,135},{8,12},{9,... | collective-permute-start | bytes 688136 | tf_op jit(solution)/shard_map/ppermute | solution.py:359
  61.5 6.4 %collective-permute-start.14 = (bf16[8,14,8,128]{3,2,1,0:T(8,128)(2,1)S(1)}, bf16[8,14,8,128]{3,2,1,0:T(8,128)(2,1)S(1)}, u32[]{:S(2)}, u32[]{:S(2)}) collective-permute-start(bf16[8,14,8,128]{3,2,1,0:T(8,128)(2,1)S(1)} %get-tuple-element.72), channel_id=1, source_target_pairs={{0,2},{1,65},{2,4},{3,67},{4,6},{5,69},{6,0},{7,71},{8,10},{9,73},... | collective-permute-start | bytes 688136 | tf_op jit(solution)/shard_map/ppermute | solution.py:359
  62.3 6.2 %collective-permute-start.15 = (bf16[8,14,8,128]{3,2,1,0:T(8,128)(2,1)S(1)}, bf16[8,14,8,128]{3,2,1,0:T(8,128)(2,1)S(1)}, u32[]{:S(2)}, u32[]{:S(2)}) collective-permute-start(bf16[8,14,8,128]{3,2,1,0:T(8,128)(2,1)S(1)} %get-tuple-element.71), channel_id=1, source_target_pairs={{0,6},{1,193},{2,0},{3,195},{4,2},{5,197},{6,4},{7,199},{8,14},{9,... | collective-permute-start | bytes 688136 | tf_op jit(solution)/shard_map/ppermute | solution.py:359

commit v5 on v4

--- a/solution.py
+++ b/solution.py
@@ -382,7 +382,7 @@
     nx, ny, nz = (lax.axis_size(a) for a in ("x", "y", "z"))
     tokens = signal.shape[0] * ny * lax.axis_size("c") * rows * nx * nz
     scale = 1.0 / math.sqrt(tokens)
-    splits = [(0, 512), (512, 256)]
+    splits = [(0, ch)]
     sizes = [9 * width // 128 for _, width in splits]
     units = [-(-size // ny) for size in sizes]
     core = lax.axis_index("c").astype(jnp.int32).reshape(1)
@@ -404,15 +404,15 @@
     cot_ext = jnp.concatenate([lo[FIRST:], cot, hi[FIRST:]])
     swap = lambda a: lax.ppermute(a, "c", [(0, 1), (1, 0)])
     far_act, far_cot = swap(act_ext), swap(cot_ext)
+    cot_ext, lo_far, hi_far = lax.optimization_barrier((cot_ext, lo_far, hi_far))
     mid, act_b, grad_m, give = front(core, act_ext, cot_ext, sig, cot, w1, w2)
     f_all = swap(give)
     pieces = [
         weights((nx, ny, nz, u), *split, core, act_b, act_ext, f_all, far_act, far_cot, grad_m, cot_ext)
         for split, u in zip(splits, units)
     ]
-    wide, _ = exchange(pieces[0], order_a, "xy")
-    narrow, inside = exchange(pieces[1], order_a, "xy", inside)
-    pieces = [wide, narrow]
+    piece, inside = lax.optimization_barrier((pieces[0], inside))
+    pieces = [exchange(piece, order_a, "xy")[0]]
     lo2, hi2 = wings(inside, act_ext, cot_ext, lo, hi, lo_far, hi_far, w1, w2)
     output, grad_s = back(act_b, lo2, hi2, grad_m, mid, sig, w1, w2)
     pieces, output, grad_s = lax.optimization_barrier((pieces, output, grad_s))

time: 98.1 us -> 104 us (1.060)
  waiting for transfers between devices: 11.6 us -> 23.9 us
  starting transfers between devices: 30.9 us -> 26.5 us
    ppermute x9 -> x6, waiting for transfers between devices: 7.42 us -> 15.4 us  [exchange(): chunk = lax.ppermute(chunk, axes, pairs(k))]
    ppermute x9 -> x6, starting transfers between devices: 16.4 us -> 11.4 us  [exchange(): chunk = lax.ppermute(chunk, axes, pairs(k))]
    ppermute x2, waiting for transfers between devices: 2.45 us -> 6.28 us  [neighbours(): lax.ppermute(low, axes, backward)]
    all_to_all x1, blocking collectives: 15.2 us -> 12.9 us  [per_device(): lax.all_to_all(jnp.broadcast_to(part[None], (2 * ny,) + part.shape), ('y'...]
    all_to_all x1, blocking collectives: 13.1 us -> 14.4 us  [per_device(): got = lax.all_to_all(part, 'z', 0, 0, tiled=True)]
    pallas_call x2 -> x1, Pallas kernels: 4.5 us -> 3.93 us  [weights(): pl.pallas_call(lambda *refs: weight_kernel(parts, *refs), grid=(1,), in_s...]
  transfers between devices with their start and end apart: 16 -> 13, of which waited for: 6 -> 7; matrix products, arithmetic and copies ran while one was open for 1% -> 1% of each run, Pallas kernels for 20% -> 16%
where the time goes in v5:
time: 104 us
  blocking collectives  27.3 us (26%)
  starting transfers between devices  26.5 us (25%)
  waiting for transfers between devices  23.9 us (23%)
  Pallas kernels  22.5 us (22%)
  other arithmetic  1.65 us (2%)
  local copies, waits for them, and re-layouts  1.25 us (1%)
    ppermute x6, waiting for transfers between devices, exchange(): chunk = lax.ppermute(chunk, axes, pairs(k))  15.4 us
    all_to_all x1, blocking collectives, per_device(): got = lax.all_to_all(part, 'z', 0, 0, tiled=True)  14.4 us
    all_to_all x1, blocking collectives, per_device(): lax.all_to_all(jnp.broadcast_to(part[None], (2 * ny,) + part.shape), ('y'...  12.9 us
    ppermute x6, starting transfers between devices, exchange(): chunk = lax.ppermute(chunk, axes, pairs(k))  11.4 us
    ppermute x2, starting transfers between devices, neighbours(): lax.ppermute(high, axes, forward)  8.56 us
    pallas_call x1, Pallas kernels, front(): pl.pallas_call(front_kernel, grid=(ch // tile,), in_specs=[pl.BlockSpec(m...  6.97 us
    ppermute x2, waiting for transfers between devices, neighbours(): lax.ppermute(low, axes, backward)  6.28 us
    pallas_call x1, Pallas kernels, back(): pl.pallas_call(back_kernel, grid=(ch // tile,), in_specs=[once(act_b), on...  6.09 us
  transfers between devices with their start and end apart: 13, of which 7 were waited for; matrix products, arithmetic and copies ran while one was open for 1% of the time, Pallas kernels for 16%

profile of v5, /device:TPU:1, one launch (start us, length us, event | category | flops | bytes accessed | tf_op | source)
XLA Modules:
  0.0 104.1 jit_solution(2263619394073313584)
XLA Ops:
  0.6 0.0 copy-start.2
  0.7 0.1 add_convert_fusion.inside
  0.8 0.0 copy-start.3
  0.8 1.5 %edges.1 = (bf16[192,768]{1,0:T(8,128)(2,1)S(1)}, bf16[192,768]{1,0:T(8,128)(2,1)S(1)}, bf16[192,768]{1,0:T(8,128)(2,1)S(1)}, bf16[192,768]{1,0:T(8,128)(2,1)S(1)}) custom-call(bf16[512,768]{1,0:T(8,128)(2,1)} %bitcast.38, bf16[512,768]{1,0:T(8,128)(2,1)} %bitcast.42), custom_call_target="tpu_custom_call" | custom-call | tf_op jit(solution)/shard_map/edges/pallas_call | solution.py:77
  2.3 4.4 %collective-permute-start = (bf16[192,768]{1,0:T(8,128)(2,1)S(1)}, bf16[192,768]{1,0:T(8,128)(2,1)S(1)}, u32[]{:S(2)}, u32[]{:S(2)}) collective-permute-start(bf16[192,768]{1,0:T(8,128)(2,1)S(1)} %get-tuple-element.39), channel_id=1, source_target_pairs={{0,8},{8,16},{16,24},{24,32},{32,40},{40,48},{48,56},{56,64},{64,7... | collective-permute-start | bytes 884744 | tf_op jit(solution)/shard_map/ppermute | solution.py:376
  6.7 1.3 %collective-permute-start.1 = (bf16[192,768]{1,0:T(8,128)(2,1)S(1)}, bf16[192,768]{1,0:T(8,128)(2,1)S(1)}, u32[]{:S(2)}, u32[]{:S(2)}) collective-permute-start(bf16[192,768]{1,0:T(8,128)(2,1)S(1)} %get-tuple-element.40), channel_id=1, source_target_pairs={{8,0},{16,8},{24,16},{32,24},{40,32},{48,40},{56,48},{64,56},{72,6... | collective-permute-start | bytes 884744 | tf_op jit(solution)/shard_map/ppermute | solution.py:376
  8.0 4.2 %collective-permute-start.2 = (bf16[192,768]{1,0:T(8,128)(2,1)S(1)}, bf16[192,768]{1,0:T(8,128)(2,1)S(1)}, u32[]{:S(2)}, u32[]{:S(2)}) collective-permute-start(bf16[192,768]{1,0:T(8,128)(2,1)S(1)} %get-tuple-element.41), channel_id=1, source_target_pairs={{0,8},{8,16},{16,24},{24,32},{32,40},{40,48},{48,56},{56,64},{64,7... | collective-permute-start | bytes 884744 | tf_op jit(solution)/shard_map/ppermute | solution.py:376
  12.1 1.3 %collective-permute-start.3 = (bf16[192,768]{1,0:T(8,128)(2,1)S(1)}, bf16[192,768]{1,0:T(8,128)(2,1)S(1)}, u32[]{:S(2)}, u32[]{:S(2)}) collective-permute-start(bf16[192,768]{1,0:T(8,128)(2,1)S(1)} %get-tuple-element.42), channel_id=1, source_target_pairs={{8,0},{16,8},{24,16},{32,24},{40,32},{48,40},{56,48},{64,56},{72,6... | collective-permute-start | bytes 884744 | tf_op jit(solution)/shard_map/ppermute | solution.py:376
  13.4 0.0 copy-done.2
  13.5 0.5 fusion.4
  14.0 0.0 collective-permute-done.lo
  14.0 2.4 %collective-permute-done.1.hi = bf16[192,768]{1,0:T(8,128)(2,1)S(1)} collective-permute-done((bf16[192,768]{1,0:T(8,128)(2,1)S(1)}, bf16[192,768]{1,0:T(8,128)(2,1)S(1)}, u32[]{:S(2)}, u32[]{:S(2)}) %collective-permute-start.1) | collective-permute-done | bytes 294944 | tf_op jit(solution)/shard_map/ppermute | solution.py:376
  16.5 0.0 copy-done.3
  16.5 0.1 pad_maximum_fusion.cot_ext.refs_5_
  16.6 2.5 %collective-permute-start.6 = (bf16[768,768]{1,0:T(8,128)(2,1)S(1)}, bf16[768,768]{1,0:T(8,128)(2,1)S(1)}, u32[]{:S(2)}, u32[]{:S(2)}) collective-permute-start(bf16[768,768]{1,0:T(8,128)(2,1)S(1)} %pad_maximum_fusion.cot_ext.refs_5_), channel_id=1, source_target_pairs={{0,1},{1,0},{2,3},{3,2},{4,5},{5,4},{6,7},{7,6},{8,9},{9,8},{10,11... | collective-permute-start | bytes 3538952 | tf_op jit(solution)/shard_map/ppermute | solution.py:405
  19.1 0.1 fusion.12
  19.2 0.1 fusion.17
  19.3 0.1 pad_maximum_fusion.1.act.refs_2_
  19.3 0.0 collective-permute-done.2.lo_far
  19.4 0.0 copy-start.4
  19.4 3.8 %collective-permute-done.3.hi_far = bf16[192,768]{1,0:T(8,128)(2,1)S(1)} collective-permute-done((bf16[192,768]{1,0:T(8,128)(2,1)S(1)}, bf16[192,768]{1,0:T(8,128)(2,1)S(1)}, u32[]{:S(2)}, u32[]{:S(2)}) %collective-permute-start.3) | collective-permute-done | bytes 294944 | tf_op jit(solution)/shard_map/ppermute | solution.py:376
  23.2 0.0 copy-start.6
  23.2 1.3 %collective-permute-start.5 = (bf16[640,768]{1,0:T(8,128)(2,1)S(1)}, bf16[640,768]{1,0:T(8,128)(2,1)S(1)}, u32[]{:S(2)}, u32[]{:S(2)}) collective-permute-start(bf16[640,768]{1,0:T(8,128)(2,1)S(1)} %pad_maximum_fusion.1.act.refs_2_), channel_id=1, source_target_pairs={{0,1},{1,0},{2,3},{3,2},{4,5},{5,4},{6,7},{7,6},{8,9},{9,8},{10,11... | collective-permute-start | bytes 2949128 | tf_op jit(solution)/shard_map/ppermute | solution.py:405
  24.5 7.0 %front.1 = (bf16[512,768]{1,0:T(8,128)(2,1)S(1)}, bf16[512,768]{1,0:T(8,128)(2,1)S(1)}, bf16[512,768]{1,0:T(8,128)(2,1)S(1)}, bf16[512,768]{1,0:T(8,128)(2,1)S(1)}) custom-call(s32[1]{0:T(128)} %bitcast.2.core.refs_0_, bf16[640,768]{1,0:T(8,128)(2,1)S(1)} %pad_maximum_fusion.1.act.refs_2_, bf16[768,768]{1,0:T(8,128)(2,1)S(1)} %pad_maximum_fusion.cot_ext.refs_5_, ...), custom_call_target="tpu_custom_call" | custom-call | flops 3623878656 | bytes 8257536 | tf_op jit(solution)/shard_map/front/pallas_call | solution.py:121
  31.5 0.2 collective-permute-start.4
  31.6 0.0 copy-done.4
  31.6 0.0 copy-done.6
  31.6 2.2 %collective-permute-done.4.refs_3_.refs_8_ = bf16[512,768]{1,0:T(8,128)(2,1)S(1)} collective-permute-done((bf16[512,768]{1,0:T(8,128)(2,1)S(1)}, bf16[512,768]{1,0:T(8,128)(2,1)S(1)}, u32[]{:S(2)}, u32[]{:S(2)}) %collective-permute-start.4) | collective-permute-done | bytes 786464 | tf_op jit(solution)/shard_map/ppermute | solution.py:405
  33.8 0.0 collective-permute-done.5.refs_4_
  33.8 0.0 collective-permute-done.6.refs_6_
  33.8 0.0 slice-start
  33.8 0.0 slice-start.1
  33.8 0.0 copy-start.5
  33.9 0.0 copy-start.7
  33.9 3.9 %weights.1 = bf16[4,4,8,14,8,128]{5,4,3,2,1,0:T(8,128)(2,1)S(1)} custom-call(s32[1]{0:T(128)} %bitcast.2.core.refs_0_, bf16[512,768]{1,0:T(8,128)(2,1)S(1)} %get-tuple-element.44.refs_1_.act_b, bf16[640,768]{1,0:T(8,128)(2,1)S(1)} %pad_maximum_fusion.1.act.refs_2_, bf16[512,768]{1,0:T(8,128)(2,1)S(1)} %collective-permute-done.4.refs_3_.refs_8_, ...), custom_call_target="tpu_custom_call" | custom-call | flops 3623878656 | bytes 7077888 | tf_op jit(solution)/shard_map/weights/pallas_call | solution.py:314
  37.8 0.0 copy-start
  37.8 0.0 copy-start.1
  37.8 0.2 dynamic-slice_bitcast_fusion.2
  38.0 3.0 %collective-permute-start.7 = (bf16[4,8,14,8,128]{4,3,2,1,0:T(8,128)(2,1)S(1)}, bf16[4,8,14,8,128]{4,3,2,1,0:T(8,128)(2,1)S(1)}, u32[]{:S(2)}, u32[]{:S(2)}) collective-permute-start(bf16[4,8,14,8,128]{4,3,2,1,0:T(8,128)(2,1)S(1)} %get-tuple-element.68), channel_id=1, source_target_pairs={{0,128},{1,5},{2,130},{3,7},{4,132},{5,1},{6,134},{7,3},{8,136},{9... | collective-permute-start | bytes 2752520 | tf_op jit(solution)/shard_map/ppermute | solution.py:359
  41.0 0.8 collective-permute-start.9
  41.8 0.7 collective-permute-start.8
  42.5 0.0 slice-done
  42.6 0.0 slice-done.1
  42.6 0.0 copy-done.5
  42.6 0.0 copy-done.7
  42.6 0.0 copy-done
  42.6 0.0 copy-done.1
  42.6 4.0 %wings.1 = (bf16[192,768]{1,0:T(8,128)(2,1)S(1)}, bf16[192,768]{1,0:T(8,128)(2,1)S(1)}) custom-call(s32[2]{0:T(128)S(1)} %add_convert_fusion.inside, bf16[640,768]{1,0:T(8,128)(2,1)S(1)} %pad_maximum_fusion.1.act.refs_2_, bf16[768,768]{1,0:T(8,128)(2,1)S(1)} %pad_maximum_fusion.cot_ext.refs_5_, bf16[192,768]{1,0:T(8,128)(2,1)S(1)} %collective-permute-done.lo, ...), custom_call_target="tpu_custom_call" | custom-call | flops 1358954496 | bytes 7077888 | tf_op jit(solution)/shard_map/wings/pallas_call | solution.py:189
  46.6 6.1 %rear.1 = (bf16[512,768]{1,0:T(8,128)(2,1)}, bf16[512,768]{1,0:T(8,128)(2,1)}) custom-call(bf16[512,768]{1,0:T(8,128)(2,1)S(1)} %get-tuple-element.44.refs_1_.act_b, bf16[192,768]{1,0:T(8,128)(2,1)S(1)} %get-tuple-element.56.lo, bf16[192,768]{1,0:T(8,128)(2,1)S(1)} %get-tuple-element.57.hi, bf16[512,768]{1,0:T(8,128)(2,1)S(1)} %get-tuple-element.46.refs_7_.grad_m.gm, ...), custom_call_target="tpu_custom_call" | custom-call | flops 3623878656 | bytes 8257536 | tf_op jit(solution)/shard_map/rear/pallas_call | solution.py:242
  52.7 0.0 collective-permute-done.7
  52.7 9.6 %collective-permute-done.9 = bf16[4,8,14,8,128]{4,3,2,1,0:T(8,128)(2,1)S(1)} collective-permute-done((bf16[4,8,14,8,128]{4,3,2,1,0:T(8,128)(2,1)S(1)}, bf16[4,8,14,8,128]{4,3,2,1,0:T(8,128)(2,1)S(1)}, u32[]{:S(2)}, u32[]{:S(2)}) %collective-permute-start.9) | collective-permute-done | bytes 917536 | tf_op jit(solution)/shard_map/ppermute | solution.py:359
  62.4 0.0 collective-permute-done.8
  62.4 0.5 fusion.2
  62.9 0.1 dynamic-slice_bitcast_fusion.5
  62.9 5.5 %collective-permute-start.10 = (bf16[8,14,8,128]{3,2,1,0:T(8,128)(2,1)S(1)}, bf16[8,14,8,128]{3,2,1,0:T(8,128)(2,1)S(1)}, u32[]{:S(2)}, u32[]{:S(2)}) collective-permute-start(bf16[8,14,8,128]{3,2,1,0:T(8,128)(2,1)S(1)} %get-tuple-element.71), channel_id=1, source_target_pairs={{0,4},{1,129},{2,6},{3,131},{4,0},{5,133},{6,2},{7,135},{8,12},{9,... | collective-permute-start | bytes 688136 | tf_op jit(solution)/shard_map/ppermute | solution.py:359
  68.4 0.9 collective-permute-start.12
  69.3 0.6 collective-permute-start.11
  69.9 2.2 %collective-permute-done.10 = bf16[8,14,8,128]{3,2,1,0:T(8,128)(2,1)S(1)} collective-permute-done((bf16[8,14,8,128]{3,2,1,0:T(8,128)(2,1)S(1)}, bf16[8,14,8,128]{3,2,1,0:T(8,128)(2,1)S(1)}, u32[]{:S(2)}, u32[]{:S(2)}) %collective-permute-start.10) | collective-permute-done | bytes 229408 | tf_op jit(solution)/shard_map/ppermute | solution.py:359
  72.1 3.1 %collective-permute-done.12 = bf16[8,14,8,128]{3,2,1,0:T(8,128)(2,1)S(1)} collective-permute-done((bf16[8,14,8,128]{3,2,1,0:T(8,128)(2,1)S(1)}, bf16[8,14,8,128]{3,2,1,0:T(8,128)(2,1)S(1)}, u32[]{:S(2)}, u32[]{:S(2)}) %collective-permute-start.12) | collective-permute-done | bytes 229408 | tf_op jit(solution)/shard_map/ppermute | solution.py:359
  75.2 0.4 collective-permute-done.11
  75.6 0.1 fusion.10
  75.8 14.4 %all_to_all.10 = bf16[8,14,8,128]{3,2,1,0:T(8,128)(2,1)S(1)} all-to-all(bf16[8,14,8,128]{3,2,1,0:T(8,128)(2,1)S(1)} %fusion.10), channel_id=1, replica_groups=mesh['x'=4,'z'=8,'y'=4,'c'=2] {'z'}, dimensions={0} | all-to-all | bytes 458752 | tf_op jit(solution)/shard_map/all_to_all | solution.py:421
  90.3 12.9 %all_to_all.11 = bf16[8,14,8,128]{3,2,1,0:T(8,128)(2,1)S(1)} all-to-all(bf16[8,14,8,128]{3,2,1,0:T(8,128)(2,1)S(1)} %broadcast_in_dim.14), channel_id=1, replica_groups=mesh['x'=4,'z'=8,'y'=4,'c'=2] {'y','c'}, dimensions={0} | all-to-all | bytes 458752 | tf_op jit(solution)/shard_map/all_to_all | solution.py:423
  103.3 0.8 copy_bitcast_fusion
  (12 shorter events, 0.3 us)
Async XLA Ops:
  0.6 12.8 %copy-start.2 = (bf16[1,512,768]{2,1,0:T(8,128)(2,1)S(1)}, bf16[1,512,768]{2,1,0:T(8,128)(2,1)}, u32[]{:S(2)}) copy-start(bf16[1,512,768]{2,1,0:T(8,128)(2,1)} %param.4) | copy-start | bytes 2359300
  0.8 15.7 %copy-start.3 = (bf16[1,512,768]{2,1,0:T(8,128)(2,1)S(1)}, bf16[1,512,768]{2,1,0:T(8,128)(2,1)}, u32[]{:S(2)}) copy-start(bf16[1,512,768]{2,1,0:T(8,128)(2,1)} %param.7) | copy-start | bytes 2359300
  2.3 11.7 %collective-permute-start = (bf16[192,768]{1,0:T(8,128)(2,1)S(1)}, bf16[192,768]{1,0:T(8,128)(2,1)S(1)}, u32[]{:S(2)}, u32[]{:S(2)}) collective-permute-start(bf16[192,768]{1,0:T(8,128)(2,1)S(1)} %get-tuple-element.39), channel_id=1, source_target_pairs={{0,8},{8,16},{16,24},{24,32},{32,40},{40,48},{48,56},{56,64},{64,7... | collective-permute-start | bytes 884744 | tf_op jit(solution)/shard_map/ppermute | solution.py:376
  6.7 9.8 %collective-permute-start.1 = (bf16[192,768]{1,0:T(8,128)(2,1)S(1)}, bf16[192,768]{1,0:T(8,128)(2,1)S(1)}, u32[]{:S(2)}, u32[]{:S(2)}) collective-permute-start(bf16[192,768]{1,0:T(8,128)(2,1)S(1)} %get-tuple-element.40), channel_id=1, source_target_pairs={{8,0},{16,8},{24,16},{32,24},{40,32},{48,40},{56,48},{64,56},{72,6... | collective-permute-start | bytes 884744 | tf_op jit(solution)/shard_map/ppermute | solution.py:376
  8.0 11.4 %collective-permute-start.2 = (bf16[192,768]{1,0:T(8,128)(2,1)S(1)}, bf16[192,768]{1,0:T(8,128)(2,1)S(1)}, u32[]{:S(2)}, u32[]{:S(2)}) collective-permute-start(bf16[192,768]{1,0:T(8,128)(2,1)S(1)} %get-tuple-element.41), channel_id=1, source_target_pairs={{0,8},{8,16},{16,24},{24,32},{32,40},{40,48},{48,56},{56,64},{64,7... | collective-permute-start | bytes 884744 | tf_op jit(solution)/shard_map/ppermute | solution.py:376
  12.1 11.1 %collective-permute-start.3 = (bf16[192,768]{1,0:T(8,128)(2,1)S(1)}, bf16[192,768]{1,0:T(8,128)(2,1)S(1)}, u32[]{:S(2)}, u32[]{:S(2)}) collective-permute-start(bf16[192,768]{1,0:T(8,128)(2,1)S(1)} %get-tuple-element.42), channel_id=1, source_target_pairs={{8,0},{16,8},{24,16},{32,24},{40,32},{48,40},{56,48},{64,56},{72,6... | collective-permute-start | bytes 884744 | tf_op jit(solution)/shard_map/ppermute | solution.py:376
  16.6 17.2 %collective-permute-start.6 = (bf16[768,768]{1,0:T(8,128)(2,1)S(1)}, bf16[768,768]{1,0:T(8,128)(2,1)S(1)}, u32[]{:S(2)}, u32[]{:S(2)}) collective-permute-start(bf16[768,768]{1,0:T(8,128)(2,1)S(1)} %pad_maximum_fusion.cot_ext.refs_5_), channel_id=1, source_target_pairs={{0,1},{1,0},{2,3},{3,2},{4,5},{5,4},{6,7},{7,6},{8,9},{9,8},{10,11... | collective-permute-start | bytes 3538952 | tf_op jit(solution)/shard_map/ppermute | solution.py:405
  19.4 12.3 %copy-start.4 = (bf16[192,768]{1,0:T(8,128)(2,1)}, bf16[192,768]{1,0:T(8,128)(2,1)S(1)}, u32[]{:S(2)}) copy-start(bf16[192,768]{1,0:T(8,128)(2,1)S(1)} %collective-permute-done.2.lo_far) | copy-start | bytes 884740
  23.2 8.4 %copy-start.6 = (bf16[192,768]{1,0:T(8,128)(2,1)}, bf16[192,768]{1,0:T(8,128)(2,1)S(1)}, u32[]{:S(2)}) copy-start(bf16[192,768]{1,0:T(8,128)(2,1)S(1)} %collective-permute-done.3.hi_far) | copy-start | bytes 884740
  23.2 10.6 %collective-permute-start.5 = (bf16[640,768]{1,0:T(8,128)(2,1)S(1)}, bf16[640,768]{1,0:T(8,128)(2,1)S(1)}, u32[]{:S(2)}, u32[]{:S(2)}) collective-permute-start(bf16[640,768]{1,0:T(8,128)(2,1)S(1)} %pad_maximum_fusion.1.act.refs_2_), channel_id=1, source_target_pairs={{0,1},{1,0},{2,3},{3,2},{4,5},{5,4},{6,7},{7,6},{8,9},{9,8},{10,11... | collective-permute-start | bytes 2949128 | tf_op jit(solution)/shard_map/ppermute | solution.py:405
  31.5 2.4 %collective-permute-start.4 = (bf16[512,768]{1,0:T(8,128)(2,1)S(1)}, bf16[512,768]{1,0:T(8,128)(2,1)S(1)}, u32[]{:S(2)}, u32[]{:S(2)}) collective-permute-start(bf16[512,768]{1,0:T(8,128)(2,1)S(1)} %get-tuple-element.45), channel_id=1, source_target_pairs={{0,1},{1,0},{2,3},{3,2},{4,5},{5,4},{6,7},{7,6},{8,9},{9,8},{10,11... | collective-permute-start | bytes 2359304 | tf_op jit(solution)/shard_map/ppermute | solution.py:405
  33.8 8.7 %slice-start = ((bf16[192,768]{1,0:T(8,128)(2,1)}), bf16[64,768]{1,0:T(8,128)(2,1)S(1)}, s32[]{:S(2)}) async-start(bf16[192,768]{1,0:T(8,128)(2,1)} %copy-done.4), calls=%async_computation.2 | async-start | bytes 196608 | tf_op jit(solution)/shard_map/slice | solution.py:185
  33.8 8.7 %slice-start.1 = ((bf16[192,768]{1,0:T(8,128)(2,1)}), bf16[64,768]{1,0:T(8,128)(2,1)S(1)}, s32[]{:S(2)}) async-start(bf16[192,768]{1,0:T(8,128)(2,1)} %copy-done.6), calls=%async_computation.3 | async-start | bytes 196608 | tf_op jit(solution)/shard_map/slice | solution.py:185
  33.8 8.8 %copy-start.5 = (bf16[192,768]{1,0:T(8,128)(2,1)S(1)}, bf16[192,768]{1,0:T(8,128)(2,1)}, u32[]{:S(2)}) copy-start(bf16[192,768]{1,0:T(8,128)(2,1)} %copy-done.4) | copy-start | bytes 884740
  33.9 8.8 %copy-start.7 = (bf16[192,768]{1,0:T(8,128)(2,1)S(1)}, bf16[192,768]{1,0:T(8,128)(2,1)}, u32[]{:S(2)}) copy-start(bf16[192,768]{1,0:T(8,128)(2,1)} %copy-done.6) | copy-start | bytes 884740
  37.8 4.8 %copy-start = (bf16[3,768,768]{2,1,0:T(8,128)(2,1)S(1)}, bf16[3,768,768]{2,1,0:T(8,128)(2,1)}, u32[]{:S(2)}) copy-start(bf16[3,768,768]{2,1,0:T(8,128)(2,1)} %w1.5) | copy-start | bytes 10616836
  37.8 4.8 %copy-start.1 = (bf16[3,768,768]{2,1,0:T(8,128)(2,1)S(1)}, bf16[3,768,768]{2,1,0:T(8,128)(2,1)}, u32[]{:S(2)}) copy-start(bf16[3,768,768]{2,1,0:T(8,128)(2,1)} %w2.5) | copy-start | bytes 10616836
  38.0 14.7 %collective-permute-start.7 = (bf16[4,8,14,8,128]{4,3,2,1,0:T(8,128)(2,1)S(1)}, bf16[4,8,14,8,128]{4,3,2,1,0:T(8,128)(2,1)S(1)}, u32[]{:S(2)}, u32[]{:S(2)}) collective-permute-start(bf16[4,8,14,8,128]{4,3,2,1,0:T(8,128)(2,1)S(1)} %get-tuple-element.68), channel_id=1, source_target_pairs={{0,128},{1,5},{2,130},{3,7},{4,132},{5,1},{6,134},{7,3},{8,136},{9... | collective-permute-start | bytes 2752520 | tf_op jit(solution)/shard_map/ppermute | solution.py:359
  41.0 21.3 %collective-permute-start.9 = (bf16[4,8,14,8,128]{4,3,2,1,0:T(8,128)(2,1)S(1)}, bf16[4,8,14,8,128]{4,3,2,1,0:T(8,128)(2,1)S(1)}, u32[]{:S(2)}, u32[]{:S(2)}) collective-permute-start(bf16[4,8,14,8,128]{4,3,2,1,0:T(8,128)(2,1)S(1)} %get-tuple-element.69), channel_id=1, source_target_pairs={{0,192},{1,7},{2,194},{3,1},{4,196},{5,3},{6,198},{7,5},{8,200},{9... | collective-permute-start | bytes 2752520 | tf_op jit(solution)/shard_map/ppermute | solution.py:359
  41.8 20.6 %collective-permute-start.8 = (bf16[4,8,14,8,128]{4,3,2,1,0:T(8,128)(2,1)S(1)}, bf16[4,8,14,8,128]{4,3,2,1,0:T(8,128)(2,1)S(1)}, u32[]{:S(2)}, u32[]{:S(2)}) collective-permute-start(bf16[4,8,14,8,128]{4,3,2,1,0:T(8,128)(2,1)S(1)} %get-tuple-element.70), channel_id=1, source_target_pairs={{0,64},{1,3},{2,66},{3,5},{4,68},{5,7},{6,70},{7,1},{8,72},{9,11},... | collective-permute-start | bytes 2752520 | tf_op jit(solution)/shard_map/ppermute | solution.py:359
  62.9 9.2 %collective-permute-start.10 = (bf16[8,14,8,128]{3,2,1,0:T(8,128)(2,1)S(1)}, bf16[8,14,8,128]{3,2,1,0:T(8,128)(2,1)S(1)}, u32[]{:S(2)}, u32[]{:S(2)}) collective-permute-start(bf16[8,14,8,128]{3,2,1,0:T(8,128)(2,1)S(1)} %get-tuple-element.71), channel_id=1, source_target_pairs={{0,4},{1,129},{2,6},{3,131},{4,0},{5,133},{6,2},{7,135},{8,12},{9,... | collective-permute-start | bytes 688136 | tf_op jit(solution)/shard_map/ppermute | solution.py:359
  68.4 6.8 %collective-permute-start.12 = (bf16[8,14,8,128]{3,2,1,0:T(8,128)(2,1)S(1)}, bf16[8,14,8,128]{3,2,1,0:T(8,128)(2,1)S(1)}, u32[]{:S(2)}, u32[]{:S(2)}) collective-permute-start(bf16[8,14,8,128]{3,2,1,0:T(8,128)(2,1)S(1)} %get-tuple-element.72), channel_id=1, source_target_pairs={{0,6},{1,193},{2,0},{3,195},{4,2},{5,197},{6,4},{7,199},{8,14},{9,... | collective-permute-start | bytes 688136 | tf_op jit(solution)/shard_map/ppermute | solution.py:359
  69.3 6.4 %collective-permute-start.11 = (bf16[8,14,8,128]{3,2,1,0:T(8,128)(2,1)S(1)}, bf16[8,14,8,128]{3,2,1,0:T(8,128)(2,1)S(1)}, u32[]{:S(2)}, u32[]{:S(2)}) collective-permute-start(bf16[8,14,8,128]{3,2,1,0:T(8,128)(2,1)S(1)} %get-tuple-element.73), channel_id=1, source_target_pairs={{0,2},{1,65},{2,4},{3,67},{4,6},{5,69},{6,0},{7,71},{8,10},{9,73},... | collective-permute-start | bytes 688136 | tf_op jit(solution)/shard_map/ppermute | solution.py:359
